TPU v7x, 32 devices: a whole 2x2x4 slice. The times are simulated.
32 devices in a mesh: dp: 16 (over z, y, x), mp: 2 (over core).
Axes of the slice: x: 2, y: 2, z: 4, core: 2. Of those that a mesh axis runs over, the one named last changes fastest.
Arguments:
- mask_features: bfloat16 [16, 32, 128, 256], P('dp', None, None, 'mp'), may hold values from -6 to 6
- grid_features: bfloat16 [16, 40, 40, 256], P('dp', None, None, 'mp'), may hold values from -6 to 6
- instance_cells: int32 [16, 100], P('dp'), may hold values from 0 to 1599, as said below
- instance_counts: int32 [16], replicated, may hold values from 1 to 100, as said below
- instance_labels: int32 [16, 100], P('dp'), may hold values from 0 to 79
- instance_masks: int32 [16, 100, 4096], P('dp'), may hold values 0 or 1
- mask_convs: float32 [2, 9, 256, 256], P(None, None, 'dp', 'mp'), may hold values from -0.125 to 0.125
- mask_convs_moment: float32 [2, 9, 256, 256], P(None, None, 'dp', 'mp'), may hold values from -1.7881393e-07 to 1.7881393e-07
- mask_convs_square: float32 [2, 9, 256, 256], P(None, None, 'dp', 'mp'), may hold values from 2.762352e-15 to 1.1049408e-14
- grid_first: float32 [9, 256, 512], P(None, 'dp', 'mp'), may hold values from -0.125 to 0.125
- grid_first_moment: float32 [9, 256, 512], P(None, 'dp', 'mp'), may hold values from -2.3841858e-07 to 2.3841858e-07
- grid_first_square: float32 [9, 256, 512], P(None, 'dp', 'mp'), may hold values from 4.9108476e-15 to 1.964339e-14
- grid_second: float32 [9, 512, 256], P(None, 'dp', 'mp'), may hold values from -0.0234375 to 0.0234375
- grid_second_moment: float32 [9, 512, 256], P(None, 'dp', 'mp'), may hold values from -3.8146973e-06 to 3.8146973e-06
- grid_second_square: float32 [9, 512, 256], P(None, 'dp', 'mp'), may hold values from 1.1049407e-12 to 4.4197627e-12
- class_conv: float32 [9, 512, 80], P(None, 'dp', 'mp'), may hold values from -0.09375 to 0.09375
- class_conv_moment: float32 [9, 512, 80], P(None, 'dp', 'mp'), may hold values from -4.7683716e-06 to 4.7683716e-06
- class_conv_square: float32 [9, 512, 80], P(None, 'dp', 'mp'), may hold values from 1.7264699e-12 to 6.9058795e-12
- mask_norms: float32 [4, 256], P(None, 'mp'), may hold values from 0.2 to 1.4
- mask_norms_moment: float32 [4, 256], P(None, 'mp'), may hold values from -2.9802322e-07 to 2.9802322e-07
- mask_norms_square: float32 [4, 256], P(None, 'mp'), may hold values from 7.6731995e-15 to 3.0692798e-14
- grid_norms: float32 [2, 512], P(None, 'mp'), may hold values from 0.2 to 1.4
- grid_norms_moment: float32 [2, 512], P(None, 'mp'), may hold values from -9.536743e-06 to 9.536743e-06
- grid_norms_square: float32 [2, 512], P(None, 'mp'), may hold values from 6.9058795e-12 to 2.7623518e-11
- class_bias: float32 [80], P('mp'), may hold values from -4.6 to -2
- class_bias_moment: float32 [80], P('mp'), may hold values from -6.1035156e-05 to 6.1035156e-05
- class_bias_square: float32 [80], P('mp'), may hold values from 3.0692798e-10 to 1.2277119e-09
Outputs:
- step_loss: float32 [], replicated
- gradient_norm: float32 [], replicated
- mask_convs_new: float32 [2, 9, 256, 256], P(None, None, 'dp', 'mp')
- mask_convs_moment_new: float32 [2, 9, 256, 256], P(None, None, 'dp', 'mp')
- mask_convs_square_new: float32 [2, 9, 256, 256], P(None, None, 'dp', 'mp')
- grid_first_new: float32 [9, 256, 512], P(None, 'dp', 'mp')
- grid_first_moment_new: float32 [9, 256, 512], P(None, 'dp', 'mp')
- grid_first_square_new: float32 [9, 256, 512], P(None, 'dp', 'mp')
- grid_second_new: float32 [9, 512, 256], P(None, 'dp', 'mp')
- grid_second_moment_new: float32 [9, 512, 256], P(None, 'dp', 'mp')
- grid_second_square_new: float32 [9, 512, 256], P(None, 'dp', 'mp')
- class_conv_new: float32 [9, 512, 80], P(None, 'dp', 'mp')
- class_conv_moment_new: float32 [9, 512, 80], P(None, 'dp', 'mp')
- class_conv_square_new: float32 [9, 512, 80], P(None, 'dp', 'mp')
- mask_norms_new: float32 [4, 256], P(None, 'mp')
- mask_norms_moment_new: float32 [4, 256], P(None, 'mp')
- mask_norms_square_new: float32 [4, 256], P(None, 'mp')
- grid_norms_new: float32 [2, 512], P(None, 'mp')
- grid_norms_moment_new: float32 [2, 512], P(None, 'mp')
- grid_norms_square_new: float32 [2, 512], P(None, 'mp')
- class_bias_new: float32 [80], P('mp')
- class_bias_moment_new: float32 [80], P('mp')
- class_bias_square_new: float32 [80], P('mp')
Inputs may be any that keep to these rules, and one draw needn't show every extreme that they name: `instance_cells`: within an image the cells of the 100 slots are distinct. `instance_counts`: some image has 100 live instances in every draw.
All inputs are finite; a program needn't handle non-finite values. No bound on the sum of `instance_masks` on one device may be relied on, other than what follows from the above.
Results may differ from a plain program's by a relative error of at most 0.007.
The roundings to bfloat16 on the way count: a program that leaves them out, or rounds other values in their place, can miss the bound.
Values may be sent and summed in bfloat16 or wider, within the bound.
A program may use at most 192 MiB of HBM per device.

v0:
```python
from functools import partial

import jax
import jax.numpy as jnp
from jax import lax
from jax.sharding import PartitionSpec as P

GROUPS = 32
G = 40
NI = 100


GN_EPS = 1e-05
CLIP_LIMIT = 0.02
LEARN_RATE = 0.02
SMALL_RATE = 0.5
BETA_ONE = 0.9
BETA_TWO = 0.95
ADAM_EPS = 1e-08
WEIGHT_DECAY = 0.05
CONTRAST_TEMP = 0.05
FOCAL_ALPHA = 0.25
DICE_WEIGHT = 3.0
STEP_TIME = 10.0
HIGHEST = lax.Precision.HIGHEST


def shifted_view(padded, tap_index, height, columns, direction):
    row_start = 1 + direction * (tap_index // 3 - 1)
    col_start = 1 + direction * (tap_index % 3 - 1)
    return padded[row_start : row_start + height, col_start : col_start + columns]


def padding(values):
    return jnp.pad(values, ((1, 1), (1, 1), (0, 0)))


def convolve(values, weight):
    height, columns = (values.shape[0], values.shape[1])
    padded = padding(values)
    summed = jnp.zeros((height, columns, weight.shape[2]), jnp.float32)
    for tap_index in range(9):
        summed = summed + jnp.einsum(
            "hwc,cd->hwd",
            shifted_view(padded, tap_index, height, columns, 1),
            weight[tap_index],
            preferred_element_type=jnp.float32,
        )
    return summed


def conv_input_grad(gradient, weight):
    height, columns = (gradient.shape[0], gradient.shape[1])
    padded = padding(gradient)
    summed = jnp.zeros((height, columns, weight.shape[1]), jnp.float32)
    for tap_index in range(9):
        summed = summed + jnp.einsum(
            "hwd,cd->hwc",
            shifted_view(padded, tap_index, height, columns, -1),
            weight[tap_index],
            preferred_element_type=jnp.float32,
        )
    return summed


def conv_weight_grad(values, gradient):
    height, columns = (values.shape[0], values.shape[1])
    padded = padding(values)
    return jnp.stack(
        [
            jnp.einsum(
                "hwc,hwd->cd",
                shifted_view(padded, tap_index, height, columns, 1),
                gradient,
                preferred_element_type=jnp.float32,
            )
            for tap_index in range(9)
        ]
    )


def norm_act(values, gain_row, bias_row, group_width):
    height, columns, channels = values.shape
    grouped = values.reshape(height * columns, channels // group_width, group_width)
    group_mean = jnp.mean(grouped, axis=(0, 2), keepdims=True)
    group_var = jnp.mean(jnp.square(grouped - group_mean), axis=(0, 2), keepdims=True)
    normed = ((grouped - group_mean) * lax.rsqrt(group_var + GN_EPS)).reshape(
        height, columns, channels
    )
    return jax.nn.relu(normed * gain_row + bias_row)


def pixel_sums(logits, mask_cols):
    probability = jax.nn.sigmoid(logits)
    return (jnp.sum(probability * mask_cols, axis=0), jnp.sum(probability * probability, axis=0))


def dice_from(intersection, squares_sum, mask_sum, live_slots, live_count):
    denominator = squares_sum + mask_sum + 1.0
    return jnp.sum(live_slots * (1.0 - 2.0 * intersection / denominator)) / live_count.astype(
        jnp.float32
    )


def focal_part(class_logits, cell_ids, live_slots, live_count, labels, class_start):
    cell_hot = (cell_ids[:, None] == jnp.arange(G * G)[None, :]).astype(jnp.float32) * live_slots[
        :, None
    ]
    class_hot = (
        labels[:, None] == class_start + jnp.arange(class_logits.shape[1])[None, :]
    ).astype(jnp.float32)
    target = jnp.dot(cell_hot.T, class_hot, precision=HIGHEST)
    class_prob = jax.nn.sigmoid(class_logits)
    log_pos = -jax.nn.softplus(-class_logits)
    log_neg = -jax.nn.softplus(class_logits)
    focal_terms = (
        FOCAL_ALPHA * target * jnp.square(1.0 - class_prob) * log_pos
        + (1.0 - FOCAL_ALPHA) * (1.0 - target) * jnp.square(class_prob) * log_neg
    )
    return -jnp.sum(focal_terms) / (live_count.astype(jnp.float32) + 1.0)


def contrast_loss(unscaled_scores, norms_all, row_start, live_slots, live_count, live_all):
    reciprocal_norm = lax.rsqrt(norms_all + 1e-06)
    reciprocal_row_norms = lax.dynamic_slice_in_dim(reciprocal_norm, row_start, NI)
    similarity_scores = (
        unscaled_scores * reciprocal_row_norms[:, None] * reciprocal_norm[None, :] / CONTRAST_TEMP
    )
    key_index = jnp.arange(norms_all.shape[0])
    query_index = row_start + jnp.arange(NI)
    allowed = (live_all[None, :] > 0.5) & (key_index[None, :] != query_index[:, None])
    similarity_scores = jnp.where(allowed, similarity_scores, -1000000000.0)
    top_score = jnp.max(similarity_scores, axis=1, keepdims=True)
    log_total = top_score[:, 0] + jnp.log(jnp.sum(jnp.exp(similarity_scores - top_score), axis=1))
    return jnp.sum(live_slots * log_total) / live_count.astype(jnp.float32)


def adam_update(weight, moment, square, gradient, rate):
    moment_new = BETA_ONE * moment + (1.0 - BETA_ONE) * gradient
    square_new = BETA_TWO * square + (1.0 - BETA_TWO) * gradient * gradient
    moment_hat = moment_new / (1.0 - BETA_ONE**STEP_TIME)
    square_hat = square_new / (1.0 - BETA_TWO**STEP_TIME)
    weight_new = weight - rate * (
        moment_hat / (jnp.sqrt(square_hat) + ADAM_EPS) + WEIGHT_DECAY * weight
    )
    return (weight_new, moment_new, square_new)


def body(
    mask_features,
    grid_features,
    instance_cells,
    instance_counts,
    instance_labels,
    instance_masks,
    mask_convs,
    mask_convs_moment,
    mask_convs_square,
    grid_first,
    grid_first_moment,
    grid_first_square,
    grid_second,
    grid_second_moment,
    grid_second_square,
    class_conv,
    class_conv_moment,
    class_conv_square,
    mask_norms,
    mask_norms_moment,
    mask_norms_square,
    grid_norms,
    grid_norms_moment,
    grid_norms_square,
    class_bias,
    class_bias_moment,
    class_bias_square,
):
    image_total = lax.axis_size("dp")
    model_total = lax.axis_size("mp")
    data_index = lax.axis_index("dp")
    model_index = lax.axis_index("mp")
    mask_low, first_low, second_low, class_low = (
        lax.all_gather(mask_convs.astype(jnp.bfloat16), "dp", axis=2, tiled=True),
        lax.all_gather(grid_first.astype(jnp.bfloat16), "dp", axis=1, tiled=True),
        lax.all_gather(grid_second.astype(jnp.bfloat16), "dp", axis=1, tiled=True),
        lax.all_gather(class_conv.astype(jnp.bfloat16), "dp", axis=1, tiled=True),
    )
    mask_full, grid_full = (
        lax.all_gather(mask_features[0], "mp", axis=2, tiled=True),
        lax.all_gather(grid_features[0], "mp", axis=2, tiled=True),
    )
    mask_width = mask_full.shape[2] // GROUPS
    grid_width = first_low.shape[2] * model_total // GROUPS
    mask_norm_act = partial(norm_act, group_width=mask_width)
    grid_norm_act = partial(norm_act, group_width=grid_width)
    first_mask = convolve(mask_full, mask_low[0])
    first_grid = convolve(grid_full, first_low)
    hidden_mask, back_mask_one = jax.vjp(mask_norm_act, first_mask, mask_norms[0], mask_norms[1])
    hidden_grid, back_grid_one = jax.vjp(grid_norm_act, first_grid, grid_norms[0], grid_norms[1])
    hidden_mask_full, hidden_grid_full = (
        lax.all_gather(hidden_mask.astype(jnp.bfloat16), "mp", axis=2, tiled=True),
        lax.all_gather(hidden_grid.astype(jnp.bfloat16), "mp", axis=2, tiled=True),
    )
    second_mask = convolve(hidden_mask_full, mask_low[1])
    kernels = convolve(hidden_grid_full, second_low)
    class_part = convolve(hidden_grid_full, class_low)
    feature_map, back_mask_two = jax.vjp(mask_norm_act, second_mask, mask_norms[2], mask_norms[3])
    local_width = feature_map.shape[2]
    feature_low = feature_map.astype(jnp.bfloat16).reshape(-1, local_width)
    kernel_flat = kernels.reshape(-1, local_width)
    cell_ids = instance_cells[0]
    kernel_rows = jnp.take(kernel_flat, cell_ids, axis=0).astype(jnp.bfloat16)
    joined = lax.all_gather(kernel_rows, ("dp", "mp"), axis=0, tiled=True)
    kernel_all = (
        joined.reshape(image_total, model_total, NI, local_width)
        .transpose(0, 2, 1, 3)
        .reshape(image_total * NI, model_total * local_width)
    )
    row_start = data_index * NI
    kernel_full = lax.dynamic_slice_in_dim(kernel_all, row_start, NI, 0)
    unscaled_scores = jnp.dot(kernel_full, kernel_all.T, preferred_element_type=jnp.float32)
    norms_all = jnp.sum(jnp.square(kernel_all.astype(jnp.float32)), axis=1)
    live_count = lax.dynamic_index_in_dim(instance_counts, data_index, keepdims=False)
    live_slots = (jnp.arange(NI) < live_count).astype(jnp.float32)
    live_all = (jnp.arange(NI)[None, :] < instance_counts[:, None]).astype(jnp.float32).reshape(-1)
    mask_cols = instance_masks[0].T.astype(jnp.float32)
    mask_sum = jnp.sum(mask_cols, axis=0)
    logits = lax.psum(
        jnp.dot(feature_low, kernel_rows.T, preferred_element_type=jnp.float32).astype(
            jnp.bfloat16
        ),
        "mp",
    ).astype(jnp.float32)
    (intersection, squares_sum), back_pixels = jax.vjp(
        partial(pixel_sums, mask_cols=mask_cols), logits
    )
    class_width = class_part.shape[2]
    class_logits = class_part.reshape(-1, class_width) + class_bias

    def loss_heads(class_in, score_in, norm_in, intersection_in, squares_in):
        focal_loss = focal_part(
            class_in,
            cell_ids,
            live_slots,
            live_count,
            instance_labels[0],
            model_index * class_width,
        )
        rest_loss = DICE_WEIGHT * dice_from(
            intersection_in, squares_in, mask_sum, live_slots, live_count
        ) + contrast_loss(score_in, norm_in, row_start, live_slots, live_count, live_all)
        return (focal_loss, rest_loss)

    (focal_loss, rest_loss), back_heads = jax.vjp(
        loss_heads, class_logits, unscaled_scores, norms_all, intersection, squares_sum
    )
    image_share = jnp.float32(1.0 / image_total)
    grad_class, grad_scores, grad_norms_all, grad_intersection, grad_squares = back_heads(
        (image_share, image_share)
    )
    grad_logits = back_pixels((grad_intersection, grad_squares))[0]
    logit_low = grad_logits.astype(jnp.bfloat16)
    score_low = grad_scores.astype(jnp.bfloat16)
    first_model = (model_index == 0).astype(jnp.float32)
    key_terms = first_model * (
        jnp.dot(score_low.T, kernel_full, preferred_element_type=jnp.float32)
        + 2.0 * kernel_all.astype(jnp.float32) * grad_norms_all[:, None]
    )
    own_terms = first_model * jnp.dot(score_low, kernel_all, preferred_element_type=jnp.float32)
    grad_feature = jnp.dot(logit_low, kernel_rows, preferred_element_type=jnp.float32).reshape(
        feature_map.shape
    )
    logit_rows = jnp.dot(logit_low.T, feature_low, preferred_element_type=jnp.float32)
    key_terms = lax.dynamic_update_slice_in_dim(
        key_terms, lax.dynamic_slice_in_dim(key_terms, row_start, NI, 0) + own_terms, row_start, 0
    )
    ordered = (
        key_terms.reshape(image_total, NI, model_total, local_width)
        .transpose(0, 2, 1, 3)
        .reshape(-1, local_width)
    )
    grad_rows = (
        lax.psum_scatter(ordered, ("dp", "mp"), scatter_dimension=0, tiled=True) + logit_rows
    )
    grad_second_mask, grad_gain_three, grad_bias_three = back_mask_two(grad_feature)
    grad_kernels = jnp.zeros(kernel_flat.shape, jnp.float32).at[cell_ids].add(grad_rows)
    class_gradient_reduced = grad_class.astype(jnp.bfloat16)
    grad_class_bias = jnp.sum(class_gradient_reduced.astype(jnp.float32), axis=0)
    mask_grad_low = grad_second_mask.astype(jnp.bfloat16)
    kernel_grad_low = grad_kernels.astype(jnp.bfloat16).reshape(kernels.shape)
    class_grad_map = class_gradient_reduced.reshape(class_part.shape)
    grad_mask_second = conv_weight_grad(hidden_mask_full, mask_grad_low)
    grad_grid_second = conv_weight_grad(hidden_grid_full, kernel_grad_low)
    grad_class_conv = conv_weight_grad(hidden_grid_full, class_grad_map)
    grid_input_terms = conv_input_grad(kernel_grad_low, second_low) + conv_input_grad(
        class_grad_map, class_low
    )
    grad_hidden_mask, grad_hidden_grid = (
        lax.psum_scatter(
            conv_input_grad(mask_grad_low, mask_low[1]).astype(jnp.bfloat16),
            "mp",
            scatter_dimension=2,
            tiled=True,
        ).astype(jnp.float32),
        lax.psum_scatter(
            grid_input_terms.astype(jnp.bfloat16), "mp", scatter_dimension=2, tiled=True
        ).astype(jnp.float32),
    )
    grad_first_mask, grad_gain_one, grad_bias_one = back_mask_one(grad_hidden_mask)
    grad_first_grid, grad_gain_five, grad_bias_five = back_grid_one(grad_hidden_grid)
    grad_mask_convs = jnp.stack(
        [conv_weight_grad(mask_full, grad_first_mask.astype(jnp.bfloat16)), grad_mask_second]
    )
    grad_grid_first = conv_weight_grad(grid_full, grad_first_grid.astype(jnp.bfloat16))
    mask_sum_w, first_sum_w, second_sum_w, class_sum_w = (
        lax.psum_scatter(grad_mask_convs, "dp", scatter_dimension=2, tiled=True),
        lax.psum_scatter(grad_grid_first, "dp", scatter_dimension=1, tiled=True),
        lax.psum_scatter(grad_grid_second, "dp", scatter_dimension=1, tiled=True),
        lax.psum_scatter(grad_class_conv, "dp", scatter_dimension=1, tiled=True),
    )
    mask_norm_grad = jnp.stack([grad_gain_one, grad_bias_one, grad_gain_three, grad_bias_three])
    grid_norm_grad = jnp.stack([grad_gain_five, grad_bias_five])
    mask_norm_sum, grid_norm_sum, bias_sum = lax.psum(
        (mask_norm_grad, grid_norm_grad, grad_class_bias), "dp"
    )
    first_device = (data_index == 0).astype(jnp.float32)
    squares = (
        jnp.sum(jnp.square(mask_sum_w))
        + jnp.sum(jnp.square(first_sum_w))
        + jnp.sum(jnp.square(second_sum_w))
        + jnp.sum(jnp.square(class_sum_w))
        + first_device
        * (
            jnp.sum(jnp.square(mask_norm_sum))
            + jnp.sum(jnp.square(grid_norm_sum))
            + jnp.sum(jnp.square(bias_sum))
        )
    )
    loss_part = (focal_loss + first_model * rest_loss) * image_share
    total_squares, step_loss = lax.psum((squares, loss_part), ("dp", "mp"))
    gradient_norm = jnp.sqrt(total_squares)
    factor = jnp.minimum(1.0, CLIP_LIMIT / gradient_norm)
    mask_new = adam_update(
        mask_convs, mask_convs_moment, mask_convs_square, mask_sum_w * factor, LEARN_RATE
    )
    first_new = adam_update(
        grid_first, grid_first_moment, grid_first_square, first_sum_w * factor, LEARN_RATE
    )
    second_new = adam_update(
        grid_second, grid_second_moment, grid_second_square, second_sum_w * factor, LEARN_RATE
    )
    class_new = adam_update(
        class_conv, class_conv_moment, class_conv_square, class_sum_w * factor, LEARN_RATE
    )
    mask_norm_new = adam_update(
        mask_norms, mask_norms_moment, mask_norms_square, mask_norm_sum * factor, SMALL_RATE
    )
    grid_norm_new = adam_update(
        grid_norms, grid_norms_moment, grid_norms_square, grid_norm_sum * factor, SMALL_RATE
    )
    bias_new = adam_update(
        class_bias, class_bias_moment, class_bias_square, bias_sum * factor, SMALL_RATE
    )
    return (
        step_loss,
        gradient_norm,
        mask_new[0],
        mask_new[1],
        mask_new[2],
        first_new[0],
        first_new[1],
        first_new[2],
        second_new[0],
        second_new[1],
        second_new[2],
        class_new[0],
        class_new[1],
        class_new[2],
        mask_norm_new[0],
        mask_norm_new[1],
        mask_norm_new[2],
        grid_norm_new[0],
        grid_norm_new[1],
        grid_norm_new[2],
        bias_new[0],
        bias_new[1],
        bias_new[2],
    )


def solution(mesh):
    in_specs = (
        P("dp", None, None, "mp"),
        P("dp", None, None, "mp"),
        P("dp", None),
        P(),
        P("dp", None),
        P("dp", None, None),
        P(None, None, "dp", "mp"),
        P(None, None, "dp", "mp"),
        P(None, None, "dp", "mp"),
        P(None, "dp", "mp"),
        P(None, "dp", "mp"),
        P(None, "dp", "mp"),
        P(None, "dp", "mp"),
        P(None, "dp", "mp"),
        P(None, "dp", "mp"),
        P(None, "dp", "mp"),
        P(None, "dp", "mp"),
        P(None, "dp", "mp"),
        P(None, "mp"),
        P(None, "mp"),
        P(None, "mp"),
        P(None, "mp"),
        P(None, "mp"),
        P(None, "mp"),
        P("mp"),
        P("mp"),
        P("mp"),
    )
    out_specs = (
        P(),
        P(),
        P(None, None, "dp", "mp"),
        P(None, None, "dp", "mp"),
        P(None, None, "dp", "mp"),
        P(None, "dp", "mp"),
        P(None, "dp", "mp"),
        P(None, "dp", "mp"),
        P(None, "dp", "mp"),
        P(None, "dp", "mp"),
        P(None, "dp", "mp"),
        P(None, "dp", "mp"),
        P(None, "dp", "mp"),
        P(None, "dp", "mp"),
        P(None, "mp"),
        P(None, "mp"),
        P(None, "mp"),
        P(None, "mp"),
        P(None, "mp"),
        P(None, "mp"),
        P("mp"),
        P("mp"),
        P("mp"),
    )
    return jax.shard_map(body, mesh=mesh, in_specs=in_specs, out_specs=out_specs, check_vma=False)
```

profile of v0, /device:TPU:0, one launch (start us, length us, event | category | flops | bytes accessed | tf_op | source)
XLA Modules:
  0.0 1036.8 jit_solution(8418053553196495641)
XLA Ops:
  11.3 2.7 all-gather
  14.0 54.3 %all-gather.10.cloned.1.call-done = bf16[9,256,256]{2,1,0:T(8,128)(2,1)} async-done(((bf16[9,16,256]{2,1,0:T(8,128)(2,1)}), bf16[9,256,256]{2,1,0:T(8,128)(2,1)}) %all-gather.10.cloned.1.call-update) | async-done | bytes 1179664 | tf_op jit(solution)/shard_map/all_gather | solution.py:184
  79.1 49.4 %all_gather.30 = bf16[9,512,40]{2,1,0:T(8,128)(2,1)} all-gather(bf16[9,32,40]{2,1,0:T(8,128)(2,1)S(1)} %convert_element_type.134), channel_id=1, replica_groups=mesh['dp'=16,'mp'=2] {'dp'}, dimensions={1}, use_global_device_ids=true | all-gather | bytes 391680 | tf_op jit(solution)/shard_map/all_gather | solution.py:186
  128.7 2.6 fusion.78
  131.4 11.1 %all-gather.14.cloned.1.call-done = bf16[2,9,256,128]{3,2,1,0:T(8,128)(2,1)} async-done(((bf16[2,9,16,128]{3,2,1,0:T(8,128)(2,1)}), bf16[2,9,256,128]{3,2,1,0:T(8,128)(2,1)}) %all-gather.14.cloned.1.call-update) | async-done | bytes 1179664 | tf_op jit(solution)/shard_map/all_gather | solution.py:183
  142.5 2.4 fusion.40
  172.3 38.7 %all-gather.18.cloned.1.call-done = bf16[9,512,128]{2,1,0:T(8,128)(2,1)} async-done(((bf16[9,32,128]{2,1,0:T(8,128)(2,1)}), bf16[9,512,128]{2,1,0:T(8,128)(2,1)}) %all-gather.18.cloned.1.call-update) | async-done | bytes 1179664 | tf_op jit(solution)/shard_map/all_gather | solution.py:185
  218.7 42.5 %all-gather.2 = bf16[32,100,128]{2,1,0:T(8,128)(2,1)S(1)} all-gather(bf16[1,100,128]{2,1,0:T(8,128)(2,1)S(1)} %fusion.464), channel_id=1, replica_groups=mesh['dp'=16,'mp'=2] {'dp','mp'}, dimensions={0}, use_global_device_ids=true | all-gather | bytes 844800 | tf_op jit(solution)/shard_map/all_gather | solution.py:213
  261.2 3.9 multiply_reduce_fusion.12
  266.5 3.5 convert_reduce_fusion.1
  271.4 3.4 fusion.255
  274.8 2.4 fusion.254
  277.1 2.3 fusion.253
  279.4 2.3 fusion.252
  281.7 2.3 fusion.251
  283.9 2.4 fusion.249
  286.3 2.4 fusion.8
  299.9 3.4 fusion.463
  312.6 3.2 fusion.250
  315.8 3.3 fusion.318
  319.1 7.6 all-reduce.13.cloned.1.call-done
  326.6 3.3 multiply_reduce_fusion.9
  335.8 2.9 reshape.386
  338.7 2.7 copy.291
  341.5 2.6 reshape.387
  344.1 80.7 %fusion = f32[112,128]{1,0:T(8,128)S(1)} fusion(f32[3200,128]{1,0:T(8,128)} %reshape.387), kind=kCustom, calls=%all-reduce-scatter | all-reduce-scatter fusion | flops 458753 | bytes 1695744
  427.5 2.3 collective-permute-start
  429.8 3.0 fusion.72
  432.9 3.0 multiply_reduce_fusion
  440.3 3.0 add_convert_fusion.3
  443.4 3.5 fusion.208
  446.9 3.7 fusion.210
  452.2 2.8 concatenate
  458.0 3.4 fusion.248
  461.4 2.3 fusion.247
  463.7 2.4 fusion.246
  466.1 2.4 fusion.245
  468.5 2.3 fusion.319
  470.8 2.4 fusion.244
  473.2 2.3 fusion.243
  475.5 2.3 fusion.241
  477.8 2.4 fusion.242
  480.2 19.5 %add_convert_fusion.1 = bf16[40,40,512]{2,1,0:T(8,128)(2,1)} fusion(f32[40,40,512]{2,1,0:T(8,128)} %fusion.255, f32[40,40,512]{2,1,0:T(8,128)} %fusion.254, f32[40,40,512]{2,1,0:T(8,128)} %fusion.253, f32[40,40,512]{2,1,0:T(8,128)} %fusion.318, f32[40,40,512]{2,1,0:T(8,128)} %fusion.252, f32[40,40,512]{2,1,0:T(8,128)} %fusion.251, ...), kind=kOutput, calls=%fused_computation.4 | convolution fusion | flops 80281600 | bytes 57603072 | tf_op jit(solution)/shard_map/hwd,cd->hwc/dot_general | solution.py:57
  500.0 3.5 fusion.212
  503.5 3.5 fusion.214
  507.0 3.5 fusion.216
  510.5 3.5 fusion.220
  514.1 3.6 fusion.218
  517.7 3.6 fusion.320
  521.3 10.6 %add_convert_fusion = bf16[32,128,256]{2,1,0:T(8,128)(2,1)} fusion(f32[32,128,256]{2,1,0:T(8,128)S(1)} %copy-done.11, f32[32,128,256]{2,1,0:T(8,128)S(1)} %copy-done.12, f32[32,128,256]{2,1,0:T(8,128)} %fusion.212, f32[32,128,256]{2,1,0:T(8,128)} %fusion.320, f32[32,128,256]{2,1,0:T(8,128)} %fusion.214, f32[32,128,256]{2,1,0:T(8,128)} %fusion.216, ...), kind=kOutput, calls=%fused_computation.3 | convolution fusion | flops 277872640 | bytes 36765696 | tf_op jit(solution)/shard_map/hwd,cd->hwc/dot_general | solution.py:57
  531.9 4.6 copy.261
  536.5 4.0 copy.290
  550.8 4.5 copy.263
  555.4 4.1 reshape.503
  580.9 2.5 multiply_reduce_fusion.10
  586.1 2.4 add_convert_fusion.4
  604.7 2.6 copy.277
  620.8 2.8 pad_maximum_fusion
  627.0 55.7 %reduce-scatter.23.cloned.1.call-done = f32[32,360]{1,0:T(8,128)} async-done(((f32[512,360]{1,0:T(8,128)}), f32[32,360]{1,0:T(8,128)}) %reduce-scatter.23.cloned.1.call-update) | async-done | bytes 46096
  684.5 40.7 %all-reduce.10 = (f32[4,128]{1,0:T(4,128)S(1)}, f32[2,256]{1,0:T(2,128)S(1)}, f32[40]{0:T(128)S(1)}) all-reduce(f32[4,128]{1,0:T(4,128)S(1)} %pad_maximum_fusion.1, f32[2,256]{1,0:T(2,128)S(1)} %pad_maximum_fusion.2, f32[40]{0:T(128)S(1)} %copy-done.76), channel_id=1, replica_groups=mesh['dp'=16,'mp'=2] {'dp'}, use_global_device_ids=true, to_apply=%region_61.63 | all-reduce | flops 1064 | bytes 8512 | tf_op jit(solution)/shard_map/psum | solution.py:323
  729.1 37.0 %reduce-scatter.19.cloned.1.call-done = f32[9,32,128]{2,1,0:T(8,128)} async-done(((f32[9,512,128]{2,1,0:T(8,128)}), f32[9,32,128]{2,1,0:T(8,128)}) %reduce-scatter.19.cloned.1.call-update) | async-done | bytes 147472 | tf_op jit(solution)/shard_map/reduce_scatter | solution.py:318
  767.6 79.1 %reduce-scatter.17.cloned.1.call-done = f32[9,16,256]{2,1,0:T(8,128)} async-done(((f32[9,256,256]{2,1,0:T(8,128)}), f32[9,16,256]{2,1,0:T(8,128)}) %reduce-scatter.17.cloned.1.call-update) | async-done | bytes 147472 | tf_op jit(solution)/shard_map/reduce_scatter | solution.py:317
  848.4 128.5 %reduce-scatter.13.cloned.1.call-done = f32[2,9,16,128]{3,2,1,0:T(8,128)} async-done(((f32[2,9,256,128]{3,2,1,0:T(8,128)}), f32[2,9,16,128]{3,2,1,0:T(8,128)}) %reduce-scatter.13.cloned.1.call-update) | async-done | bytes 147472 | tf_op jit(solution)/shard_map/reduce_scatter | solution.py:316
  981.2 40.1 %all-reduce.9 = (f32[]{:T(128)}, f32[]{:T(128)}) all-reduce(f32[]{:T(128)S(6)} %mul.752, f32[]{:T(128)S(6)} %add.644), channel_id=1, replica_groups=mesh['dp'=16,'mp'=2] {'dp','mp'}, use_global_device_ids=true, to_apply=%region_22.24 | all-reduce | flops 2 | bytes 16 | tf_op jit(solution)/shard_map/psum | solution.py:340
  (437 shorter events, 170.2 us)
Async XLA Ops:
  7.2 6.8 copy-start.59
  7.2 61.1 %all-gather.10.cloned.1.call-start = ((), (), s32[]{:S(2)}) async-start(), calls=%async_computation.6 | async-start | bytes 1253376 | tf_op jit(solution)/shard_map/all_gather | solution.py:184
  8.8 122.6 %all-gather.20.cloned.1.call-start = ((), (), s32[]{:S(2)}) async-start(), calls=%async_computation.16 | async-start | bytes 3145728 | tf_op jit(solution)/shard_map/all_gather | solution.py:189
  9.6 132.9 %all-gather.14.cloned.1.call-start = ((), (), s32[]{:S(2)}) async-start(), calls=%async_computation.8 | async-start | bytes 1253376 | tf_op jit(solution)/shard_map/all_gather | solution.py:183
  11.2 150.5 %all-gather.12.cloned.1.call-start = ((), (), s32[]{:S(2)}) async-start(), calls=%async_computation.7 | async-start | bytes 2457600 | tf_op jit(solution)/shard_map/all_gather | solution.py:202
  13.9 58.6 %copy-start.5 = (bf16[1,40,40,256]{3,2,1,0:T(8,128)(2,1)}, bf16[1,40,40,256]{3,2,1,0:T(8,128)(2,1)S(1)}, u32[]{:S(2)}) copy-start(bf16[1,40,40,256]{3,2,1,0:T(8,128)(2,1)S(1)} %all-gather) | copy-start | bytes 2457604
  14.0 61.0 %copy-start.53 = (f32[1,256]{1,0:T(1,128)}, f32[1,256]{1,0:T(1,128)S(1)}, u32[]{:S(2)}) copy-start(f32[1,256]{1,0:T(1,128)S(1)} %get-tuple-element.181) | copy-start | bytes 3076
  14.0 61.0 %copy-start.55 = (f32[1,256]{1,0:T(1,128)}, f32[1,256]{1,0:T(1,128)S(1)}, u32[]{:S(2)}) copy-start(f32[1,256]{1,0:T(1,128)S(1)} %get-tuple-element.182) | copy-start | bytes 3076
  73.4 71.5 %copy-start.10 = (f32[40,40,256]{2,1,0:T(8,128)}, f32[40,40,256]{2,1,0:T(8,128)S(1)}, u32[]{:S(2)}) copy-start(f32[40,40,256]{2,1,0:T(8,128)S(1)} %get-tuple-element.189) | copy-start | bytes 4915204
  74.0 4.8 copy-start.84
  74.1 5.1 copy-start.35
  74.9 4.2 copy-start.51
  75.0 53.7 %copy-start.57 = (f32[4,128]{1,0:T(4,128)S(1)}, f32[4,128]{1,0:T(4,128)}, u32[]{:S(2)}) copy-start(f32[4,128]{1,0:T(4,128)} %param.46) | copy-start | bytes 6148
  76.2 134.8 %all-gather.18.cloned.1.call-start = ((), (), s32[]{:S(2)}) async-start(), calls=%async_computation.10 | async-start | bytes 1253376 | tf_op jit(solution)/shard_map/all_gather | solution.py:185
  76.9 209.4 %all-gather.16.cloned.1.call-start = ((), (), s32[]{:S(2)}) async-start(), calls=%async_computation.9 | async-start | bytes 3145728 | tf_op jit(solution)/shard_map/all_gather | solution.py:201
  128.6 31.1 %copy-start.63 = (f32[128]{0:T(128)}, f32[128]{0:T(128)S(1)}, u32[]{:S(2)}) copy-start(f32[128]{0:T(128)S(1)} %get-tuple-element.178) | copy-start | bytes 1540
  128.6 31.1 %copy-start.65 = (f32[128]{0:T(128)}, f32[128]{0:T(128)S(1)}, u32[]{:S(2)}) copy-start(f32[128]{0:T(128)S(1)} %get-tuple-element.179) | copy-start | bytes 1540
  161.2 165.4 %all-reduce.13.cloned.1.call-start = ((), (), s32[]{:S(2)}) async-start(), calls=%async_computation.11 | async-start | bytes 1703936 | tf_op jit(solution)/shard_map/psum | solution.py:228
  265.4 4.6 copy-start.17
  310.9 270.0 %reduce-scatter.15.cloned.1.call-start = ((), (), s32[]{:S(2)}) async-start(), calls=%async_computation.13 | async-start | bytes 2457600 | tf_op jit(solution)/shard_map/reduce_scatter | solution.py:305
  326.6 5.5 copy-start.18
  341.5 88.4 %copy-start.26 = (bf16[4096,100]{0,1:T(8,128)(2,1)S(1)}, bf16[4096,100]{0,1:T(8,128)(2,1)}, u32[]{:S(2)}) copy-start(bf16[4096,100]{0,1:T(8,128)(2,1)} %all-reduce.13.cloned.1.call-done) | copy-start | bytes 2457604
  424.8 8.1 copy-start.9
  424.8 26.1 %collective-permute-start.2 = (f32[112,128]{1,0:T(8,128)S(1)}, f32[112,128]{1,0:T(8,128)S(1)}, u32[]{:S(2)}, u32[]{:S(2)}) collective-permute-start(f32[112,128]{1,0:T(8,128)S(1)} %fusion), channel_id=1, source_target_pairs={{0,3},{1,4},{2,5},{3,6},{4,7},{5,8},{6,9},{7,10},{8,11},{9,12},{10... | collective-permute-start | bytes 172040
  426.2 24.7 %collective-permute-start.1 = (f32[112,128]{1,0:T(8,128)S(1)}, f32[112,128]{1,0:T(8,128)S(1)}, u32[]{:S(2)}, u32[]{:S(2)}) collective-permute-start(f32[112,128]{1,0:T(8,128)S(1)} %fusion), channel_id=1, source_target_pairs={{0,2},{1,3},{2,4},{3,5},{4,6},{5,7},{6,8},{7,9},{8,10},{9,11},{10,... | collective-permute-start | bytes 172040
  427.5 24.7 %collective-permute-start = (f32[112,128]{1,0:T(8,128)S(1)}, f32[112,128]{1,0:T(8,128)}, u32[]{:S(2)}, u32[]{:S(2)}) collective-permute-start(f32[112,128]{1,0:T(8,128)S(1)} %fusion), channel_id=1, source_target_pairs={{0,1},{1,2},{2,3},{3,4},{4,5},{5,6},{6,7},{7,8},{8,9},{9,10},{10,1... | collective-permute-start | bytes 172040
  439.0 11.9 %collective-permute-start.3 = (f32[36,128]{1,0:T(8,128)S(1)}, f32[36,128]{1,0:T(8,128)S(1)}, u32[]{:S(2)}, u32[]{:S(2)}) collective-permute-start(f32[36,128]{1,0:T(8,128)S(1)} %slice.602), channel_id=1, source_target_pairs={{0,4},{1,5},{2,6},{3,7},{4,8},{5,9},{6,10},{7,11},{8,12},{9,13},{1... | collective-permute-start | bytes 55304
  499.8 104.9 %reduce-scatter.21.cloned.1.call-start = ((), (), s32[]{:S(2)}) async-start(), calls=%async_computation.17 | async-start | bytes 3145728
  514.1 7.3 copy-start.12
  540.5 142.2 %reduce-scatter.23.cloned.1.call-start = ((), (), s32[]{:S(2)}) async-start(), calls=%async_computation.18 | async-start | bytes 835584
  559.5 206.6 %reduce-scatter.19.cloned.1.call-start = ((), (), s32[]{:S(2)}) async-start(), calls=%async_computation.15 | async-start | bytes 2506752 | tf_op jit(solution)/shard_map/reduce_scatter | solution.py:318
  572.2 274.5 %reduce-scatter.17.cloned.1.call-start = ((), (), s32[]{:S(2)}) async-start(), calls=%async_computation.14 | async-start | bytes 2506752 | tf_op jit(solution)/shard_map/reduce_scatter | solution.py:317
  579.5 4.2 copy-start.75
  598.9 378.0 %reduce-scatter.13.cloned.1.call-start = ((), (), s32[]{:S(2)}) async-start(), calls=%async_computation.12 | async-start | bytes 2506752 | tf_op jit(solution)/shard_map/reduce_scatter | solution.py:316
  604.7 4.7 copy-start.8
  604.7 4.7 copy-start.50
  604.7 4.7 copy-start.62
  604.7 4.7 copy-start.64
  604.7 4.7 copy-start.66
  623.7 60.8 %copy-start.67 = (f32[128]{0:T(128)S(1)}, f32[128]{0:T(128)}, u32[]{:S(2)}) copy-start(f32[128]{0:T(128)} %get-tuple-element.123) | copy-start | bytes 1540
  623.7 60.8 %copy-start.68 = (f32[128]{0:T(128)S(1)}, f32[128]{0:T(128)}, u32[]{:S(2)}) copy-start(f32[128]{0:T(128)} %get-tuple-element.126) | copy-start | bytes 1540
  623.7 60.9 %copy-start.76 = (f32[40]{0:T(128)S(1)}, f32[40]{0:T(128)}, u32[]{:S(2)}) copy-start(f32[40]{0:T(128)} %get-tuple-element.167) | copy-start | bytes 484
  623.7 357.4 %copy-start.44 = (f32[9,32,40]{2,1,0:T(8,128)S(1)}, f32[9,32,40]{2,1,0:T(8,128)}, u32[]{:S(2)}) copy-start(f32[9,32,40]{2,1,0:T(8,128)} %param.45) | copy-start | bytes 138244
  624.8 399.8 %copy-start.58 = (f32[4,128]{1,0:T(4,128)S(1)}, f32[4,128]{1,0:T(4,128)}, u32[]{:S(2)}) copy-start(f32[4,128]{1,0:T(4,128)} %param.46) | copy-start | bytes 6148
  624.8 399.8 %copy-start.69 = (f32[4,128]{1,0:T(4,128)S(1)}, f32[4,128]{1,0:T(4,128)}, u32[]{:S(2)}) copy-start(f32[4,128]{1,0:T(4,128)} %param.47) | copy-start | bytes 6148
  624.8 399.8 %copy-start.70 = (f32[4,128]{1,0:T(4,128)S(1)}, f32[4,128]{1,0:T(4,128)}, u32[]{:S(2)}) copy-start(f32[4,128]{1,0:T(4,128)} %param.48) | copy-start | bytes 6148
  624.8 400.4 %copy-start.60 = (f32[2,256]{1,0:T(2,128)S(1)}, f32[2,256]{1,0:T(2,128)}, u32[]{:S(2)}) copy-start(f32[2,256]{1,0:T(2,128)} %param.49) | copy-start | bytes 6148
  624.9 400.4 %copy-start.71 = (f32[2,256]{1,0:T(2,128)S(1)}, f32[2,256]{1,0:T(2,128)}, u32[]{:S(2)}) copy-start(f32[2,256]{1,0:T(2,128)} %param.50) | copy-start | bytes 6148
  624.9 400.4 %copy-start.72 = (f32[2,256]{1,0:T(2,128)S(1)}, f32[2,256]{1,0:T(2,128)}, u32[]{:S(2)}) copy-start(f32[2,256]{1,0:T(2,128)} %param.51) | copy-start | bytes 6148
  626.3 399.6 %copy-start.80 = (f32[40]{0:T(128)S(1)}, f32[40]{0:T(128)}, u32[]{:S(2)}) copy-start(f32[40]{0:T(128)} %param.52) | copy-start | bytes 484
  626.3 399.6 %copy-start.81 = (f32[40]{0:T(128)S(1)}, f32[40]{0:T(128)}, u32[]{:S(2)}) copy-start(f32[40]{0:T(128)} %param.53) | copy-start | bytes 484
  626.3 399.6 %copy-start.82 = (f32[40]{0:T(128)S(1)}, f32[40]{0:T(128)}, u32[]{:S(2)}) copy-start(f32[40]{0:T(128)} %param.54) | copy-start | bytes 484
  627.0 399.4 %copy-start.28 = (f32[2,9,16,128]{3,2,1,0:T(8,128)S(1)}, f32[2,9,16,128]{3,2,1,0:T(8,128)}, u32[]{:S(2)}) copy-start(f32[2,9,16,128]{3,2,1,0:T(8,128)} %param.34) | copy-start | bytes 442372
  627.0 399.4 %copy-start.37 = (f32[2,9,16,128]{3,2,1,0:T(8,128)S(1)}, f32[2,9,16,128]{3,2,1,0:T(8,128)}, u32[]{:S(2)}) copy-start(f32[2,9,16,128]{3,2,1,0:T(8,128)} %param.35) | copy-start | bytes 442372
  627.0 399.4 %copy-start.38 = (f32[2,9,16,128]{3,2,1,0:T(8,128)S(1)}, f32[2,9,16,128]{3,2,1,0:T(8,128)}, u32[]{:S(2)}) copy-start(f32[2,9,16,128]{3,2,1,0:T(8,128)} %param.36) | copy-start | bytes 442372
  729.0 298.2 %copy-start.29 = (f32[9,16,256]{2,1,0:T(8,128)S(1)}, f32[9,16,256]{2,1,0:T(8,128)}, u32[]{:S(2)}) copy-start(f32[9,16,256]{2,1,0:T(8,128)} %param.37) | copy-start | bytes 442372
  729.1 298.2 %copy-start.39 = (f32[9,16,256]{2,1,0:T(8,128)S(1)}, f32[9,16,256]{2,1,0:T(8,128)}, u32[]{:S(2)}) copy-start(f32[9,16,256]{2,1,0:T(8,128)} %param.38) | copy-start | bytes 442372
  729.1 298.2 %copy-start.40 = (f32[9,16,256]{2,1,0:T(8,128)S(1)}, f32[9,16,256]{2,1,0:T(8,128)}, u32[]{:S(2)}) copy-start(f32[9,16,256]{2,1,0:T(8,128)} %param.39) | copy-start | bytes 442372
  846.8 180.5 %copy-start.33 = (f32[9,16,256]{2,1,0:T(8,128)S(1)}, f32[9,16,256]{2,1,0:T(8,128)}, u32[]{:S(2)}) copy-start(f32[9,16,256]{2,1,0:T(8,128)} %reduce-scatter.17.cloned.1.call-done) | copy-start | bytes 442372
  976.9 49.5 %copy-start.34 = (f32[2,9,16,128]{3,2,1,0:T(8,128)S(1)}, f32[2,9,16,128]{3,2,1,0:T(8,128)}, u32[]{:S(2)}) copy-start(f32[2,9,16,128]{3,2,1,0:T(8,128)} %reduce-scatter.13.cloned.1.call-done) | copy-start | bytes 442372
  1022.1 6.0 copy-start.31
  1022.1 6.0 copy-start.32
  1022.1 6.0 copy-start.41
  1022.1 6.0 copy-start.42
  (38 other events, 72.9 us)
Sparse Core Ops, SparseCore 0:
  11.3 56.9 all-gather.9
  69.8 9.6 all-gather.19
  82.8 59.5 all-gather.13
  143.9 8.4 all-gather.11
  155.5 55.4 all-gather.17
  212.4 9.7 all-gather.15
  311.1 15.5 all-reduce.12
  499.9 9.7 reduce-scatter.14
  540.6 10.1 reduce-scatter.20
  559.6 123.1 reduce-scatter.22
  685.1 80.8 reduce-scatter.18
  768.3 78.3 reduce-scatter.16
  852.4 124.4 reduce-scatter.12
where the time goes:
time: 1040 us
  waiting for transfers between devices  413 us (40%)
  blocking collectives  256 us (25%)
  matrix products  217 us (21%)
  other arithmetic  62.9 us (6%)
  local copies, waits for them, and re-layouts  54.7 us (5%)
  between operations  24.9 us (2%)
    reduce_scatter x1, waiting for transfers between devices, body(): lax.psum_scatter(grad_mask_convs, 'dp', scatter_dimension=2, tiled=True)  129 us
    dot_general x27, matrix products, conv_input_grad(): jnp.einsum('hwd,cd->hwc', shifted_view(padded, tap_index, height, columns...  102 us
    unnamed x1, blocking collectives  80.7 us
    reduce_scatter x1, waiting for transfers between devices, body(): lax.psum_scatter(grad_grid_first, 'dp', scatter_dimension=1, tiled=True)  79.1 us
    unnamed x19, waiting for transfers between devices  56.6 us
    all_gather x1, waiting for transfers between devices, body(): lax.all_gather(grid_first.astype(jnp.bfloat16), 'dp', axis=1, tiled=True)  54.3 us
    dot_general x45, matrix products, conv_weight_grad(): jnp.einsum('hwc,hwd->cd', shifted_view(padded, tap_index, height, columns...  52.8 us
    dot_general x45, matrix products, convolve(): jnp.einsum('hwc,cd->hwd', shifted_view(padded, tap_index, height, columns...  52.5 us
  transfers between devices with their start and end apart: 17, of which 8 were waited for; matrix products, arithmetic and copies ran while one was open for 22% of the time, Pallas kernels for 0%

commit v1 on v0

--- a/solution.py
+++ b/solution.py
@@ -3,6 +3,8 @@
 import jax
 import jax.numpy as jnp
 from jax import lax
+from jax.experimental import pallas as pl
+from jax.experimental.pallas import tpu as pltpu
 from jax.sharding import PartitionSpec as P
 
 GROUPS = 32
@@ -23,6 +25,587 @@
 DICE_WEIGHT = 3.0
 STEP_TIME = 10.0
 HIGHEST = lax.Precision.HIGHEST
+
+
+MESH = pl.DeviceIdType.MESH
+VMEM = pltpu.VMEM
+ANY = pl.ANY
+VMEM_LIMIT = 60 * 2**20
+F32 = jnp.float32
+BF16 = jnp.bfloat16
+
+
+def line_lengths(total):
+    if total & (total - 1):
+        return (total, 1, 1)
+    bits = total.bit_length() - 1
+    last = bits // 3
+    middle = (bits - last) // 2
+    return (1 << (bits - last - middle), 1 << middle, 1 << last)
+
+
+def place(dims):
+    index = lax.axis_index("dp")
+    return (index // (dims[1] * dims[2]), (index // dims[2]) % dims[1], index % dims[2])
+
+
+def along(dims, axis, step):
+    stride = (dims[1] * dims[2], dims[2], 1)[axis]
+    return {"dp": lax.axis_index("dp") + step * stride}
+
+
+def partner():
+    return {"mp": 1 - lax.axis_index("mp")}
+
+
+def greet_lines(dims, pair):
+    sem = pltpu.get_barrier_semaphore()
+    pos = place(dims)
+    count = jnp.int32(0)
+    for axis in range(3):
+        for step in (-1, 1):
+            there = (pos[axis] + step >= 0) & (pos[axis] + step < dims[axis])
+
+            @pl.when(there)
+            def _(axis=axis, step=step):
+                pl.semaphore_signal(
+                    sem, inc=1, device_id=along(dims, axis, step), device_id_type=MESH
+                )
+
+            count = count + there.astype(jnp.int32)
+    if pair:
+        pl.semaphore_signal(sem, inc=1, device_id=partner(), device_id_type=MESH)
+        count = count + 1
+    pl.semaphore_wait(sem, count)
+
+
+def greet_partner():
+    sem = pltpu.get_barrier_semaphore()
+    pl.semaphore_signal(sem, inc=1, device_id=partner(), device_id_type=MESH)
+    pl.semaphore_wait(sem, 1)
+
+
+def ring_step(dims, pos, axis, offset):
+    other = lax.rem(pos[axis] + offset, dims[axis])
+    return along(dims, axis, other - pos[axis])
+
+
+def greet_all_lines(dims):
+    sem = pltpu.get_barrier_semaphore()
+    pos = place(dims)
+    count = 1
+    for axis in range(3):
+        for offset in range(1, dims[axis]):
+            pl.semaphore_signal(
+                sem, inc=1, device_id=ring_step(dims, pos, axis, offset), device_id_type=MESH
+            )
+            count += 1
+    pl.semaphore_signal(sem, inc=1, device_id=partner(), device_id_type=MESH)
+    pl.semaphore_wait(sem, count)
+
+
+GATHER_ORDERS = ((2, 1, 0), (0, 2, 1), (0, 1, 2))
+REDUCE_ORDERS = tuple(tuple(reversed(order)) for order in GATHER_ORDERS)
+
+
+def rounds_of(dims, order):
+    return [
+        (stage, axis, step) for stage, axis in enumerate(order) for step in range(dims[axis] - 1)
+    ]
+
+
+def round_count(dims):
+    return sum(n - 1 for n in dims)
+
+
+def row_cuts(rows, unit=16):
+    if rows % unit or rows < 3 * unit:
+        return ((0, 0, rows),)
+    tiles = rows // unit
+    first = max(1, round(tiles * 0.2))
+    second = (tiles - first) // 2
+    sizes = (first, second, tiles - first - second)
+    cuts, start = [], 0
+    for order, size in enumerate(sizes):
+        cuts.append((order, start * unit, size * unit))
+        start += size
+    return tuple(cuts)
+
+
+class Flow:
+    def __init__(self, rounds):
+        self.rounds = rounds
+
+    def start(self, r):
+        for copy, sends, *_ in self.rounds[r]:
+
+            @pl.when(sends)
+            def _(copy=copy):
+                copy.start()
+
+    def finish(self, r):
+        for copy, _, receives, land in self.rounds[r]:
+
+            @pl.when(receives)
+            def _(copy=copy, land=land):
+                copy.wait_recv()
+                if land is not None:
+                    land()
+
+    def drain(self):
+        for copies in self.rounds:
+            for copy, sends, *_ in copies:
+
+                @pl.when(sends)
+                def _(copy=copy):
+                    copy.wait_send()
+
+
+def gather_flow(dims, out, send_sems, recv_sems, base, rows, order):
+    pos = place(dims)
+    result = []
+    for r, (stage, axis, step) in enumerate(rounds_of(dims, order)):
+        n, done = dims[axis], set(order[:stage])
+        copies = []
+        for side, delta in ((0, 1), (1, -1)):
+            block = pos[axis] - delta * step
+            sends = (
+                (pos[axis] + delta >= 0)
+                & (pos[axis] + delta < n)
+                & (block >= 0)
+                & (block < n)
+            )
+            block = jnp.clip(block, 0, n - 1)
+            source = pos[axis] - delta * (1 + step)
+            receives = (source >= 0) & (source < n)
+            view = out.at[
+                tuple(
+                    pl.ds(0, dims[k]) if k in done else (block if k == axis else pos[k])
+                    for k in range(3)
+                )
+                + (rows,)
+            ]
+            copy = pltpu.make_async_remote_copy(
+                src_ref=view,
+                dst_ref=view,
+                send_sem=send_sems.at[base + 2 * r + side],
+                recv_sem=recv_sems.at[base + 2 * r + side],
+                device_id=along(dims, axis, delta),
+                device_id_type=MESH,
+            )
+            copies.append((copy, sends, receives, None))
+        result.append(copies)
+    return Flow(result)
+
+
+def landing_shapes(dims, rows, width, order):
+    shapes, left = [], {0, 1, 2}
+    for axis in order:
+        left = left - {axis}
+        n = dims[axis]
+        slots = max(1, n - 1) * (1 if n <= 2 else 2)
+        shapes.append((slots,) + tuple(dims[k] for k in sorted(left)) + (rows, width))
+    return shapes
+
+
+def reduce_flow(dims, total, staged, lands, send_sems, recv_sems, base, rows, order):
+    pos = place(dims)
+    result = []
+    for r, (stage, axis, step) in enumerate(rounds_of(dims, order)):
+        n, reduced = dims[axis], set(order[:stage])
+        free = [k for k in range(3) if k not in reduced and k != axis]
+
+        def view(block, lead=None, axis=axis, reduced=reduced):
+            lead = iter(lead) if lead is not None else None
+            index = []
+            for k in range(3):
+                if k == axis:
+                    index.append(block)
+                elif k in reduced:
+                    index.append(pos[k])
+                else:
+                    index.append(pl.ds(0, dims[k]) if lead is None else next(lead))
+            return tuple(index) + (rows,)
+
+        copies = []
+        for side, delta in ((0, 1), (1, -1)):
+            place_in_flow = pos[axis] if delta == 1 else n - 1 - pos[axis]
+            sends = place_in_flow <= step
+            block = n - 1 - step + place_in_flow
+            block = jnp.clip(block if delta == 1 else n - 1 - block, 0, n - 1)
+            receives = (place_in_flow >= 1) & (place_in_flow - 1 <= step)
+            taken = n - 1 - step + place_in_flow - 1
+            taken = jnp.clip(taken if delta == 1 else n - 1 - taken, 0, n - 1)
+            land_ref = lands[stage].at[step if n <= 2 else side * (n - 1) + step]
+            copy = pltpu.make_async_remote_copy(
+                src_ref=staged.at[view(block)],
+                dst_ref=land_ref,
+                send_sem=send_sems.at[base + 2 * r + side],
+                recv_sem=recv_sems.at[base + 2 * r + side],
+                device_id=along(dims, axis, delta),
+                device_id_type=MESH,
+            )
+
+            def land(taken=taken, land_ref=land_ref, free=free, view=view):
+                sizes = [dims[k] for k in free]
+                blocks = 1
+                for size in sizes:
+                    blocks *= size
+
+                def add(i, carry):
+                    lead, rest = [], i
+                    for size in reversed(sizes):
+                        lead.append(lax.rem(rest, size))
+                        rest = rest // size
+                    lead = lead[::-1]
+                    index = view(taken, lead)
+                    value = total[index] + land_ref[tuple(lead)].astype(F32)
+                    total[index] = value
+                    staged[index] = value.astype(BF16)
+                    return carry
+
+                if blocks == 1:
+                    add(jnp.int32(0), 0)
+                else:
+                    lax.fori_loop(0, blocks, add, 0)
+
+            copies.append((copy, sends, receives, land))
+        result.append(copies)
+    return Flow(result)
+
+
+def run_flows(flows, count):
+    for r in range(count + 1):
+        for flow in flows:
+            if r > 0:
+                flow.finish(r - 1)
+            if r < count:
+                flow.start(r)
+    for flow in flows:
+        flow.drain()
+
+
+def params(collective_id):
+    return pltpu.CompilerParams(
+        collective_id=collective_id, has_side_effects=True, vmem_limit_bytes=VMEM_LIMIT
+    )
+
+
+def gather_kernel(dims, count, maps, *refs):
+    shards, inputs = refs[:count], refs[count : count + maps]
+    at = count + maps
+    outs, fulls = refs[at : at + count], refs[at + count : at + count + maps]
+    send_sems, recv_sems, local_sems, pair_sems = refs[at + count + maps :]
+    pos = place(dims)
+    model = lax.axis_index("mp")
+    local = []
+    for i in range(count):
+        local.append(
+            pltpu.make_async_copy(
+                shards[i], outs[i].at[pos[0], pos[1], pos[2]], local_sems.at[i]
+            )
+        )
+    for i in range(maps):
+        width = inputs[i].shape[1]
+        lanes = pl.ds(pl.multiple_of(model * width, width), width)
+        local.append(
+            pltpu.make_async_copy(inputs[i], fulls[i].at[:, lanes], local_sems.at[count + i])
+        )
+    for copy in local:
+        copy.start()
+    greet_lines(dims, True)
+    pairs = []
+    for i in range(maps):
+        width = inputs[i].shape[1]
+        lanes = pl.ds(pl.multiple_of(model * width, width), width)
+        pairs.append(
+            pltpu.make_async_remote_copy(
+                src_ref=inputs[i],
+                dst_ref=fulls[i].at[:, lanes],
+                send_sem=pair_sems.at[0, i],
+                recv_sem=pair_sems.at[1, i],
+                device_id=partner(),
+                device_id_type=MESH,
+            )
+        )
+    for copy in pairs:
+        copy.start()
+    for copy in local:
+        copy.wait()
+    per_flow = 2 * round_count(dims)
+    flows, base = [], 0
+    for i in range(count):
+        for order, start, size in row_cuts(shards[i].shape[0]):
+            flows.append(
+                gather_flow(
+                    dims,
+                    outs[i],
+                    send_sems,
+                    recv_sems,
+                    base,
+                    pl.ds(start, size),
+                    GATHER_ORDERS[order],
+                )
+            )
+            base += per_flow
+    run_flows(flows, round_count(dims))
+    for copy in pairs:
+        copy.wait()
+
+
+def gather_all(dims, shards, maps):
+    count = len(shards)
+    slots = 2 * round_count(dims) * sum(len(row_cuts(s.shape[0])) for s in shards)
+    slots = max(slots, 1)
+    shapes = [jax.ShapeDtypeStruct(dims + s.shape, s.dtype) for s in shards]
+    shapes += [jax.ShapeDtypeStruct((m.shape[0], 2 * m.shape[1]), m.dtype) for m in maps]
+    result = pl.pallas_call(
+        partial(gather_kernel, dims, count, len(maps)),
+        name="gather_weights",
+        out_shape=shapes,
+        in_specs=[pl.BlockSpec(memory_space=VMEM)] * (count + len(maps)),
+        out_specs=[pl.BlockSpec(memory_space=VMEM)] * (count + len(maps)),
+        scratch_shapes=[
+            pltpu.SemaphoreType.DMA((slots,)),
+            pltpu.SemaphoreType.DMA((slots,)),
+            pltpu.SemaphoreType.DMA((count + len(maps),)),
+            pltpu.SemaphoreType.DMA((2, len(maps))),
+        ],
+        compiler_params=params(0),
+    )(*shards, *maps)
+    return result[:count], result[count:]
+
+
+def reduce_kernel(dims, count, *refs):
+    parts, outs = refs[:count], refs[count : 2 * count]
+    send_sems, recv_sems, local_sems = refs[2 * count : 2 * count + 3]
+    rest = list(refs[2 * count + 3 :])
+    totals, staged, rest = rest[:count], rest[count : 2 * count], rest[2 * count :]
+    pos = place(dims)
+    local = [
+        pltpu.make_async_copy(parts[i], totals[i], local_sems.at[i]) for i in range(count)
+    ]
+    for copy in local:
+        copy.start()
+    greet_lines(dims, False)
+    per_flow = 2 * round_count(dims)
+    flows, base = [], 0
+    for i in range(count):
+        for order, start, size in row_cuts(parts[i].shape[3]):
+            lands, rest = rest[:3], rest[3:]
+            flows.append(
+                reduce_flow(
+                    dims,
+                    totals[i],
+                    staged[i],
+                    lands,
+                    send_sems,
+                    recv_sems,
+                    base,
+                    pl.ds(start, size),
+                    REDUCE_ORDERS[order],
+                )
+            )
+            base += per_flow
+    for i in range(count):
+        local[i].wait()
+
+        def cast(j, carry, i=i):
+            index = (j // (dims[1] * dims[2]), lax.rem(j // dims[2], dims[1]), lax.rem(j, dims[2]))
+            staged[i][index] = totals[i][index].astype(BF16)
+            return carry
+
+        lax.fori_loop(0, dims[0] * dims[1] * dims[2], cast, 0)
+    run_flows(flows, round_count(dims))
+    for i in range(count):
+        outs[i][...] = totals[i][pos[0], pos[1], pos[2]]
+
+
+def reduce_all(dims, parts):
+    count = len(parts)
+    cuts = [row_cuts(p.shape[3]) for p in parts]
+    slots = max(1, 2 * round_count(dims) * sum(len(c) for c in cuts))
+    scratch = [
+        pltpu.SemaphoreType.DMA((slots,)),
+        pltpu.SemaphoreType.DMA((slots,)),
+        pltpu.SemaphoreType.DMA((count,)),
+    ]
+    scratch += [VMEM(p.shape, F32) for p in parts] + [VMEM(p.shape, BF16) for p in parts]
+    for part, cut in zip(parts, cuts):
+        for order, _, size in cut:
+            for shape in landing_shapes(dims, size, part.shape[4], REDUCE_ORDERS[order]):
+                scratch.append(VMEM(shape, BF16))
+    return pl.pallas_call(
+        partial(reduce_kernel, dims, count),
+        name="reduce_gradients",
+        out_shape=[jax.ShapeDtypeStruct(p.shape[3:], F32) for p in parts],
+        in_specs=[pl.BlockSpec(memory_space=ANY)] * count,
+        out_specs=[pl.BlockSpec(memory_space=VMEM)] * count,
+        scratch_shapes=scratch,
+        compiler_params=params(1),
+    )(*parts)
+
+
+def share_kernel(dims, own, out, send_sems, recv_sems, local_sem):
+    pos = place(dims)
+    model = lax.axis_index("mp")
+    local = pltpu.make_async_copy(own, out.at[pos[0], pos[1], pos[2], model], local_sem)
+    local.start()
+    greet_all_lines(dims)
+    local.wait()
+    done, slot, sent = set(), 0, []
+    for axis in (2, 1, 0):
+        view = out.at[
+            tuple(pl.ds(0, dims[k]) if k in done else pos[k] for k in range(3)) + (model,)
+        ]
+        now = []
+        for offset in range(1, dims[axis]):
+            now.append(
+                pltpu.make_async_remote_copy(
+                    src_ref=view,
+                    dst_ref=view,
+                    send_sem=send_sems.at[slot],
+                    recv_sem=recv_sems.at[slot],
+                    device_id=ring_step(dims, pos, axis, offset),
+                    device_id_type=MESH,
+                )
+            )
+            slot += 1
+        for copy in now:
+            copy.start()
+        for copy in now:
+            copy.wait_recv()
+        sent += now
+        done.add(axis)
+    view = out.at[:, :, :, model]
+    last = pltpu.make_async_remote_copy(
+        src_ref=view,
+        dst_ref=view,
+        send_sem=send_sems.at[slot],
+        recv_sem=recv_sems.at[slot],
+        device_id=partner(),
+        device_id_type=MESH,
+    )
+    last.start()
+    last.wait()
+    for copy in sent:
+        copy.wait_send()
+
+
+def share(dims, own, collective_id):
+    slots = round_count(dims) + 1
+    return pl.pallas_call(
+        partial(share_kernel, dims),
+        name="share_blocks",
+        out_shape=jax.ShapeDtypeStruct(dims + (2,) + own.shape, own.dtype),
+        in_specs=[pl.BlockSpec(memory_space=VMEM)],
+        out_specs=pl.BlockSpec(memory_space=VMEM),
+        scratch_shapes=[
+            pltpu.SemaphoreType.DMA((slots,)),
+            pltpu.SemaphoreType.DMA((slots,)),
+            pltpu.SemaphoreType.DMA,
+        ],
+        compiler_params=params(collective_id),
+    )(own)
+
+
+def swap_kernel(count, *refs):
+    ins, outs = refs[:count], refs[count : 2 * count]
+    send_sems, recv_sems = refs[2 * count :]
+    greet_partner()
+    copies = [
+        pltpu.make_async_remote_copy(
+            src_ref=ins[i],
+            dst_ref=outs[i],
+            send_sem=send_sems.at[i],
+            recv_sem=recv_sems.at[i],
+            device_id=partner(),
+            device_id_type=MESH,
+        )
+        for i in range(count)
+    ]
+    for copy in copies:
+        copy.start()
+    for copy in copies:
+        copy.wait()
+
+
+def swap(arrays, collective_id):
+    count = len(arrays)
+    return pl.pallas_call(
+        partial(swap_kernel, count),
+        name="swap_cores",
+        out_shape=[jax.ShapeDtypeStruct(a.shape, a.dtype) for a in arrays],
+        in_specs=[pl.BlockSpec(memory_space=VMEM)] * count,
+        out_specs=[pl.BlockSpec(memory_space=VMEM)] * count,
+        scratch_shapes=[
+            pltpu.SemaphoreType.DMA((count,)),
+            pltpu.SemaphoreType.DMA((count,)),
+        ],
+        compiler_params=params(collective_id),
+    )(*arrays)
+
+def flat_rows(weight):
+    return weight.reshape(-1, weight.shape[-1])
+
+
+def columns_in_lanes(weight):
+    _, depth, width = weight.shape
+    return weight.reshape(3, 3, depth, width).transpose(0, 2, 1, 3).reshape(3, depth, 3 * width)
+
+
+def columns_from_lanes(weight):
+    _, depth, width = weight.shape
+    return (
+        weight.reshape(3, depth, 3, width // 3).transpose(0, 2, 1, 3).reshape(9, depth, width // 3)
+    )
+
+
+def whole_weight(blocks, taps):
+    rows, width = blocks.shape[3:]
+    return (
+        blocks.reshape(-1, taps, rows // taps, width)
+        .transpose(1, 0, 2, 3)
+        .reshape(taps, -1, width)
+    )
+
+
+def owner_blocks(gradient, dims):
+    taps, _, width = gradient.shape
+    owners = dims[0] * dims[1] * dims[2]
+    return (
+        gradient.reshape(taps, owners, -1, width)
+        .transpose(1, 0, 2, 3)
+        .reshape(dims + (-1, width))
+    )
+
+
+def both_cores(arrays, model_index, collective_id):
+    flat = [flat_rows(a) for a in arrays]
+    others = swap(flat, collective_id)
+    first = model_index == 0
+    return [
+        jnp.where(
+            first, jnp.concatenate([own, other], axis=1), jnp.concatenate([other, own], axis=1)
+        ).reshape(a.shape[:-1] + (-1,))
+        for a, own, other in zip(arrays, flat, others)
+    ]
+
+
+def own_half_sums(arrays, model_index, collective_id):
+    halves = []
+    for array in arrays:
+        flat = flat_rows(array)
+        halves.append(flat.reshape(flat.shape[0], 2, -1))
+    away = [
+        lax.dynamic_index_in_dim(half, 1 - model_index, 1, keepdims=False) for half in halves
+    ]
+    here = [lax.dynamic_index_in_dim(half, model_index, 1, keepdims=False) for half in halves]
+    received = swap(away, collective_id)
+    return [
+        (own.astype(jnp.float32) + other.astype(jnp.float32)).reshape(a.shape[:-1] + (-1,))
+        for a, own, other in zip(arrays, here, received)
+    ]
 
 
 def shifted_view(padded, tap_index, height, columns, direction):
@@ -118,21 +701,6 @@
         + (1.0 - FOCAL_ALPHA) * (1.0 - target) * jnp.square(class_prob) * log_neg
     )
     return -jnp.sum(focal_terms) / (live_count.astype(jnp.float32) + 1.0)
-
-
-def contrast_loss(unscaled_scores, norms_all, row_start, live_slots, live_count, live_all):
-    reciprocal_norm = lax.rsqrt(norms_all + 1e-06)
-    reciprocal_row_norms = lax.dynamic_slice_in_dim(reciprocal_norm, row_start, NI)
-    similarity_scores = (
-        unscaled_scores * reciprocal_row_norms[:, None] * reciprocal_norm[None, :] / CONTRAST_TEMP
-    )
-    key_index = jnp.arange(norms_all.shape[0])
-    query_index = row_start + jnp.arange(NI)
-    allowed = (live_all[None, :] > 0.5) & (key_index[None, :] != query_index[:, None])
-    similarity_scores = jnp.where(allowed, similarity_scores, -1000000000.0)
-    top_score = jnp.max(similarity_scores, axis=1, keepdims=True)
-    log_total = top_score[:, 0] + jnp.log(jnp.sum(jnp.exp(similarity_scores - top_score), axis=1))
-    return jnp.sum(live_slots * log_total) / live_count.astype(jnp.float32)
 
 
 def adam_update(weight, moment, square, gradient, rate):
@@ -179,16 +747,30 @@
     model_total = lax.axis_size("mp")
     data_index = lax.axis_index("dp")
     model_index = lax.axis_index("mp")
-    mask_low, first_low, second_low, class_low = (
-        lax.all_gather(mask_convs.astype(jnp.bfloat16), "dp", axis=2, tiled=True),
-        lax.all_gather(grid_first.astype(jnp.bfloat16), "dp", axis=1, tiled=True),
-        lax.all_gather(grid_second.astype(jnp.bfloat16), "dp", axis=1, tiled=True),
-        lax.all_gather(class_conv.astype(jnp.bfloat16), "dp", axis=1, tiled=True),
-    )
-    mask_full, grid_full = (
-        lax.all_gather(mask_features[0], "mp", axis=2, tiled=True),
-        lax.all_gather(grid_features[0], "mp", axis=2, tiled=True),
-    )
+    dims = line_lengths(image_total)
+    pixels_high, pixels_wide, _ = mask_features.shape[1:]
+    class_share = class_conv.shape[2]
+    shards = [
+        flat_rows(mask_convs[0]),
+        flat_rows(grid_first),
+        flat_rows(mask_convs[1]),
+        flat_rows(grid_second),
+        flat_rows(columns_in_lanes(class_conv)),
+    ]
+    gathered, maps = gather_all(
+        dims,
+        [shard.astype(jnp.bfloat16) for shard in shards],
+        [
+            mask_features.reshape(-1, mask_features.shape[3]),
+            grid_features.reshape(-1, grid_features.shape[3]),
+        ],
+    )
+    mask_low = [whole_weight(gathered[0], 9), whole_weight(gathered[2], 9)]
+    first_low = whole_weight(gathered[1], 9)
+    second_low = whole_weight(gathered[3], 9)
+    class_low = columns_from_lanes(whole_weight(gathered[4], 3))
+    mask_full = maps[0].reshape(pixels_high, pixels_wide, -1)
+    grid_full = maps[1].reshape(G, G, -1)
     mask_width = mask_full.shape[2] // GROUPS
     grid_width = first_low.shape[2] * model_total // GROUPS
     mask_norm_act = partial(norm_act, group_width=mask_width)
@@ -197,9 +779,8 @@
     first_grid = convolve(grid_full, first_low)
     hidden_mask, back_mask_one = jax.vjp(mask_norm_act, first_mask, mask_norms[0], mask_norms[1])
     hidden_grid, back_grid_one = jax.vjp(grid_norm_act, first_grid, grid_norms[0], grid_norms[1])
-    hidden_mask_full, hidden_grid_full = (
-        lax.all_gather(hidden_mask.astype(jnp.bfloat16), "mp", axis=2, tiled=True),
-        lax.all_gather(hidden_grid.astype(jnp.bfloat16), "mp", axis=2, tiled=True),
+    hidden_mask_full, hidden_grid_full = both_cores(
+        [hidden_mask.astype(jnp.bfloat16), hidden_grid.astype(jnp.bfloat16)], model_index, 2
     )
     second_mask = convolve(hidden_mask_full, mask_low[1])
     kernels = convolve(hidden_grid_full, second_low)
@@ -210,7 +791,7 @@
     kernel_flat = kernels.reshape(-1, local_width)
     cell_ids = instance_cells[0]
     kernel_rows = jnp.take(kernel_flat, cell_ids, axis=0).astype(jnp.bfloat16)
-    joined = lax.all_gather(kernel_rows, ("dp", "mp"), axis=0, tiled=True)
+    joined = share(dims, kernel_rows, 3)
     kernel_all = (
         joined.reshape(image_total, model_total, NI, local_width)
         .transpose(0, 2, 1, 3)
@@ -225,19 +806,17 @@
     live_all = (jnp.arange(NI)[None, :] < instance_counts[:, None]).astype(jnp.float32).reshape(-1)
     mask_cols = instance_masks[0].T.astype(jnp.float32)
     mask_sum = jnp.sum(mask_cols, axis=0)
-    logits = lax.psum(
-        jnp.dot(feature_low, kernel_rows.T, preferred_element_type=jnp.float32).astype(
-            jnp.bfloat16
-        ),
-        "mp",
-    ).astype(jnp.float32)
+    logits_part = jnp.dot(
+        feature_low, kernel_rows.T, preferred_element_type=jnp.float32
+    ).astype(jnp.bfloat16)
+    logits = logits_part.astype(jnp.float32) + swap([logits_part], 4)[0].astype(jnp.float32)
     (intersection, squares_sum), back_pixels = jax.vjp(
         partial(pixel_sums, mask_cols=mask_cols), logits
     )
     class_width = class_part.shape[2]
     class_logits = class_part.reshape(-1, class_width) + class_bias
 
-    def loss_heads(class_in, score_in, norm_in, intersection_in, squares_in):
+    def loss_heads(class_in, intersection_in, squares_in):
         focal_loss = focal_part(
             class_in,
             cell_ids,
@@ -246,41 +825,63 @@
             instance_labels[0],
             model_index * class_width,
         )
-        rest_loss = DICE_WEIGHT * dice_from(
-            intersection_in, squares_in, mask_sum, live_slots, live_count
-        ) + contrast_loss(score_in, norm_in, row_start, live_slots, live_count, live_all)
-        return (focal_loss, rest_loss)
-
-    (focal_loss, rest_loss), back_heads = jax.vjp(
-        loss_heads, class_logits, unscaled_scores, norms_all, intersection, squares_sum
+        dice_loss = dice_from(intersection_in, squares_in, mask_sum, live_slots, live_count)
+        return (focal_loss, DICE_WEIGHT * dice_loss)
+
+    (focal_loss, dice_loss), back_heads = jax.vjp(
+        loss_heads, class_logits, intersection, squares_sum
     )
     image_share = jnp.float32(1.0 / image_total)
-    grad_class, grad_scores, grad_norms_all, grad_intersection, grad_squares = back_heads(
-        (image_share, image_share)
-    )
+    grad_class, grad_intersection, grad_squares = back_heads((image_share, image_share))
     grad_logits = back_pixels((grad_intersection, grad_squares))[0]
     logit_low = grad_logits.astype(jnp.bfloat16)
-    score_low = grad_scores.astype(jnp.bfloat16)
     first_model = (model_index == 0).astype(jnp.float32)
-    key_terms = first_model * (
-        jnp.dot(score_low.T, kernel_full, preferred_element_type=jnp.float32)
-        + 2.0 * kernel_all.astype(jnp.float32) * grad_norms_all[:, None]
-    )
-    own_terms = first_model * jnp.dot(score_low, kernel_all, preferred_element_type=jnp.float32)
+
+    reciprocal = lax.rsqrt(norms_all + 1e-06)
+    own_reciprocal = lax.dynamic_slice_in_dim(reciprocal, row_start, NI)
+    scale = own_reciprocal[:, None] * reciprocal[None, :] / CONTRAST_TEMP
+    similarity = unscaled_scores * scale
+    other_row = (
+        jnp.arange(image_total * NI)[None, :] != (row_start + jnp.arange(NI))[:, None]
+    )
+    allowed = (live_all[None, :] > 0.5) & other_row
+    masked = jnp.where(allowed, similarity, -1000000000.0)
+    top_score = jnp.max(masked, axis=1, keepdims=True)
+    log_total = top_score[:, 0] + jnp.log(jnp.sum(jnp.exp(masked - top_score), axis=1))
+    contrast = jnp.sum(live_slots * log_total) / live_count.astype(jnp.float32)
+    rest_loss = dice_loss + contrast
+    own_totals = jnp.zeros((8, 128), jnp.float32).at[0, :NI].set(log_total)
+    log_all = share(dims, own_totals, 5).reshape(image_total, model_total, 8, 128)[
+        :, 0, 0, :NI
+    ].reshape(-1)
+    weight_all = live_all * jnp.repeat(image_share / instance_counts.astype(jnp.float32), NI)
+    own_weight = lax.dynamic_slice_in_dim(weight_all, row_start, NI)
+    query_part = jnp.where(
+        allowed, jnp.exp(similarity - log_total[:, None]) * own_weight[:, None], 0.0
+    )
+    keyed = (live_slots[:, None] > 0.5) & other_row & (live_all[None, :] > 0.5)
+    key_part = jnp.where(
+        keyed, jnp.exp(similarity - log_all[None, :]) * weight_all[None, :], 0.0
+    )
+    query_low = (query_part * scale).astype(jnp.bfloat16)
+    key_low = (key_part * scale).astype(jnp.bfloat16)
+    grad_reciprocal = jnp.sum(
+        (query_part + key_part) * unscaled_scores * reciprocal[None, :] / CONTRAST_TEMP, axis=1
+    )
+    grad_norms_own = -0.5 * own_reciprocal * own_reciprocal * own_reciprocal * grad_reciprocal
+    kernel_part = lax.dynamic_slice_in_dim(kernel_all, model_index * local_width, local_width, 1)
     grad_feature = jnp.dot(logit_low, kernel_rows, preferred_element_type=jnp.float32).reshape(
         feature_map.shape
     )
     logit_rows = jnp.dot(logit_low.T, feature_low, preferred_element_type=jnp.float32)
-    key_terms = lax.dynamic_update_slice_in_dim(
-        key_terms, lax.dynamic_slice_in_dim(key_terms, row_start, NI, 0) + own_terms, row_start, 0
-    )
-    ordered = (
-        key_terms.reshape(image_total, NI, model_total, local_width)
-        .transpose(0, 2, 1, 3)
-        .reshape(-1, local_width)
-    )
     grad_rows = (
-        lax.psum_scatter(ordered, ("dp", "mp"), scatter_dimension=0, tiled=True) + logit_rows
+        jnp.dot(
+            jnp.concatenate([query_low, key_low], axis=1),
+            jnp.concatenate([kernel_part, kernel_part], axis=0),
+            preferred_element_type=jnp.float32,
+        )
+        + 2.0 * kernel_rows.astype(jnp.float32) * grad_norms_own[:, None]
+        + logit_rows
     )
     grad_second_mask, grad_gain_three, grad_bias_three = back_mask_two(grad_feature)
     grad_kernels = jnp.zeros(kernel_flat.shape, jnp.float32).at[cell_ids].add(grad_rows)
@@ -295,34 +896,51 @@
     grid_input_terms = conv_input_grad(kernel_grad_low, second_low) + conv_input_grad(
         class_grad_map, class_low
     )
-    grad_hidden_mask, grad_hidden_grid = (
-        lax.psum_scatter(
+    grad_hidden_mask, grad_hidden_grid = own_half_sums(
+        [
             conv_input_grad(mask_grad_low, mask_low[1]).astype(jnp.bfloat16),
-            "mp",
-            scatter_dimension=2,
-            tiled=True,
-        ).astype(jnp.float32),
-        lax.psum_scatter(
-            grid_input_terms.astype(jnp.bfloat16), "mp", scatter_dimension=2, tiled=True
-        ).astype(jnp.float32),
+            grid_input_terms.astype(jnp.bfloat16),
+        ],
+        model_index,
+        6,
     )
     grad_first_mask, grad_gain_one, grad_bias_one = back_mask_one(grad_hidden_mask)
     grad_first_grid, grad_gain_five, grad_bias_five = back_grid_one(grad_hidden_grid)
-    grad_mask_convs = jnp.stack(
-        [conv_weight_grad(mask_full, grad_first_mask.astype(jnp.bfloat16)), grad_mask_second]
-    )
+    grad_mask_first = conv_weight_grad(mask_full, grad_first_mask.astype(jnp.bfloat16))
     grad_grid_first = conv_weight_grad(grid_full, grad_first_grid.astype(jnp.bfloat16))
-    mask_sum_w, first_sum_w, second_sum_w, class_sum_w = (
-        lax.psum_scatter(grad_mask_convs, "dp", scatter_dimension=2, tiled=True),
-        lax.psum_scatter(grad_grid_first, "dp", scatter_dimension=1, tiled=True),
-        lax.psum_scatter(grad_grid_second, "dp", scatter_dimension=1, tiled=True),
-        lax.psum_scatter(grad_class_conv, "dp", scatter_dimension=1, tiled=True),
-    )
-    mask_norm_grad = jnp.stack([grad_gain_one, grad_bias_one, grad_gain_three, grad_bias_three])
-    grid_norm_grad = jnp.stack([grad_gain_five, grad_bias_five])
-    mask_norm_sum, grid_norm_sum, bias_sum = lax.psum(
-        (mask_norm_grad, grid_norm_grad, grad_class_bias), "dp"
-    )
+    reduced = reduce_all(
+        dims,
+        [
+            owner_blocks(grad_mask_first, dims),
+            owner_blocks(grad_grid_first, dims),
+            owner_blocks(grad_mask_second, dims),
+            owner_blocks(grad_grid_second, dims),
+            owner_blocks(columns_in_lanes(grad_class_conv), dims),
+        ],
+    )
+    mask_sum_w = jnp.stack(
+        [reduced[0].reshape(mask_convs.shape[1:]), reduced[2].reshape(mask_convs.shape[1:])]
+    )
+    first_sum_w = reduced[1].reshape(grid_first.shape)
+    second_sum_w = reduced[3].reshape(grid_second.shape)
+    class_sum_w = columns_from_lanes(reduced[4].reshape(3, -1, 3 * class_share))
+    small = jnp.concatenate(
+        [
+            jnp.stack([grad_gain_one, grad_bias_one, grad_gain_three, grad_bias_three]),
+            grad_gain_five.reshape(-1, local_width),
+            grad_bias_five.reshape(-1, local_width),
+            jnp.pad(grad_class_bias, (0, local_width - class_share))[None, :],
+        ]
+    )
+    small_all = share(dims, jnp.pad(small, ((0, 16 - small.shape[0]), (0, 0))), 7).reshape(
+        image_total, model_total, 16, local_width
+    )
+    small_sum = jnp.sum(
+        lax.dynamic_index_in_dim(small_all, model_index, 1, keepdims=False), axis=0
+    )
+    mask_norm_sum = small_sum[:4]
+    grid_norm_sum = small_sum[4:8].reshape(2, -1)
+    bias_sum = small_sum[8, :class_share]
     first_device = (data_index == 0).astype(jnp.float32)
     squares = (
         jnp.sum(jnp.square(mask_sum_w))
@@ -337,7 +955,11 @@
         )
     )
     loss_part = (focal_loss + first_model * rest_loss) * image_share
-    total_squares, step_loss = lax.psum((squares, loss_part), ("dp", "mp"))
+    pair = jnp.concatenate([jnp.full((1, 128), squares), jnp.full((1, 128), loss_part)])
+    pair_sum = jnp.sum(
+        share(dims, jnp.pad(pair, ((0, 6), (0, 0))), 8).reshape(-1, 8, 128), axis=0
+    )
+    total_squares, step_loss = pair_sum[0, 0], pair_sum[1, 0]
     gradient_norm = jnp.sqrt(total_squares)
     factor = jnp.minimum(1.0, CLIP_LIMIT / gradient_norm)
     mask_new = adam_update(

time: 1040 us -> 618 us (0.59)
  waiting for transfers between devices: 413 us -> 0 us
  blocking collectives: 256 us -> 0 us
  Pallas kernels: 0 us -> 178 us
  local copies, waits for them, and re-layouts: 54.7 us -> 145 us
  matrix products: 217 us -> 201 us
  between operations: 24.9 us -> 12.5 us
    reduce_scatter x4 -> x0, waiting for transfers between devices: 245 us -> none  [the longest x1 129 us: body(): lax.psum_scatter(grad_mask_convs, 'dp', scatter_dimension=2, tiled=True)]
    pallas_call x0 -> x9, Pallas kernels: none -> 178 us  [the longest x4 61.2 us: share(): pl.pallas_call(partial(share_kernel, dims), name='share_blocks', out_shap...]
    all_gather x6 -> x0, waiting for transfers between devices: 104 us -> none  [the longest x1 54.3 us: body(): lax.all_gather(grid_first.astype(jnp.bfloat16), 'dp', axis=1, tiled=True)]
    all_gather x3 -> x0, blocking collectives: 94.6 us -> none  [the longest x1 49.4 us: body(): lax.all_gather(class_conv.astype(jnp.bfloat16), 'dp', axis=1, tiled=True)]
    psum x2 -> x0, blocking collectives: 80.8 us -> none  [the longest x1 40.7 us: body(): lax.psum((mask_norm_grad, grid_norm_grad, grad_class_bias), 'dp')]
    unnamed x1 -> x0, blocking collectives: 80.7 us -> none
    another operation x0 -> x15, local copies, waits for them, and re-layouts: none -> 62.4 us
    unnamed x19 -> x0, waiting for transfers between devices: 56.6 us -> none
  transfers between devices with their start and end apart: 17 -> 0, of which waited for: 8 -> 0; matrix products, arithmetic and copies ran while one was open for 22% -> 0% of each run, Pallas kernels for 0% -> 0%
where the time goes in v1:
time: 618 us; the launch traced here: 607 us
  matrix products  201 us (33%)
  Pallas kernels  178 us (29%)
  local copies, waits for them, and re-layouts  145 us (23%)
  other arithmetic  70.9 us (11%)
  between operations  12.5 us (2%)
    dot_general x27, matrix products, conv_input_grad(): jnp.einsum('hwd,cd->hwc', shifted_view(padded, tap_index, height, columns...  86.8 us
    dot_general x45, matrix products, conv_weight_grad(): jnp.einsum('hwc,hwd->cd', shifted_view(padded, tap_index, height, columns...  71.9 us
    pallas_call x4, Pallas kernels, share(): pl.pallas_call(partial(share_kernel, dims), name='share_blocks', out_shap...  61.2 us
    pallas_call x1, Pallas kernels, gather_all(): pl.pallas_call(partial(gather_kernel, dims, count, len(maps)), name='gath...  51.5 us
    pallas_call x1, Pallas kernels, reduce_all(): pl.pallas_call(partial(reduce_kernel, dims, count), name='reduce_gradient...  46.9 us
    another operation x8, local copies, waits for them, and re-layouts  46.9 us
    dot_general x45, matrix products, convolve(): jnp.einsum('hwc,cd->hwd', shifted_view(padded, tap_index, height, columns...  32.1 us
    unnamed x334, local copies, waits for them, and re-layouts  23.3 us

profile of v1, /device:TPU:0, one launch (start us, length us, event | category | flops | bytes accessed | tf_op | source)
XLA Modules:
  0.0 607.1 jit_solution(4235268719862032331)
XLA Ops:
  7.0 51.5 %gather_weights.1 = (bf16[4,2,2,144,128]{4,3,2,1,0:T(8,128)(2,1)}, bf16[4,2,2,144,256]{4,3,2,1,0:T(8,128)(2,1)}, bf16[4,2,2,144,128]{4,3,2,1,0:T(8,128)(2,1)}, b...) custom-call(bf16[144,128]{1,0:T(8,128)(2,1)} %bitcast.872, ...), custom_call_target="tpu_custom_call" | custom-call | tf_op jit(solution)/shard_map/gather_weights/pallas_call | solution.py:362
  66.7 2.7 maximum_convert_fusion.2
  75.3 2.6 fusion.438
  78.3 2.8 multiply_reduce_fusion.6
  83.7 6.6 %swap_cores.3 = (bf16[4096,128]{1,0:T(8,128)(2,1)}, bf16[1600,256]{1,0:T(8,128)(2,1)}) custom-call(bf16[4096,128]{1,0:T(8,128)(2,1)} %bitcast.741, bf16[1600,256]{1,0:T(8,128)(2,1)} %bitcast.748), custom_call_target="tpu_custom_call" | custom-call | tf_op jit(solution)/shard_map/swap_cores/pallas_call | solution.py:535
  90.4 2.5 maximum_select_fusion
  102.6 2.7 maximum_select_fusion.1
  114.8 4.9 swap_cores.4
  119.6 5.1 copy.231
  124.8 2.8 fusion.20
  127.6 19.2 %share_blocks.4 = bf16[4,2,2,2,100,128]{5,4,3,2,1,0:T(8,128)(2,1)} custom-call(bf16[100,128]{1,0:T(8,128)(2,1)} %copy-done.90), custom_call_target="tpu_custom_call" | custom-call | tf_op jit(solution)/shard_map/share_blocks/pallas_call | solution.py:497
  146.8 5.1 multiply_reduce_fusion.13
  160.6 14.3 %share_blocks.5 = f32[4,2,2,2,8,128]{5,4,3,2,1,0:T(8,128)} custom-call(f32[8,128]{1,0:T(8,128)} %scatter.4.own), custom_call_target="tpu_custom_call" | custom-call | tf_op jit(solution)/shard_map/share_blocks/pallas_call | solution.py:497
  185.7 2.4 fusion.211
  190.5 2.4 fusion.213
  195.2 2.4 fusion.215
  199.9 2.4 fusion.216
  202.2 2.3 fusion.217
  208.5 3.0 reshape_reshape.15
  240.1 19.6 %add_convert_fusion.1 = bf16[40,40,512]{2,1,0:T(8,128)(2,1)} fusion(f32[40,40,512]{2,1,0:T(8,128)} %fusion.225, f32[40,40,512]{2,1,0:T(8,128)} %fusion.224, f32[40,40,512]{2,1,0:T(8,128)} %fusion.223, f32[40,40,512]{2,1,0:T(8,128)} %fusion.300, f32[40,40,512]{2,1,0:T(8,128)} %fusion.222, f32[40,40,512]{2,1,0:T(8,128)} %fusion.221, ...), kind=kOutput, calls=%fused_computation.20 | convolution fusion | flops 80281600 | bytes 57794560 | tf_op jit(solution)/shard_map/hwd,cd->hwc/dot_general | solution.py:640
  259.8 4.8 reshape_reshape.16
  264.6 6.0 constant_dynamic-slice_fusion
  272.5 2.9 fusion.420
  279.8 3.1 add_convert_fusion.3
  284.6 2.7 fusion.167
  287.2 2.7 fusion.169
  289.9 2.7 fusion.171
  292.6 2.7 fusion.442
  295.3 2.7 fusion.161
  298.0 2.6 fusion.159
  300.6 10.5 %add_convert_fusion = bf16[32,128,256]{2,1,0:T(8,128)(2,1)} fusion(f32[32,128,256]{2,1,0:T(8,128)} %fusion.159, f32[32,128,256]{2,1,0:T(8,128)} %fusion.161, f32[32,128,256]{2,1,0:T(8,128)S(1)} %fusion.163, f32[32,128,256]{2,1,0:T(8,128)} %fusion.442, f32[32,128,256]{2,1,0:T(8,128)S(1)} %fusion.165, f32[32,128,256]{2,1,0:T(8,128)} %fusion.167, ...), kind=kOutput, calls=%fused_computation.19 | convolution fusion | flops 277872640 | bytes 36765696 | tf_op jit(solution)/shard_map/hwd,cd->hwc/dot_general | solution.py:640
  311.2 4.0 reshape.879
  315.2 7.2 %constant_dynamic-slice_fusion.4 = (bf16[4096,1,128]{2,1,0:T(2,128)(2,1)}, bf16[4096,1,128]{2,1,0:T(2,128)(2,1)S(1)}) fusion(bf16[4096,2,128]{2,1,0:T(2,128)(2,1)} %reshape.879, s32[]{:T(128)S(6)} %select_n.104, s32[]{:T(128)S(6)} %select_n.105), kind=kLoop, calls=%fused_computation.483 | loop fusion | bytes 4194312 | tf_op jit(solution)/shard_map/jit(dynamic_index_in_dim)/dynamic_slice | solution.py:603
  323.5 6.6 %swap_cores.5 = (bf16[4096,128]{1,0:T(8,128)(2,1)}, bf16[1600,256]{1,0:T(8,128)(2,1)}) custom-call(bf16[4096,128]{1,0:T(8,128)(2,1)} %bitcast.753, bf16[1600,256]{1,0:T(8,128)(2,1)} %bitcast.755), custom_call_target="tpu_custom_call" | custom-call | tf_op jit(solution)/shard_map/swap_cores/pallas_call | solution.py:535
  334.8 2.9 fusion.419
  340.3 13.9 %share_blocks.6 = f32[4,2,2,2,16,128]{5,4,3,2,1,0:T(8,128)} custom-call(f32[16,128]{1,0:T(8,128)} %pad.61.own), custom_call_target="tpu_custom_call" | custom-call | tf_op jit(solution)/shard_map/share_blocks/pallas_call | solution.py:497
  364.1 3.0 reshape_reshape.17
  367.2 3.0 copy.290
  370.2 7.7 %fusion.240 = (bf16[512,40,40]{0,2,1:T(8,128)(2,1)}, bf16[512,40,40]{0,2,1:T(8,128)(2,1)}, bf16[512,40,40]{0,2,1:T(8,128)(2,1)}, bf16[512,40,40]{0,2,1:T(8,128)(...) fusion(bf16[40,40,512]{2,1,0:T(8,128)(2,1)S(1)} %maximum_select, ...), kind=kLoop, calls=%fused_computation.329 | loop fusion | bytes 14745600 | tf_op jit(solution)/shard_map/hwc,hwd->cd/dot_general | solution.py:654
  377.9 8.6 %reshape.756 = bf16[16,32,40,40]{1,0,3,2:T(8,128)(2,1)} reshape(bf16[512,40,40]{0,2,1:T(8,128)(2,1)} %get-tuple-element.128) | data formatting | bytes 3276800 | tf_op jit(solution)/shard_map/reshape.532
  386.6 5.6 fusion.91
  392.2 5.4 reshape.757
  397.6 5.6 fusion.97
  403.2 5.4 reshape.758
  408.6 5.6 fusion.103
  414.2 5.4 reshape.759
  419.6 5.5 fusion.109
  426.6 5.6 reshape.760
  432.1 5.6 fusion.115
  437.7 5.4 reshape.761
  443.2 5.6 fusion.121
  448.8 5.4 reshape.762
  454.2 5.6 fusion.127
  459.8 5.6 reshape.763
  465.4 5.5 fusion.133
  470.8 3.5 copy.281
  492.7 4.4 copy.252
  497.1 2.7 fusion.139
  503.1 3.5 copy.254
  508.2 3.2 add_convert_fusion.2
  514.6 3.3 copy.244
  518.0 2.8 fusion.145
  525.2 46.9 %reduce_gradients.1 = (f32[144,128]{1,0:T(8,128)}, f32[144,256]{1,0:T(8,128)}, f32[144,128]{1,0:T(8,128)}, f32[288,128]{1,0:T(8,128)}, f32[96,120]{1,0:T(8,128)}) custom-call(f32[4,2,2,144,128]{4,3,2,1,0:T(8,128)} %bitcast.752, f32[4,2,2,144,256]{4,3,2,1,0:T(8,128)} %bitcast.743, f32[4,2,2,144,128]{4,3,2,1,0:T(8,128)} %bitcast.242.refs_2_, ...), custom_call_target="tpu_custom_call" | custom-call | tf_op jit(solution)/shard_map/reduce_gradients/pallas_call | solution.py:438
  583.5 13.7 %share_blocks.7 = f32[4,2,2,2,8,128]{5,4,3,2,1,0:T(8,128)} custom-call(f32[8,128]{1,0:T(8,128)} %pad.63.own), custom_call_target="tpu_custom_call" | custom-call | tf_op jit(solution)/shard_map/share_blocks/pallas_call | solution.py:497
  (585 shorter events, 170.1 us)
Async XLA Ops:
  64.4 5.0 copy-start.84
  64.7 4.8 copy-start.105
  65.7 3.8 copy-start.2
  66.7 3.6 copy-start.111
  66.7 3.6 copy-start.113
  66.7 3.6 copy-start.115
  78.0 4.2 copy-start.117
  78.0 4.3 copy-start.6
  78.3 5.4 copy-start.107
  82.1 8.2 %copy-start.121 = (f32[128]{0:T(128)}, f32[128]{0:T(128)S(1)}, u32[]{:S(2)}) copy-start(f32[128]{0:T(128)S(1)} %mul.727) | copy-start | bytes 1540
  82.2 8.2 %copy-start.125 = (f32[128]{0:T(128)}, f32[128]{0:T(128)S(1)}, u32[]{:S(2)}) copy-start(f32[128]{0:T(128)S(1)} %get-tuple-element.177) | copy-start | bytes 1540
  82.2 8.2 %copy-start.127 = (f32[128]{0:T(128)}, f32[128]{0:T(128)S(1)}, u32[]{:S(2)}) copy-start(f32[128]{0:T(128)S(1)} %get-tuple-element.178) | copy-start | bytes 1540
  82.2 19.9 %copy-start.129 = (f32[128]{0:T(128)}, f32[128]{0:T(128)S(1)}, u32[]{:S(2)}) copy-start(f32[128]{0:T(128)S(1)} %get-tuple-element.176) | copy-start | bytes 1540
  82.2 19.9 %copy-start.131 = (f32[128]{0:T(128)}, f32[128]{0:T(128)S(1)}, u32[]{:S(2)}) copy-start(f32[128]{0:T(128)S(1)} %get-tuple-element.179) | copy-start | bytes 1540
  83.7 6.7 %copy-start.18 = (bf16[32,128,128]{2,1,0:T(8,128)(2,1)S(1)}, bf16[32,128,128]{2,1,0:T(8,128)(2,1)}, u32[]{:S(2)}) copy-start(bf16[32,128,128]{2,1,0:T(8,128)(2,1)} %maximum_convert_fusion.1) | copy-start | bytes 3145732
  92.9 6.1 copy-start
  93.1 3.7 copy-start.69
  93.1 4.4 copy-start.67
  93.1 5.1 copy-start.64
  93.1 5.8 copy-start.71
  102.6 10.7 %copy-start.20 = (bf16[32,128,128]{2,1,0:T(8,128)(2,1)}, bf16[32,128,128]{2,1,0:T(8,128)(2,1)S(1)}, u32[]{:S(2)}) copy-start(bf16[32,128,128]{2,1,0:T(8,128)(2,1)S(1)} %maximum_convert_fusion) | copy-start | bytes 3145732
  105.7 3.5 copy-start.48
  105.7 4.2 copy-start.44
  105.7 4.9 copy-start.42
  105.7 5.5 copy-start.38
  113.3 6.3 %copy-start.90 = (bf16[100,128]{1,0:T(8,128)(2,1)}, bf16[100,128]{1,0:T(8,128)(2,1)S(1)}, u32[]{:S(2)}) copy-start(bf16[100,128]{1,0:T(8,128)(2,1)S(1)} %select_convert_fusion.own) | copy-start | bytes 76804
  119.6 5.1 copy-start.16
  127.6 25.5 %copy-start.139 = (s32[16]{0:T(128)S(1)}, s32[16]{0:T(128)}, u32[]{:S(2)}) copy-start(s32[16]{0:T(128)} %param.33) | copy-start | bytes 196
  156.7 23.4 %copy-start.91 = (bf16[100,128]{1,0:T(8,128)(2,1)S(1)}, bf16[100,128]{1,0:T(8,128)(2,1)}, u32[]{:S(2)}) copy-start(bf16[100,128]{1,0:T(8,128)(2,1)} %copy-done.90) | copy-start | bytes 76804
  211.6 5.2 copy-start.34
  264.6 7.1 %copy-start.23 = (bf16[4096,100]{1,0:T(8,128)(2,1)S(1)}, bf16[4096,100]{1,0:T(8,128)(2,1)}, u32[]{:S(2)}) copy-start(bf16[4096,100]{1,0:T(8,128)(2,1)} %copy-done.22) | copy-start | bytes 2457604
  330.1 3.5 copy-start.24
  386.6 5.6 copy-start.33
  397.6 5.6 copy-start.32
  408.6 5.6 copy-start.31
  419.6 5.6 copy-start.26
  419.6 5.6 copy-start.60
  432.1 5.6 copy-start.29
  443.2 5.6 copy-start.28
  454.2 5.6 copy-start.27
  470.8 3.5 copy-start.1
  503.1 3.5 copy-start.134
  503.1 3.7 copy-start.141
  503.1 3.9 copy-start.8
  525.0 74.4 %copy-start.147 = (f32[40]{0:T(128)S(1)}, f32[40]{0:T(128)}, u32[]{:S(2)}) copy-start(f32[40]{0:T(128)} %param.54) | copy-start | bytes 484
  525.0 74.4 %copy-start.148 = (f32[40]{0:T(128)S(1)}, f32[40]{0:T(128)}, u32[]{:S(2)}) copy-start(f32[40]{0:T(128)} %param.55) | copy-start | bytes 484
  525.1 74.4 %copy-start.149 = (f32[40]{0:T(128)S(1)}, f32[40]{0:T(128)}, u32[]{:S(2)}) copy-start(f32[40]{0:T(128)} %param.56) | copy-start | bytes 484
  525.1 75.0 %copy-start.118 = (f32[4,128]{1,0:T(4,128)S(1)}, f32[4,128]{1,0:T(4,128)}, u32[]{:S(2)}) copy-start(f32[4,128]{1,0:T(4,128)} %param.48) | copy-start | bytes 6148
  525.1 75.0 %copy-start.135 = (f32[4,128]{1,0:T(4,128)S(1)}, f32[4,128]{1,0:T(4,128)}, u32[]{:S(2)}) copy-start(f32[4,128]{1,0:T(4,128)} %param.49) | copy-start | bytes 6148
  525.1 75.0 %copy-start.136 = (f32[4,128]{1,0:T(4,128)S(1)}, f32[4,128]{1,0:T(4,128)}, u32[]{:S(2)}) copy-start(f32[4,128]{1,0:T(4,128)} %param.50) | copy-start | bytes 6148
  525.1 75.6 %copy-start.120 = (f32[2,256]{1,0:T(2,128)S(1)}, f32[2,256]{1,0:T(2,128)}, u32[]{:S(2)}) copy-start(f32[2,256]{1,0:T(2,128)} %param.51) | copy-start | bytes 6148
  525.1 75.6 %copy-start.137 = (f32[2,256]{1,0:T(2,128)S(1)}, f32[2,256]{1,0:T(2,128)}, u32[]{:S(2)}) copy-start(f32[2,256]{1,0:T(2,128)} %param.52) | copy-start | bytes 6148
  525.1 75.6 %copy-start.138 = (f32[2,256]{1,0:T(2,128)S(1)}, f32[2,256]{1,0:T(2,128)}, u32[]{:S(2)}) copy-start(f32[2,256]{1,0:T(2,128)} %param.53) | copy-start | bytes 6148
  525.1 77.2 %copy-start.87 = (f32[9,32,40]{2,1,0:T(8,128)S(1)}, f32[9,32,40]{2,1,0:T(8,128)}, u32[]{:S(2)}) copy-start(f32[9,32,40]{2,1,0:T(8,128)} %param.45) | copy-start | bytes 138244
  525.1 77.2 %copy-start.97 = (f32[9,32,40]{2,1,0:T(8,128)S(1)}, f32[9,32,40]{2,1,0:T(8,128)}, u32[]{:S(2)}) copy-start(f32[9,32,40]{2,1,0:T(8,128)} %param.46) | copy-start | bytes 138244
  525.1 77.1 %copy-start.98 = (f32[9,32,40]{2,1,0:T(8,128)S(1)}, f32[9,32,40]{2,1,0:T(8,128)}, u32[]{:S(2)}) copy-start(f32[9,32,40]{2,1,0:T(8,128)} %param.47) | copy-start | bytes 138244
  572.0 31.1 %copy-start.86 = (f32[288,128]{1,0:T(8,128)S(1)}, f32[288,128]{1,0:T(8,128)}, u32[]{:S(2)}) copy-start(f32[288,128]{1,0:T(8,128)} %get-tuple-element.73) | copy-start | bytes 442372
  572.1 31.1 %copy-start.88 = (f32[9,32,128]{2,1,0:T(8,128)S(1)}, f32[9,32,128]{2,1,0:T(8,128)}, u32[]{:S(2)}) copy-start(f32[9,32,128]{2,1,0:T(8,128)} %param.42) | copy-start | bytes 442372
  572.1 31.1 %copy-start.99 = (f32[9,32,128]{2,1,0:T(8,128)S(1)}, f32[9,32,128]{2,1,0:T(8,128)}, u32[]{:S(2)}) copy-start(f32[9,32,128]{2,1,0:T(8,128)} %param.43) | copy-start | bytes 442372
  572.1 31.1 %copy-start.100 = (f32[9,32,128]{2,1,0:T(8,128)S(1)}, f32[9,32,128]{2,1,0:T(8,128)}, u32[]{:S(2)}) copy-start(f32[9,32,128]{2,1,0:T(8,128)} %param.44) | copy-start | bytes 442372
  572.1 31.9 %copy-start.85 = (f32[144,256]{1,0:T(8,128)S(1)}, f32[144,256]{1,0:T(8,128)}, u32[]{:S(2)}) copy-start(f32[144,256]{1,0:T(8,128)} %get-tuple-element.72) | copy-start | bytes 442372
  572.1 31.9 %copy-start.89 = (f32[9,16,256]{2,1,0:T(8,128)S(1)}, f32[9,16,256]{2,1,0:T(8,128)}, u32[]{:S(2)}) copy-start(f32[9,16,256]{2,1,0:T(8,128)} %param.39) | copy-start | bytes 442372
  572.1 31.9 %copy-start.101 = (f32[9,16,256]{2,1,0:T(8,128)S(1)}, f32[9,16,256]{2,1,0:T(8,128)}, u32[]{:S(2)}) copy-start(f32[9,16,256]{2,1,0:T(8,128)} %param.40) | copy-start | bytes 442372
  572.1 31.9 %copy-start.102 = (f32[9,16,256]{2,1,0:T(8,128)S(1)}, f32[9,16,256]{2,1,0:T(8,128)}, u32[]{:S(2)}) copy-start(f32[9,16,256]{2,1,0:T(8,128)} %param.41) | copy-start | bytes 442372
  (90 other events, 189.2 us)

commit v2 on v0

v2 whole, which is shorter than its diff:
```python
from functools import partial

import jax
import jax.numpy as jnp
from jax import lax
from jax.experimental import pallas as pl
from jax.experimental.pallas import tpu as pltpu
from jax.sharding import PartitionSpec as P

GROUPS = 32
GN_EPS = 1e-05
CLIP_LIMIT = 0.02
LEARN_RATE = 0.02
SMALL_RATE = 0.5
BETA_ONE = 0.9
BETA_TWO = 0.95
ADAM_EPS = 1e-08
WEIGHT_DECAY = 0.05
CONTRAST_TEMP = 0.05
FOCAL_ALPHA = 0.25
DICE_WEIGHT = 3.0
STEP_TIME = 10.0
HIGHEST = lax.Precision.HIGHEST

MESH = pl.DeviceIdType.MESH
VMEM = pltpu.VMEM
ANY = pl.ANY
VMEM_LIMIT = 67043328
F32 = jnp.float32
BF16 = jnp.bfloat16
I32 = jnp.int32
SLOTS = 128
DMA = pltpu.SemaphoreType.DMA


def line_lengths(total):
    if total & (total - 1):
        return (total, 1, 1)
    bits = total.bit_length() - 1
    last = bits // 3
    middle = (bits - last) // 2
    return (1 << (bits - last - middle), 1 << middle, 1 << last)


def place(dims):
    index = lax.axis_index("dp")
    return (index // (dims[1] * dims[2]), (index // dims[2]) % dims[1], index % dims[2])


def split_index(dims, index):
    return (
        index // (dims[1] * dims[2]),
        lax.rem(index // dims[2], dims[1]),
        lax.rem(index, dims[2]),
    )


def along(dims, axis, step):
    stride = (dims[1] * dims[2], dims[2], 1)[axis]
    return {"dp": lax.axis_index("dp") + step * stride}


def partner():
    return {"mp": 1 - lax.axis_index("mp")}


def ring_step(dims, pos, axis, offset):
    other = lax.rem(pos[axis] + offset, dims[axis])
    return along(dims, axis, other - pos[axis])


def greet(dims):
    sem = pltpu.get_barrier_semaphore()
    pos = place(dims)
    count = 1
    for axis in range(3):
        for offset in range(1, dims[axis]):
            pl.semaphore_signal(
                sem, inc=1, device_id=ring_step(dims, pos, axis, offset), device_id_type=MESH
            )
            count += 1
    pl.semaphore_signal(sem, inc=1, device_id=partner(), device_id_type=MESH)
    pl.semaphore_wait(sem, count)


GATHER_ORDERS = ((2, 1, 0), (0, 2, 1), (0, 1, 2))
REDUCE_ORDERS = tuple(tuple(reversed(order)) for order in GATHER_ORDERS)


def rounds_of(dims, order):
    return [
        (stage, axis, step) for stage, axis in enumerate(order) for step in range(dims[axis] - 1)
    ]


def round_count(dims):
    return sum(n - 1 for n in dims)


def lane_cuts(width):
    tiles = width // 128
    if width % 128 or tiles < 3:
        return ((0, 0, width),)
    first = max(1, round(tiles * 0.2))
    second = (tiles - first) // 2
    sizes = (first, second, tiles - first - second)
    cuts, start = [], 0
    for order, size in enumerate(sizes):
        cuts.append((order, start * 128, size * 128))
        start += size
    return tuple(cuts)


class Flow:
    def __init__(self, rounds):
        self.rounds = rounds

    def start(self, r):
        for copy, sends, *_ in self.rounds[r]:

            @pl.when(sends)
            def _(copy=copy):
                copy.start()

    def finish(self, r):
        for copy, _, receives, land in self.rounds[r]:

            @pl.when(receives)
            def _(copy=copy, land=land):
                copy.wait_recv()
                if land is not None:
                    land()

    def drain(self):
        for copies in self.rounds:
            for copy, sends, *_ in copies:

                @pl.when(sends)
                def _(copy=copy):
                    copy.wait_send()


def gather_flow(dims, out, send_sems, recv_sems, base, lanes, order):
    pos = place(dims)
    result = []
    for r, (stage, axis, step) in enumerate(rounds_of(dims, order)):
        n, done = dims[axis], set(order[:stage])
        copies = []
        for side, delta in ((0, 1), (1, -1)):
            block = pos[axis] - delta * step
            sends = (
                (pos[axis] + delta >= 0)
                & (pos[axis] + delta < n)
                & (block >= 0)
                & (block < n)
            )
            block = jnp.clip(block, 0, n - 1)
            source = pos[axis] - delta * (1 + step)
            receives = (source >= 0) & (source < n)
            view = out.at[
                tuple(
                    pl.ds(0, dims[k]) if k in done else (block if k == axis else pos[k])
                    for k in range(3)
                )
                + (slice(None), lanes)
            ]
            copy = pltpu.make_async_remote_copy(
                src_ref=view,
                dst_ref=view,
                send_sem=send_sems.at[base + 2 * r + side],
                recv_sem=recv_sems.at[base + 2 * r + side],
                device_id=along(dims, axis, delta),
                device_id_type=MESH,
            )
            copies.append((copy, sends, receives, None))
        result.append(copies)
    return Flow(result)


def landing_shapes(dims, rows, width, order):
    shapes, left = [], {0, 1, 2}
    for axis in order:
        left = left - {axis}
        n = dims[axis]
        slots = max(1, n - 1) * (1 if n <= 2 else 2)
        shapes.append((slots,) + tuple(dims[k] for k in sorted(left)) + (rows, width))
    return shapes


def reduce_flow(dims, total, staged, lands, send_sems, recv_sems, base, lanes, order):
    pos = place(dims)
    result = []
    for r, (stage, axis, step) in enumerate(rounds_of(dims, order)):
        n, reduced = dims[axis], set(order[:stage])
        free = [k for k in range(3) if k not in reduced and k != axis]

        def view(block, lead=None, axis=axis, reduced=reduced):
            lead = iter(lead) if lead is not None else None
            index = []
            for k in range(3):
                if k == axis:
                    index.append(block)
                elif k in reduced:
                    index.append(pos[k])
                else:
                    index.append(pl.ds(0, dims[k]) if lead is None else next(lead))
            return tuple(index) + (slice(None), lanes)

        copies = []
        for side, delta in ((0, 1), (1, -1)):
            rank = pos[axis] if delta == 1 else n - 1 - pos[axis]
            sends = rank <= step
            if n == 1:
                sends = sends & False
            block = n - 1 - step + rank
            block = jnp.clip(block if delta == 1 else n - 1 - block, 0, n - 1)
            receives = (rank >= 1) & (rank - 1 <= step)
            taken = n - 1 - step + rank - 1
            taken = jnp.clip(taken if delta == 1 else n - 1 - taken, 0, n - 1)
            land_ref = lands[stage].at[step if n <= 2 else side * (n - 1) + step]
            copy = pltpu.make_async_remote_copy(
                src_ref=staged.at[view(block)],
                dst_ref=land_ref,
                send_sem=send_sems.at[base + 2 * r + side],
                recv_sem=recv_sems.at[base + 2 * r + side],
                device_id=along(dims, axis, delta),
                device_id_type=MESH,
            )

            def land(taken=taken, land_ref=land_ref, free=free, view=view):
                sizes = [dims[k] for k in free]
                blocks = 1
                for size in sizes:
                    blocks *= size

                def add(i, carry):
                    lead, rest = [], i
                    for size in reversed(sizes):
                        lead.append(lax.rem(rest, size))
                        rest = rest // size
                    lead = lead[::-1]
                    index = view(taken, lead)
                    value = total[index] + land_ref[tuple(lead)].astype(F32)
                    total[index] = value
                    staged[index] = value.astype(BF16)
                    return carry

                if blocks == 1:
                    add(jnp.int32(0), 0)
                else:
                    lax.fori_loop(0, blocks, add, 0)

            copies.append((copy, sends, receives, land))
        result.append(copies)
    return Flow(result)


class Share:
    def __init__(self, dims, out, send_sems, recv_sems, core):
        pos = place(dims)
        model = lax.axis_index("mp")
        tail = (model,) if core else ()
        self.stages, done, slot = [], set(), 0
        for axis in (2, 1, 0):
            view = out.at[
                tuple(pl.ds(0, dims[k]) if k in done else pos[k] for k in range(3)) + tail
            ]
            copies = []
            for offset in range(1, dims[axis]):
                copies.append(
                    pltpu.make_async_remote_copy(
                        src_ref=view,
                        dst_ref=view,
                        send_sem=send_sems.at[slot],
                        recv_sem=recv_sems.at[slot],
                        device_id=ring_step(dims, pos, axis, offset),
                        device_id_type=MESH,
                    )
                )
                slot += 1
            if copies:
                self.stages.append(copies)
            done.add(axis)
        if core:
            view = out.at[:, :, :, model]
            self.stages.append(
                [
                    pltpu.make_async_remote_copy(
                        src_ref=view,
                        dst_ref=view,
                        send_sem=send_sems.at[slot],
                        recv_sem=recv_sems.at[slot],
                        device_id=partner(),
                        device_id_type=MESH,
                    )
                ]
            )
        self.next = 0

    def advance(self):
        if self.next > len(self.stages):
            return
        if self.next > 0:
            for copy in self.stages[self.next - 1]:
                copy.wait_recv()
        if self.next < len(self.stages):
            for copy in self.stages[self.next]:
                copy.start()
        self.next += 1

    def complete(self):
        while self.next <= len(self.stages):
            self.advance()

    def drain(self):
        for stage in self.stages:
            for copy in stage:
                copy.wait_send()


def share_sems(dims):
    return [DMA((round_count(dims) + 1,)), DMA((round_count(dims) + 1,))]


def pair_copy(source, target, sems):
    return pltpu.make_async_remote_copy(
        src_ref=source,
        dst_ref=target,
        send_sem=sems.at[0],
        recv_sem=sems.at[1],
        device_id=partner(),
        device_id_type=MESH,
    )


def params(collective_id):
    return pltpu.CompilerParams(
        collective_id=collective_id, has_side_effects=True, vmem_limit_bytes=VMEM_LIMIT
    )


def gather_flows(dims, outs, send_sems, recv_sems):
    groups, base = [], 0
    for out in outs:
        group = []
        for order, start, size in lane_cuts(out.shape[4]):
            group.append(
                gather_flow(
                    dims, out, send_sems, recv_sems, base, pl.ds(start, size), GATHER_ORDERS[order]
                )
            )
            base += 2 * round_count(dims)
        groups.append(group)
    return groups


def reduce_flows(dims, totals, staged, lands, send_sems, recv_sems):
    groups, base, lands = [], 0, list(lands)
    for total, stage in zip(totals, staged):
        group = []
        for order, start, size in lane_cuts(total.shape[4]):
            group.append(
                reduce_flow(
                    dims,
                    total,
                    stage,
                    lands[:3],
                    send_sems,
                    recv_sems,
                    base,
                    pl.ds(start, size),
                    REDUCE_ORDERS[order],
                )
            )
            lands = lands[3:]
            base += 2 * round_count(dims)
        groups.append(group)
    return groups


def flow_slots(dims, shapes):
    return max(1, 2 * round_count(dims) * sum(len(lane_cuts(s[-1])) for s in shapes))


def landing_scratch(dims, shapes):
    scratch = []
    for shape in shapes:
        for order, _, size in lane_cuts(shape[-1]):
            for land in landing_shapes(dims, shape[-2], size, REDUCE_ORDERS[order]):
                scratch.append(VMEM(land, BF16))
    return scratch


def cast_blocks(dims, total, staged):
    def cast(j, carry):
        index = split_index(dims, j)
        staged[index] = total[index].astype(BF16)
        return carry

    lax.fori_loop(0, dims[0] * dims[1] * dims[2], cast, 0)


def run_rounds(dims, groups):
    flows = [flow for group in groups for flow in group]
    for r in range(round_count(dims) + 1):
        for flow in flows:
            if r > 0:
                flow.finish(r - 1)
            if r < round_count(dims):
                flow.start(r)
    for flow in flows:
        flow.drain()


def gather_kernel(dims, count, *refs):
    shards, outs = refs[:count], refs[count : 2 * count]
    send_sems, recv_sems, local_sems = refs[2 * count :]
    pos = place(dims)
    local = [
        pltpu.make_async_copy(shards[i], outs[i].at[pos[0], pos[1], pos[2]], local_sems.at[i])
        for i in range(count)
    ]
    for copy in local:
        copy.start()
    greet(dims)
    for copy in local:
        copy.wait()
    run_rounds(dims, gather_flows(dims, outs, send_sems, recv_sems))


def gather_all(dims, shards):
    count = len(shards)
    shapes = [dims + s.shape for s in shards]
    slots = flow_slots(dims, shapes)
    return pl.pallas_call(
        partial(gather_kernel, dims, count),
        name="gather_weights",
        out_shape=[jax.ShapeDtypeStruct(s, BF16) for s in shapes],
        in_specs=[pl.BlockSpec(memory_space=VMEM)] * count,
        out_specs=[pl.BlockSpec(memory_space=VMEM)] * count,
        scratch_shapes=[DMA((slots,)), DMA((slots,)), DMA((count,))],
        compiler_params=params(1),
    )(*shards)


def reduce_kernel(dims, count, *refs):
    parts, outs = refs[:count], refs[count : 2 * count]
    send_sems, recv_sems, local_sems = refs[2 * count : 2 * count + 3]
    rest = list(refs[2 * count + 3 :])
    totals, staged, lands = rest[:count], rest[count : 2 * count], rest[2 * count :]
    pos = place(dims)
    local = [pltpu.make_async_copy(parts[i], totals[i], local_sems.at[i]) for i in range(count)]
    for copy in local:
        copy.start()
    greet(dims)
    for i in range(count):
        local[i].wait()
        cast_blocks(dims, totals[i], staged[i])
    run_rounds(dims, reduce_flows(dims, totals, staged, lands, send_sems, recv_sems))
    for i in range(count):
        outs[i][...] = totals[i][pos[0], pos[1], pos[2]]


def reduce_all(dims, parts):
    count = len(parts)
    shapes = [p.shape for p in parts]
    slots = flow_slots(dims, shapes)
    scratch = [DMA((slots,)), DMA((slots,)), DMA((count,))]
    scratch += [VMEM(s, F32) for s in shapes] + [VMEM(s, BF16) for s in shapes]
    scratch += landing_scratch(dims, shapes)
    return pl.pallas_call(
        partial(reduce_kernel, dims, count),
        name="reduce_gradients",
        out_shape=[jax.ShapeDtypeStruct(s[3:], F32) for s in shapes],
        in_specs=[pl.BlockSpec(memory_space=ANY)] * count,
        out_specs=[pl.BlockSpec(memory_space=VMEM)] * count,
        scratch_shapes=scratch,
        compiler_params=params(2),
    )(*parts)


def group_sums(row, spread):
    width = row.shape[1]
    return lax.dot_general(
        jnp.broadcast_to(row, (8, width)),
        spread,
        (((1,), (0,)), ((), ())),
        precision=HIGHEST,
        preferred_element_type=F32,
    )[0:1]


def group_spread(width, group):
    rows = lax.broadcasted_iota(I32, (width, width), 0) // group
    cols = lax.broadcasted_iota(I32, (width, width), 1) // group
    return (rows == cols).astype(F32)


def column_of(tile, width, lanes):
    return lax.broadcasted_iota(I32, (tile // width, width, lanes), 1).reshape(tile, lanes)


def dot(a, b, contract):
    return lax.dot_general(a, b, ((contract[0], contract[1]), ((), ())), preferred_element_type=F32)


NN = ((1,), (0,))
NT = ((1,), (1,))
TN = ((0,), (0,))


def conv_forward(source, weight, raw, rows, width, tile, n, live):
    def body(i, total):
        start = pl.multiple_of(i * tile, tile)
        wide = None
        for du in range(3):
            rows_in = pl.ds(pl.multiple_of(start + du * width, 16), tile)
            part = dot(source[rows_in, :], weight(du), NN)
            wide = part if wide is None else wide + part
        left = pltpu.roll(wide[:, :n], 1, 0)
        right = pltpu.roll(wide[:, 2 * n :], tile - 1, 0)
        column = column_of(tile, width, n)
        if live == width:
            left = jnp.where(column == 0, 0.0, left)
            right = jnp.where(column == width - 1, 0.0, right)
        value = left + wide[:, n : 2 * n] + right
        if live < width:
            value = jnp.where(column < live, value, 0.0)
        raw[pl.ds(start, tile), :] = value
        return total + jnp.sum(value, axis=0, keepdims=True)

    return lax.fori_loop(0, rows // tile, body, jnp.zeros((1, n), F32))


def norm_forward(raw, total, rows, width, tile, n, live, count, spread, gain, bias, store):
    mean = group_sums(total, spread) / count

    def spread_of(i, acc):
        start = pl.multiple_of(i * tile, tile)
        away = raw[pl.ds(start, tile), :] - mean
        if live < width:
            away = jnp.where(column_of(tile, width, n) < live, away, 0.0)
        return acc + jnp.sum(away * away, axis=0, keepdims=True)

    squares = lax.fori_loop(0, rows // tile, spread_of, jnp.zeros((1, n), F32))
    scale = lax.rsqrt(group_sums(squares, spread) / count + GN_EPS)

    def normalize(i, carry):
        start = pl.multiple_of(i * tile, tile)
        normed = (raw[pl.ds(start, tile), :] - mean) * scale
        raw[pl.ds(start, tile), :] = normed
        value = jnp.maximum(normed * gain + bias, 0.0)
        if live < width:
            value = jnp.where(column_of(tile, width, n) < live, value, 0.0)
        store(start, value.astype(BF16))
        return carry

    lax.fori_loop(0, rows // tile, normalize, 0)
    return scale


def norm_backward(
    normed, upstream, spare, shifted, rows, width, tile, n, live, count, spread, gain, bias, scale
):
    def first(i, sums):
        start = pl.multiple_of(i * tile, tile)
        here = normed[pl.ds(start, tile), :]
        value = jnp.where(here * gain + bias > 0.0, upstream(start), 0.0)
        if live < width:
            value = jnp.where(column_of(tile, width, n) < live, value, 0.0)
        spare[pl.ds(start, tile), :] = value
        return (
            sums[0] + jnp.sum(value * here, axis=0, keepdims=True),
            sums[1] + jnp.sum(value, axis=0, keepdims=True),
        )

    zero = jnp.zeros((1, n), F32)
    gain_sum, bias_sum = lax.fori_loop(0, rows // tile, first, (zero, zero))
    level = group_sums(bias_sum * gain, spread) / count
    slope = group_sums(gain_sum * gain, spread) / count

    def second(i, carry):
        start = pl.multiple_of(i * tile, tile)
        value = scale * (
            spare[pl.ds(start, tile), :] * gain - level - normed[pl.ds(start, tile), :] * slope
        )
        column = column_of(tile, width, n)
        if live < width:
            value = jnp.where(column < live, value, 0.0)
        left = pltpu.roll(value, tile - 1, 0)
        right = pltpu.roll(value, 1, 0)
        if live == width:
            left = jnp.where(column == width - 1, 0.0, left)
            right = jnp.where(column == 0, 0.0, right)
        into = pl.ds(pl.multiple_of(start + width, 16), tile)
        shifted[into, 0:n] = left.astype(BF16)
        shifted[into, n : 2 * n] = value.astype(BF16)
        shifted[into, 2 * n : 3 * n] = right.astype(BF16)
        return carry

    lax.fori_loop(0, rows // tile, second, 0)
    return gain_sum, bias_sum


def weight_gradient(source, shifted, total, rows, width, tile, lanes):
    span = lanes.stop - lanes.start

    def body(i, carry):
        start = pl.multiple_of(i * tile, tile)
        right = shifted[pl.ds(pl.multiple_of(start + width, 16), tile), lanes]
        for du in range(3):
            left = source[pl.ds(pl.multiple_of(start + du * width, 16), tile), :]
            value = dot(left, right, TN)
            into = total.at[..., du * span : (du + 1) * span]
            value = value.reshape(into.shape)

            @pl.when(i == 0)
            def _(into=into, value=value):
                into[...] = value

            @pl.when(i > 0)
            def _(into=into, value=value):
                into[...] += value

        return carry

    lax.fori_loop(0, rows // tile, body, 0)


def zero_rows(ref, rows):
    ref[0:rows, :] = jnp.zeros((rows, ref.shape[1]), ref.dtype)
    last = ref.shape[0]
    ref[last - rows : last, :] = jnp.zeros((rows, ref.shape[1]), ref.dtype)


def as_row(column):
    n = column.shape[0]
    rows = lax.broadcasted_iota(I32, (n, n), 0)
    cols = lax.broadcasted_iota(I32, (n, n), 1)
    return jnp.sum(jnp.where(rows == cols, column, 0.0), axis=0, keepdims=True)


def step_kernel(cfg, names, *refs):
    r = dict(zip(names, refs))
    dims, images = cfg["dims"], cfg["images"]
    wide, rows = cfg["wide"], cfg["rows"]
    pad, grid_rows, grid = cfg["pad"], cfg["grid_rows"], cfg["grid"]
    nm, ng, kc = cfg["nm"], cfg["ng"], cfg["kc"]
    fused = cfg["fused"]
    tile, small_tile = cfg["tile"], cfg["small_tile"]
    gtile = cfg["gtile"]
    pos = place(dims)
    model = lax.axis_index("mp")
    own_m = pl.ds(pl.multiple_of(model * nm, nm), nm)
    away_m = pl.ds(pl.multiple_of((1 - model) * nm, nm), nm)
    own_g = pl.ds(pl.multiple_of(model * ng, ng), ng)
    away_g = pl.ds(pl.multiple_of((1 - model) * ng, ng), ng)
    gin = r["xg_own"].shape[1]
    own_x = pl.ds(pl.multiple_of(model * gin, gin), gin)
    map_rows = pl.ds(wide, rows)
    grid_span = pl.ds(pad, grid_rows)
    mask_count = float(rows * (2 * nm // GROUPS))
    grid_count = float(grid * grid * (2 * ng // GROUPS))
    spread_m = group_spread(nm, 2 * nm // GROUPS)
    spread_g = group_spread(ng, 2 * ng // GROUPS)

    xm, xg = r["xm"], r["xg"]
    local = [
        pltpu.make_async_copy(r["xm_own"], xm.at[map_rows, own_x], r["local"].at[0]),
        pltpu.make_async_copy(r["xg_own"], xg.at[grid_span, own_x], r["local"].at[1]),
    ]
    if fused:
        for i in range(5):
            local.append(
                pltpu.make_async_copy(
                    r["w%d_own" % i],
                    r["w%d" % i].at[pos[0], pos[1], pos[2]],
                    r["local"].at[2 + i],
                )
            )
    for copy in local:
        copy.start()
    for name, count in (("xm", wide), ("hm", wide), ("dm", wide)):
        zero_rows(r[name], count)
    for name in ("xg", "hg", "dg2", "dg1"):
        zero_rows(r[name], pad)
    greet(dims)
    feature_copies = [
        pair_copy(r["xm_own"], xm.at[map_rows, own_x], r["pair"].at[0]),
        pair_copy(r["xg_own"], xg.at[grid_span, own_x], r["pair"].at[1]),
    ]
    for copy in feature_copies:
        copy.start()
    for copy in local:
        copy.wait()
    if fused:
        weights = [r["w%d" % i] for i in range(5)]
        run_rounds(dims, gather_flows(dims, weights, r["gs"], r["gr"]))

    def weight(i, span):
        def part(du):
            value = r["w%d" % i][..., du * span : (du + 1) * span]
            return value.reshape(-1, span) if fused else value

        return part

    mask_one, grid_one, mask_two = weight(0, 3 * nm), weight(1, 3 * ng), weight(2, 3 * nm)
    grid_two, class_two = weight(3, 3 * nm), weight(4, 128)

    norms, gnorms = r["mask_norms"], r["grid_norms"]
    row = lambda ref, k: ref[k : k + 1, :]
    feature_copies[0].wait()
    xh1, hm = r["xh1"], r["hm"]
    total = conv_forward(xm, mask_one, xh1, rows, wide, tile, nm, wide)

    def keep_mask(start, value):
        hm[pl.ds(pl.multiple_of(start + wide, 16), value.shape[0]), own_m] = value

    scale_one = norm_forward(
        xh1, total, rows, wide, small_tile, nm, wide, mask_count, spread_m,
        row(norms, 0), row(norms, 1), keep_mask,
    )
    hm_copy = pair_copy(hm.at[map_rows, own_m], hm.at[map_rows, own_m], r["pair"].at[2])
    hm_copy.start()
    feature_copies[1].wait()
    xhg, hg = r["xhg"], r["hg"]
    total = conv_forward(xg, grid_one, xhg, grid_rows, pad, gtile, ng, grid)

    def keep_grid(start, value):
        hg[pl.ds(pl.multiple_of(start + pad, 16), value.shape[0]), own_g] = value

    scale_grid = norm_forward(
        xhg, total, grid_rows, pad, gtile, ng, grid, grid_count, spread_g,
        row(gnorms, 0), row(gnorms, 1), keep_grid,
    )
    hg_copy = pair_copy(hg.at[grid_span, own_g], hg.at[grid_span, own_g], r["pair"].at[3])
    hg_copy.start()

    hm_copy.wait()
    xh2, feature = r["xh2"], r["feature"]
    total = conv_forward(hm, mask_two, xh2, rows, wide, tile, nm, wide)

    def keep_feature(start, value):
        feature[pl.ds(start, value.shape[0]), :] = value

    scale_two = norm_forward(
        xh2, total, rows, wide, small_tile, nm, wide, mask_count, spread_m,
        row(norms, 2), row(norms, 3), keep_feature,
    )

    hg_copy.wait()
    cells_col, cells_row = r["cells_col"][...], r["cells_row"][...]
    patches = r["patches"]
    lane = lax.broadcasted_iota(I32, (SLOTS, grid_rows), 1)
    depth = hg.shape[1]
    picked = None
    for t in range(9):
        chosen = (lane == cells_col + ((t // 3 - 1) * pad + t % 3 - 1)).astype(F32).astype(BF16)
        part = dot(chosen, hg[grid_span, :], NN).astype(BF16)
        patches[:, t * depth : (t + 1) * depth] = part
        w = grid_two(t // 3)[:, (t % 3) * nm : (t % 3 + 1) * nm]
        part = dot(part, w, NN)
        picked = part if picked is None else picked + part
    kernels = r["kernels"]
    kernels[pos[0], pos[1], pos[2], model] = picked.astype(BF16)
    kernel_share = Share(dims, kernels, r["ks"], r["kr"], True)
    kernel_share.advance()

    kernel_rows = kernels[pos[0], pos[1], pos[2], model]
    logits, logits_in = r["logits"], r["logits_in"]
    high_slots = logits.shape[0]
    for i in range(rows // tile):
        span = slice(i * tile, (i + 1) * tile)
        logits[:, span] = dot(kernel_rows[:high_slots], feature[span, :], NT).astype(BF16)
    logits_copy = pair_copy(logits, logits_in, r["pair"].at[4])
    logits_copy.start()
    kernel_share.advance()

    cdx = r["dg2"]
    focal_rows = r["focal_rows"][...]
    class_hot = (
        (lax.broadcasted_iota(I32, (SLOTS, 128), 1) == r["labels_col"][...])
        .astype(F32)
        .astype(BF16)
    )
    live_row = focal_rows[1:2]
    focal_scale = focal_rows[2:3]
    class_bias = focal_rows[0:1]

    def class_tile(i, sums):
        start = pl.multiple_of(i * gtile, gtile)
        value = None
        for du in range(3):
            part = dot(
                hg[pl.ds(pl.multiple_of(start + du * pad, 16), gtile), :], class_two(du), NN
            )
            value = part if value is None else value + part
        x = (
            pltpu.roll(value, 1, 0)
            + pltpu.roll(value, 128 - kc, 1)
            + pltpu.roll(pltpu.roll(value, 128 - 2 * kc, 1), gtile - 1, 0)
            + class_bias
        )
        at = lax.broadcasted_iota(I32, (gtile, SLOTS), 0) + start
        cell_hot = jnp.where(at == cells_row, live_row, 0.0).astype(BF16)
        t = dot(cell_hot, class_hot, NN)
        lanes = lax.broadcasted_iota(I32, (gtile, 128), 1)
        real = (column_of(gtile, pad, 128) < grid) & (lanes < kc)
        small = jnp.exp(-jnp.abs(x))
        extra = jnp.log1p(small)
        inverse = 1.0 / (1.0 + small)
        q = jnp.where(x >= 0.0, 1.0, small) * inverse
        p = jnp.where(x >= 0.0, small, 1.0) * inverse
        log_q = -(jnp.maximum(-x, 0.0) + extra)
        log_p = -(jnp.maximum(x, 0.0) + extra)
        terms = FOCAL_ALPHA * t * p * p * log_q + (1.0 - FOCAL_ALPHA) * (1.0 - t) * q * q * log_p
        slope = FOCAL_ALPHA * t * p * p * (p - 2.0 * q * log_q) + (1.0 - FOCAL_ALPHA) * (
            1.0 - t
        ) * q * q * (2.0 * p * log_p - q)
        slope = jnp.where(real, -focal_scale * slope, 0.0).astype(BF16).astype(F32)
        shifted = (
            pltpu.roll(slope, gtile - 1, 0)
            + pltpu.roll(slope, kc, 1)
            + pltpu.roll(pltpu.roll(slope, 2 * kc, 1), 1, 0)
        )
        cdx[pl.ds(pl.multiple_of(start + pad, 16), gtile), 3 * nm :] = shifted.astype(BF16)
        return (
            sums[0] + jnp.sum(jnp.where(real, -focal_scale * terms, 0.0), axis=0, keepdims=True),
            sums[1] + jnp.sum(slope, axis=0, keepdims=True),
        )

    zero = jnp.zeros((1, 128), F32)
    focal_sum, class_bias_sum = lax.fori_loop(
        0, grid_rows // gtile, class_tile, (zero, zero)
    )
    kernel_share.advance()

    logits_copy.wait()
    cols = r["cols"][...]
    dice_col = cols[:, 0:1]
    masks = r["masks"]
    slots = masks.shape[0]
    dice_sum = jnp.zeros((1, 1), F32)
    for start in range(0, slots, 16):
        span = slice(start, start + 16)
        x = logits[span, :].astype(F32) + logits_in[span, :].astype(F32)
        s = jax.nn.sigmoid(x)
        m = masks[start : min(start + 16, slots), :].astype(F32)
        if m.shape[0] < 16:
            m = jnp.concatenate([m, jnp.zeros((16 - m.shape[0], rows), F32)], axis=0)
        inter = jnp.sum(s * m, axis=1, keepdims=True)
        whole = jnp.sum(s * s, axis=1, keepdims=True) + jnp.sum(m, axis=1, keepdims=True) + 1.0
        share_here = dice_col[span]
        dice_sum += jnp.sum(share_here * (1.0 - 2.0 * inter / whole), keepdims=True)
        a = -2.0 * share_here / whole
        b = 2.0 * share_here * inter / (whole * whole)
        logits[span, :] = ((a * m + 2.0 * b * s) * s * (1.0 - s)).astype(BF16)
    kernel_share.complete()

    own_full = [kernels[pos[0], pos[1], pos[2], k] for k in range(2)]

    def key_block(d):
        index = split_index(dims, d)
        return [kernels[index[0], index[1], index[2], k] for k in range(2)]

    def squares_of(block):
        return sum(
            jnp.sum(jnp.square(part.astype(F32)), axis=1, keepdims=True) for part in block
        )

    own_scale = lax.rsqrt(squares_of(own_full) + 1e-06)
    own_image = lax.axis_index("dp")
    diagonal = lax.broadcasted_iota(I32, (SLOTS, SLOTS), 0) == lax.broadcasted_iota(
        I32, (SLOTS, SLOTS), 1
    )

    def scores(d):
        block = key_block(d)
        raw = dot(own_full[0], block[0], NT) + dot(own_full[1], block[1], NT)
        key_scale = lax.rsqrt(as_row(squares_of(block)) + 1e-06)
        scale = own_scale * key_scale / CONTRAST_TEMP
        keys = r["keys"][d]
        allowed = (keys[0:1] > 0.5) & jnp.logical_not(diagonal & (d == own_image))
        return block, raw, key_scale, scale, keys, allowed

    def sum_keys(d, acc):
        _, raw, _, scale, _, allowed = scores(d)
        value = jnp.where(allowed, jnp.exp(raw * scale), 0.0)
        return acc + jnp.sum(value, axis=1, keepdims=True)

    totals_col = lax.fori_loop(0, images, sum_keys, jnp.zeros((SLOTS, 1), F32))
    log_col = jnp.log(totals_col)
    weight_col = cols[:, 1:2]
    live_col = cols[:, 2:3]
    contrast_sum = jnp.sum(
        jnp.where(weight_col > 0.0, weight_col * log_col, 0.0), keepdims=True
    )
    logs = r["logs"]
    logs[pos[0], pos[1], pos[2]] = jnp.broadcast_to(as_row(log_col), (8, SLOTS))
    log_share = Share(dims, logs, r["ls"], r["lr"], False)
    log_share.advance()

    logit_rows = dot(logits[...], feature[...], NN)
    log_share.advance()
    dlogits = logits

    def from_logits(start):
        return dot(dlogits[:, pl.ds(start, small_tile)], kernel_rows[:high_slots], TN)

    dm = r["dm"]
    gain_two, bias_two = norm_backward(
        xh2, from_logits, r["spare"], dm, rows, wide, small_tile, nm, wide, mask_count, spread_m,
        row(norms, 2), row(norms, 3), scale_two,
    )
    log_share.advance()
    weight_gradient(hm, dm, r["g2"], rows, wide, tile, slice(0, 3 * nm))
    hidden = hm

    def input_tile(i, carry):
        start = pl.multiple_of(i * tile, tile)
        value = None
        for du in range(3):
            part = dot(
                dm[pl.ds(pl.multiple_of(start + (2 - du) * wide, 16), tile), :], mask_two(du), NT
            )
            value = part if value is None else value + part
        hidden[pl.ds(pl.multiple_of(start + wide, 16), tile), :] = value.astype(BF16)
        return carry

    lax.fori_loop(0, rows // tile, input_tile, 0)
    hidden_copy = pair_copy(hidden.at[map_rows, away_m], r["dhm_in"], r["pair"].at[5])
    hidden_copy.start()
    log_share.complete()

    def row_terms(d, acc):
        block, raw, key_scale, scale, keys, allowed = scores(d)
        index = split_index(dims, d)
        log_row = logs[index[0], index[1], index[2]][0:1]
        value = raw * scale
        query = jnp.where(allowed, jnp.exp(value - log_col) * weight_col, 0.0)
        keyed = allowed & (live_col > 0.5)
        key = jnp.where(keyed, jnp.exp(value - log_row) * keys[1:2], 0.0)
        query_low = (query * scale).astype(BF16)
        key_low = (key * scale).astype(BF16)
        mine = jnp.where(model == 0, block[0].astype(F32), block[1].astype(F32)).astype(BF16)
        return (
            acc[0] + dot(query_low, mine, NN) + dot(key_low, mine, NN),
            acc[1]
            + jnp.sum((query + key) * raw * key_scale / CONTRAST_TEMP, axis=1, keepdims=True),
        )

    row_sum, scale_sum = lax.fori_loop(
        0, images, row_terms, (jnp.zeros((SLOTS, nm), F32), jnp.zeros((SLOTS, 1), F32))
    )
    norm_grad = -0.5 * own_scale * own_scale * own_scale * scale_sum
    row_grad = row_sum + 2.0 * kernel_rows.astype(F32) * norm_grad
    row_grad = row_grad + jnp.concatenate(
        [logit_rows, jnp.zeros((SLOTS - high_slots, nm), F32)], axis=0
    )
    row_low = row_grad.astype(BF16)

    dg2 = r["dg2"]
    for i in range(grid_rows // gtile):
        at = lax.broadcasted_iota(I32, (gtile, SLOTS), 0) + i * gtile
        for dv in range(3):
            chosen = (at == cells_row + (dv - 1)).astype(F32).astype(BF16)
            dg2[pad + i * gtile : pad + (i + 1) * gtile, dv * nm : (dv + 1) * nm] = dot(
                chosen, row_low, NN
            ).astype(BF16)
    for t in range(9):
        value = dot(patches[:, t * depth : (t + 1) * depth], row_low, TN)
        into = r["g3"].at[..., t * nm : (t + 1) * nm]
        into[...] = value.reshape(into.shape)
    weight_gradient(hg, dg2, r["g4"], grid_rows, pad, gtile, slice(3 * nm, 3 * nm + 128))
    hidden_grid = hg

    def grid_input_tile(i, carry):
        start = pl.multiple_of(i * gtile, gtile)
        value = None
        for du in range(3):
            here = pl.ds(pl.multiple_of(start + (2 - du) * pad, 16), gtile)
            part = dot(dg2[here, : 3 * nm], grid_two(du), NT) + dot(
                dg2[here, 3 * nm :], class_two(du), NT
            )
            value = part if value is None else value + part
        hidden_grid[pl.ds(pl.multiple_of(start + pad, 16), gtile), :] = value.astype(BF16)
        return carry

    lax.fori_loop(0, grid_rows // gtile, grid_input_tile, 0)
    hidden_grid_copy = pair_copy(hidden_grid.at[grid_span, away_g], r["dhg_in"], r["pair"].at[6])
    hidden_grid_copy.start()

    hidden_copy.wait()
    hidden_in = r["dhm_in"]

    def both_halves(start):
        here = pl.ds(pl.multiple_of(start + wide, 16), small_tile)
        received = hidden_in[pl.ds(start, small_tile), :]
        return hidden[here, own_m].astype(F32) + received.astype(F32)

    gain_one, bias_one = norm_backward(
        xh1, both_halves, r["spare"], dm, rows, wide, small_tile, nm, wide, mask_count, spread_m,
        row(norms, 0), row(norms, 1), scale_one,
    )
    weight_gradient(xm, dm, r["g0"], rows, wide, tile, slice(0, 3 * nm))
    hidden_grid_copy.wait()
    hidden_grid_in = r["dhg_in"]

    def both_grid_halves(start):
        here = pl.ds(pl.multiple_of(start + pad, 16), gtile)
        received = hidden_grid_in[pl.ds(start, gtile), :]
        return hidden_grid[here, own_g].astype(F32) + received.astype(F32)

    dg1 = r["dg1"]
    gain_grid, bias_grid = norm_backward(
        xhg, both_grid_halves, r["spare_g"], dg1, grid_rows, pad, gtile, ng, grid, grid_count,
        spread_g, row(gnorms, 0), row(gnorms, 1), scale_grid,
    )
    weight_gradient(xg, dg1, r["g1"], grid_rows, pad, gtile, slice(0, 3 * ng))

    smalls = r["smalls"]
    blank = jnp.zeros((1, 128), F32)
    pieces = [gain_one, bias_one, gain_two, bias_two]
    pieces += [gain_grid[:, i : i + nm] for i in range(0, ng, nm)]
    pieces += [bias_grid[:, i : i + nm] for i in range(0, ng, nm)]
    pieces += [class_bias_sum]
    pieces += [blank] * (16 - len(pieces))
    smalls[pos[0], pos[1], pos[2]] = jnp.concatenate(pieces, axis=0)
    small_share = Share(dims, smalls, r["ss"], r["sr"], False)
    small_share.advance()

    if fused:
        totals = [r["g%d" % i] for i in range(5)]
        staged = weights
        lands = [r["land%d" % i] for i in range(cfg["lands"])]
        for a, b in zip(totals, staged):
            cast_blocks(dims, a, b)
        run_rounds(dims, reduce_flows(dims, totals, staged, lands, r["rs"], r["rr"]))
        squares = jnp.zeros((1, 1), F32)
        for i in range(5):
            value = totals[i][pos[0], pos[1], pos[2]]
            r["out%d" % i][...] = value
            squares += jnp.sum(value * value, keepdims=True)
    small_share.complete()

    def add_small(d, acc):
        index = split_index(dims, d)
        return acc + smalls[index[0], index[1], index[2]]

    small_sum = lax.fori_loop(0, images, add_small, jnp.zeros((16, 128), F32))
    r["small_out"][...] = small_sum
    first_model = (model == 0).astype(F32)
    loss = jnp.sum(focal_sum, keepdims=True) + first_model * (dice_sum + contrast_sum)
    if fused:
        first_device = (own_image == 0).astype(F32)
        squares += first_device * jnp.sum(small_sum * small_sum, keepdims=True)
        sums = r["sums"]
        at = lax.broadcasted_iota(I32, (8, 128), 0)
        sums[pos[0], pos[1], pos[2], model] = jnp.where(at == 0, squares, loss)
        sum_share = Share(dims, sums, r["us"], r["ur"], True)
        sum_share.complete()

        def add_sums(d, acc):
            index = split_index(dims, d)
            return acc + sums[index[0], index[1], index[2], 0] + sums[
                index[0], index[1], index[2], 1
            ]

        r["sum_out"][...] = lax.fori_loop(0, images, add_sums, jnp.zeros((8, 128), F32))
        sum_share.drain()
    else:
        r["sum_out"][...] = jnp.broadcast_to(loss, (8, 128))
    for shared in (kernel_share, log_share, small_share):
        shared.drain()


def run_step(cfg, inputs, weights):
    dims, fused = cfg["dims"], cfg["fused"]
    rows, wide, pad, grid_rows = cfg["rows"], cfg["wide"], cfg["pad"], cfg["grid_rows"]
    nm, ng = cfg["nm"], cfg["ng"]
    any_space = {"xm_own", "xg_own"}
    names, args, specs = [], [], []
    for name, value in inputs.items():
        names.append(name)
        args.append(value)
        specs.append(pl.BlockSpec(memory_space=ANY if name in any_space else VMEM))
    for i, value in enumerate(weights):
        names.append("w%d_own" % i if fused else "w%d" % i)
        args.append(value)
        specs.append(pl.BlockSpec(memory_space=VMEM))
    outs = {"small_out": ((16, 128), F32), "sum_out": ((8, 128), F32)}
    scratch = {}
    if fused:
        blocks = [dims + w.shape for w in weights]
        for i, shape in enumerate(blocks):
            outs["out%d" % i] = (shape[3:], F32)
            scratch["w%d" % i] = VMEM(shape, BF16)
            scratch["g%d" % i] = VMEM(shape, F32)
        lands = landing_scratch(dims, blocks)
        cfg = dict(cfg, lands=len(lands))
        for i, land in enumerate(lands):
            scratch["land%d" % i] = land
        slots = flow_slots(dims, blocks)
        for name in ("gs", "gr", "rs", "rr"):
            scratch[name] = DMA((slots,))
        scratch["sums"] = VMEM(dims + (2, 8, 128), F32)
        scratch["us"], scratch["ur"] = share_sems(dims)
    else:
        for i, w in enumerate(weights):
            outs["g%d" % i] = (w.shape, F32)
    c_in = 2 * inputs["xm_own"].shape[1]
    depth = 2 * ng
    slot_rows = -(-inputs["masks"].shape[0] // 16) * 16
    scratch.update(
        xm=VMEM((rows + 2 * wide, c_in), BF16),
        xg=VMEM((grid_rows + 2 * pad, c_in), BF16),
        xh1=VMEM((rows, nm), F32),
        hm=VMEM((rows + 2 * wide, 2 * nm), BF16),
        xhg=VMEM((grid_rows, ng), F32),
        hg=VMEM((grid_rows + 2 * pad, depth), BF16),
        xh2=VMEM((rows, nm), F32),
        feature=VMEM((rows, nm), BF16),
        patches=VMEM((SLOTS, 9 * depth), BF16),
        kernels=VMEM(dims + (2, SLOTS, nm), BF16),
        logits=VMEM((slot_rows, rows), BF16),
        logits_in=VMEM((slot_rows, rows), BF16),
        logs=VMEM(dims + (8, SLOTS), F32),
        dm=VMEM((rows + 2 * wide, 3 * nm), BF16),
        spare=VMEM((rows, nm), F32),
        dhm_in=VMEM((rows, nm), BF16),
        dg2=VMEM((grid_rows + 2 * pad, 3 * nm + 128), BF16),
        dhg_in=VMEM((grid_rows, ng), BF16),
        dg1=VMEM((grid_rows + 2 * pad, 3 * ng), BF16),
        spare_g=VMEM((grid_rows, ng), F32),
        smalls=VMEM(dims + (16, 128), F32),
        local=DMA((7,)),
        pair=DMA((7, 2)),
    )
    for a, b in (("ks", "kr"), ("ls", "lr"), ("ss", "sr")):
        scratch[a], scratch[b] = share_sems(dims)
    names += list(outs) + list(scratch)
    result = pl.pallas_call(
        partial(step_kernel, cfg, tuple(names)),
        name="step",
        out_shape=[jax.ShapeDtypeStruct(s, d) for s, d in outs.values()],
        in_specs=specs,
        out_specs=[pl.BlockSpec(memory_space=VMEM)] * len(outs),
        scratch_shapes=list(scratch.values()),
        compiler_params=params(0),
    )(*args)
    return dict(zip(outs, result))


def lanes_of_taps(weight):
    taps, depth, width = weight.shape
    return weight.transpose(1, 0, 2).reshape(depth, taps * width)


def taps_of_lanes(weight, width):
    depth = weight.shape[0]
    return weight.reshape(depth, -1, width).transpose(1, 0, 2)


def class_lanes(weight):
    _, depth, width = weight.shape
    rows = weight.transpose(1, 0, 2).reshape(depth, 3, 3 * width)
    return jnp.pad(rows, ((0, 0), (0, 0), (0, 128 - 3 * width))).reshape(depth, 384)


def class_taps(weight, width):
    depth = weight.shape[0]
    rows = weight.reshape(depth, 3, 128)[:, :, : 3 * width]
    return rows.reshape(depth, 9, width).transpose(1, 0, 2)


def adam_update(weight, moment, square, gradient, rate):
    moment_new = BETA_ONE * moment + (1.0 - BETA_ONE) * gradient
    square_new = BETA_TWO * square + (1.0 - BETA_TWO) * gradient * gradient
    moment_hat = moment_new / (1.0 - BETA_ONE**STEP_TIME)
    square_hat = square_new / (1.0 - BETA_TWO**STEP_TIME)
    weight_new = weight - rate * (
        moment_hat / (jnp.sqrt(square_hat) + ADAM_EPS) + WEIGHT_DECAY * weight
    )
    return (weight_new, moment_new, square_new)


def body(
    mask_features,
    grid_features,
    instance_cells,
    instance_counts,
    instance_labels,
    instance_masks,
    mask_convs,
    mask_convs_moment,
    mask_convs_square,
    grid_first,
    grid_first_moment,
    grid_first_square,
    grid_second,
    grid_second_moment,
    grid_second_square,
    class_conv,
    class_conv_moment,
    class_conv_square,
    mask_norms,
    mask_norms_moment,
    mask_norms_square,
    grid_norms,
    grid_norms_moment,
    grid_norms_square,
    class_bias,
    class_bias_moment,
    class_bias_square,
):
    images = lax.axis_size("dp")
    data_index = lax.axis_index("dp")
    model_index = lax.axis_index("mp")
    dims = line_lengths(images)
    _, high, wide, half = mask_features.shape
    grid = grid_features.shape[1]
    pad = -(-(grid + 1) // 16) * 16
    nm, ng, kc = mask_convs.shape[3], grid_first.shape[2], class_conv.shape[2]
    count = instance_cells.shape[1]
    owner_rows = grid_first.shape[1]
    fused = owner_rows % 16 == 0
    cfg = dict(
        dims=dims,
        images=images,
        wide=wide,
        rows=high * wide,
        pad=pad,
        grid=grid,
        grid_rows=grid * pad,
        nm=nm,
        ng=ng,
        kc=kc,
        fused=fused,
        tile=8 * wide,
        small_tile=4 * wide,
        gtile=grid // 2 * pad,
    )

    share = jnp.float32(1.0 / images)
    counts = instance_counts.astype(F32)
    slot = jnp.arange(SLOTS)
    live = (slot[None, :] < instance_counts[:, None]).astype(F32)
    weights_all = live * (share / counts)[:, None]
    keys = jnp.stack([live, weights_all], axis=1)
    keys = jnp.pad(keys, ((0, 0), (0, 6), (0, 0)))
    own_live = lax.dynamic_index_in_dim(live, data_index, keepdims=False)
    own_weight = lax.dynamic_index_in_dim(weights_all, data_index, keepdims=False)
    own_count = lax.dynamic_index_in_dim(counts, data_index, keepdims=False)
    cols = jnp.stack([DICE_WEIGHT * own_weight, own_weight, own_live], axis=1)
    cols = jnp.pad(cols, ((0, 0), (0, 5)))
    cells = instance_cells[0]
    cells = (cells // grid) * pad + cells % grid
    cells = jnp.pad(cells, (0, SLOTS - count), constant_values=-(1 << 20))
    labels = instance_labels[0] - model_index * kc
    labels = jnp.pad(labels, (0, SLOTS - count), constant_values=-1)
    labels = jnp.where((labels >= 0) & (labels < kc), labels, -1)
    focal_rows = jnp.stack(
        [
            jnp.pad(class_bias, (0, 128 - kc)),
            own_live,
            jnp.full((128,), share / (own_count + 1.0)),
        ]
    )
    inputs = dict(
        xm_own=mask_features.reshape(-1, half),
        xg_own=jnp.pad(grid_features[0], ((0, 0), (0, pad - grid), (0, 0))).reshape(-1, half),
        masks=instance_masks[0],
        mask_norms=mask_norms,
        grid_norms=grid_norms,
        focal_rows=jnp.pad(focal_rows, ((0, 5), (0, 0))),
        cols=cols,
        cells_col=cells[:, None],
        cells_row=cells[None, :],
        labels_col=labels[:, None],
        keys=keys,
    )
    shards = [
        lanes_of_taps(mask_convs[0].astype(BF16)),
        lanes_of_taps(grid_first.astype(BF16)),
        lanes_of_taps(mask_convs[1].astype(BF16)),
        lanes_of_taps(grid_second.astype(BF16)),
        class_lanes(class_conv.astype(BF16)),
    ]
    if fused:
        out = run_step(cfg, inputs, shards)
        reduced = [out["out%d" % i] for i in range(5)]
        sums = out["sum_out"]
        total_squares, step_loss = sums[0, 0], sums[1, 0]
    else:
        blocks = gather_all(dims, shards)
        out = run_step(cfg, inputs, [b.reshape(-1, b.shape[-1]) for b in blocks])
        reduced = reduce_all(
            dims, [out["g%d" % i].reshape(b.shape) for i, b in enumerate(blocks)]
        )
        squares = sum(jnp.sum(jnp.square(value)) for value in reduced)
        squares += (data_index == 0).astype(F32) * jnp.sum(jnp.square(out["small_out"]))
        total_squares, step_loss = lax.psum((squares, out["sum_out"][0, 0]), ("dp", "mp"))
    small = out["small_out"]
    mask_sum_w = jnp.stack([taps_of_lanes(reduced[0], nm), taps_of_lanes(reduced[2], nm)])
    first_sum_w = taps_of_lanes(reduced[1], ng)
    second_sum_w = taps_of_lanes(reduced[3], nm)
    class_sum_w = class_taps(reduced[4], kc)
    per = ng // nm
    mask_norm_sum = small[:4]
    grid_norm_sum = small[4 : 4 + 2 * per].reshape(2, ng)
    bias_sum = small[4 + 2 * per, :kc]
    gradient_norm = jnp.sqrt(total_squares)
    factor = jnp.minimum(1.0, CLIP_LIMIT / gradient_norm)
    mask_new = adam_update(
        mask_convs, mask_convs_moment, mask_convs_square, mask_sum_w * factor, LEARN_RATE
    )
    first_new = adam_update(
        grid_first, grid_first_moment, grid_first_square, first_sum_w * factor, LEARN_RATE
    )
    second_new = adam_update(
        grid_second, grid_second_moment, grid_second_square, second_sum_w * factor, LEARN_RATE
    )
    class_new = adam_update(
        class_conv, class_conv_moment, class_conv_square, class_sum_w * factor, LEARN_RATE
    )
    mask_norm_new = adam_update(
        mask_norms, mask_norms_moment, mask_norms_square, mask_norm_sum * factor, SMALL_RATE
    )
    grid_norm_new = adam_update(
        grid_norms, grid_norms_moment, grid_norms_square, grid_norm_sum * factor, SMALL_RATE
    )
    bias_new = adam_update(
        class_bias, class_bias_moment, class_bias_square, bias_sum * factor, SMALL_RATE
    )
    return (
        step_loss,
        gradient_norm,
        mask_new[0],
        mask_new[1],
        mask_new[2],
        first_new[0],
        first_new[1],
        first_new[2],
        second_new[0],
        second_new[1],
        second_new[2],
        class_new[0],
        class_new[1],
        class_new[2],
        mask_norm_new[0],
        mask_norm_new[1],
        mask_norm_new[2],
        grid_norm_new[0],
        grid_norm_new[1],
        grid_norm_new[2],
        bias_new[0],
        bias_new[1],
        bias_new[2],
    )


def solution(mesh):
    in_specs = (
        P("dp", None, None, "mp"),
        P("dp", None, None, "mp"),
        P("dp", None),
        P(),
        P("dp", None),
        P("dp", None, None),
        P(None, None, "dp", "mp"),
        P(None, None, "dp", "mp"),
        P(None, None, "dp", "mp"),
        P(None, "dp", "mp"),
        P(None, "dp", "mp"),
        P(None, "dp", "mp"),
        P(None, "dp", "mp"),
        P(None, "dp", "mp"),
        P(None, "dp", "mp"),
        P(None, "dp", "mp"),
        P(None, "dp", "mp"),
        P(None, "dp", "mp"),
        P(None, "mp"),
        P(None, "mp"),
        P(None, "mp"),
        P(None, "mp"),
        P(None, "mp"),
        P(None, "mp"),
        P("mp"),
        P("mp"),
        P("mp"),
    )
    out_specs = (
        P(),
        P(),
        P(None, None, "dp", "mp"),
        P(None, None, "dp", "mp"),
        P(None, None, "dp", "mp"),
        P(None, "dp", "mp"),
        P(None, "dp", "mp"),
        P(None, "dp", "mp"),
        P(None, "dp", "mp"),
        P(None, "dp", "mp"),
        P(None, "dp", "mp"),
        P(None, "dp", "mp"),
        P(None, "dp", "mp"),
        P(None, "dp", "mp"),
        P(None, "mp"),
        P(None, "mp"),
        P(None, "mp"),
        P(None, "mp"),
        P(None, "mp"),
        P(None, "mp"),
        P("mp"),
        P("mp"),
        P("mp"),
    )
    return jax.shard_map(body, mesh=mesh, in_specs=in_specs, out_specs=out_specs, check_vma=False)
```

time: 1040 us -> 236 us (0.23)
  waiting for transfers between devices: 413 us -> 0 us
  blocking collectives: 256 us -> 0 us
  matrix products: 217 us -> 0 us
  Pallas kernels: 0 us -> 198 us
  other arithmetic: 62.9 us -> 19.2 us
  local copies, waits for them, and re-layouts: 54.7 us -> 14.6 us
  between operations: 24.9 us -> 3.45 us
    reduce_scatter x4 -> x0, waiting for transfers between devices: 245 us -> none  [the longest x1 129 us: body(): lax.psum_scatter(grad_mask_convs, 'dp', scatter_dimension=2, tiled=True)]
    dot_general x124 -> x0, matrix products: 217 us -> none  [the longest x27 102 us: conv_input_grad(): jnp.einsum('hwd,cd->hwc', shifted_view(padded, tap_index, height, columns...]
    pallas_call x0 -> x1, Pallas kernels: none -> 198 us  [run_step(): pl.pallas_call(partial(step_kernel, cfg, tuple(names)), name='step', out_...]
    all_gather x6 -> x0, waiting for transfers between devices: 104 us -> none  [the longest x1 54.3 us: body(): lax.all_gather(grid_first.astype(jnp.bfloat16), 'dp', axis=1, tiled=True)]
    all_gather x3 -> x0, blocking collectives: 94.6 us -> none  [the longest x1 49.4 us: body(): lax.all_gather(class_conv.astype(jnp.bfloat16), 'dp', axis=1, tiled=True)]
    psum x2 -> x0, blocking collectives: 80.8 us -> none  [the longest x1 40.7 us: body(): lax.psum((mask_norm_grad, grid_norm_grad, grad_class_bias), 'dp')]
    unnamed x1 -> x0, blocking collectives: 80.7 us -> none
    unnamed x19 -> x0, waiting for transfers between devices: 56.6 us -> none
  transfers between devices with their start and end apart: 17 -> 0, of which waited for: 8 -> 0; matrix products, arithmetic and copies ran while one was open for 22% -> 0% of each run, Pallas kernels for 0% -> 0%
where the time goes in v2:
time: 236 us; the launch traced here: 235 us
  Pallas kernels  198 us (84%)
  other arithmetic  19.2 us (8%)
  local copies, waits for them, and re-layouts  14.6 us (6%)
  between operations  3.45 us (1%)
    pallas_call x1, Pallas kernels, run_step(): pl.pallas_call(partial(step_kernel, cfg, tuple(names)), name='step', out_...  198 us
    sub x7, other arithmetic, adam_update(): weight - rate * (moment_hat / (jnp.sqrt(square_hat) + ADAM_EPS) + WEIGHT_...  8.38 us

profile of v2, /device:TPU:0, one launch (start us, length us, event | category | flops | bytes accessed | tf_op | source)
XLA Modules:
  0.0 235.3 jit_solution(2903952784852379351)
XLA Ops:
  0.7 0.0 copy-start.1
  0.7 0.0 copy-start
  0.7 0.0 copy-start.5
  0.7 0.8 subtract_bitcast_fusion
  1.5 0.7 broadcast_divide_fusion
  2.2 0.6 dynamic-slice
  2.8 0.7 fusion.12
  3.4 0.7 pad_bitcast_fusion
  4.1 0.7 convert_element_type.45
  4.7 0.6 dynamic_slice.12
  6.0 0.1 pad.48.clone
  6.1 0.5 pad_bitcast_fusion.1
  6.6 0.7 iota_compare_fusion.1
  7.4 0.7 broadcast_multiply_fusion.1
  8.1 0.1 maximum_maximum_fusion
  8.1 0.6 pad.33.refs_5_
  8.7 0.7 compare_select_fusion
  9.5 0.7 compare_convert_fusion
  10.2 0.7 select_maximum_fusion.refs_10_
  10.9 0.1 copy.137
  11.0 0.6 pad.34.refs_6_
  11.6 0.7 copy.144.refs_9_
  12.4 0.7 copy.143.refs_7_
  13.1 0.9 convert.4
  14.0 0.6 copy_bitcast_fusion.2
  14.7 0.9 convert_bitcast_fusion.2
  15.6 0.6 copy.156
  16.2 1.6 copy_bitcast_fusion.1.refs_14_
  17.8 0.0 copy-done.1
  17.9 0.1 reshape.195
  18.0 0.6 copy.180
  18.6 0.0 copy-done.5
  18.6 0.8 pad.31
  19.5 0.0 copy-done
  19.5 2.4 %copy.179 = s32[1,100,4096]{2,1,0:T(8,128)} copy(s32[1,100,4096]{2,0,1:T(1,128)S(1)} %copy-done) | data formatting | bytes 3276800
  21.9 198.0 %step.1 = (f32[16,128]{1,0:T(8,128)}, f32[8,128]{1,0:T(8,128)}, f32[16,1152]{1,0:T(8,128)}, f32[16,2304]{1,0:T(8,128)}, f32[16,1152]{1,0:T(8,128)}, /*index=5*/f32[32,1152]{1,0:T(8,128)}, f32[32,384]{1,0:T(8,128)}) custom-call(bf16[4096,128]{1,0:T(8,128)(2,1)} %bitcast.147, bf16[1920,128]{1,0:T(8,128)(2,1)} %bitcast.146, s32[100,4096]{1,0:T(8,128)} %bitcast.145, ...), custom_call_target="tpu_custom_call" | custom-call | tf_op jit(solution)/shard_map/step/pallas_call | solution.py:1142
  219.8 0.0 copy-start.2
  219.8 0.0 copy-start.6
  219.9 0.0 copy-start.7
  219.9 1.3 fusion.28
  221.9 0.0 copy-start.3
  221.9 0.0 copy-start.8
  221.9 0.0 copy-start.9
  221.9 0.0 copy-start.10
  221.9 1.0 broadcast_multiply_fusion
  222.9 1.2 multiply_subtract_fusion.6
  224.2 1.4 multiply_subtract_fusion.5
  225.5 1.3 multiply_subtract_fusion.4
  226.8 0.8 reshape.199
  227.7 0.9 bitcast_bitcast_fusion.3
  228.6 0.9 bitcast_bitcast_fusion.2
  229.5 0.0 copy-start.12
  229.5 0.1 mul.385
  229.6 2.0 multiply_subtract_fusion
  231.6 0.0 copy-done.2
  231.6 0.0 copy-done.6
  231.6 0.0 copy-done.7
  231.6 0.8 multiply_subtract_fusion.3
  232.4 0.0 copy-done.3
  232.4 0.0 copy-done.8
  232.4 0.0 copy-done.9
  232.5 0.8 multiply_subtract_fusion.1
  233.3 0.0 copy-done.12
  233.3 0.8 multiply_subtract_fusion.2
  (15 shorter events, 0.2 us)
Async XLA Ops:
  0.7 17.1 %copy-start.1 = (f32[9,32,40]{2,1,0:T(8,128)S(1)}, f32[9,32,40]{2,1,0:T(8,128)}, u32[]{:S(2)}) copy-start(f32[9,32,40]{2,1,0:T(8,128)} %param.42) | copy-start | bytes 138244
  0.7 18.8 %copy-start = (s32[1,100,4096]{2,0,1:T(1,128)S(1)}, s32[1,100,4096]{2,0,1:T(1,128)}, u32[]{:S(2)}) copy-start(s32[1,100,4096]{2,0,1:T(1,128)} %param.32) | copy-start | bytes 4915204
  0.7 18.0 %copy-start.5 = (bf16[1,40,40,128]{3,2,1,0:T(8,128)(2,1)S(1)}, bf16[1,40,40,128]{3,2,1,0:T(8,128)(2,1)}, u32[]{:S(2)}) copy-start(bf16[1,40,40,128]{3,2,1,0:T(8,128)(2,1)} %param.28) | copy-start | bytes 1228804
  219.8 11.8 %copy-start.2 = (f32[2,9,16,128]{3,2,1,0:T(8,128)S(1)}, f32[2,9,16,128]{3,2,1,0:T(8,128)}, u32[]{:S(2)}) copy-start(f32[2,9,16,128]{3,2,1,0:T(8,128)} %param.33) | copy-start | bytes 442372
  219.8 11.7 %copy-start.6 = (f32[2,9,16,128]{3,2,1,0:T(8,128)S(1)}, f32[2,9,16,128]{3,2,1,0:T(8,128)}, u32[]{:S(2)}) copy-start(f32[2,9,16,128]{3,2,1,0:T(8,128)} %param.34) | copy-start | bytes 442372
  219.9 11.7 %copy-start.7 = (f32[2,9,16,128]{3,2,1,0:T(8,128)S(1)}, f32[2,9,16,128]{3,2,1,0:T(8,128)}, u32[]{:S(2)}) copy-start(f32[2,9,16,128]{3,2,1,0:T(8,128)} %param.35) | copy-start | bytes 442372
  221.9 10.6 %copy-start.3 = (f32[9,32,128]{2,1,0:T(8,128)S(1)}, f32[9,32,128]{2,1,0:T(8,128)}, u32[]{:S(2)}) copy-start(f32[9,32,128]{2,1,0:T(8,128)} %param.39) | copy-start | bytes 442372
  221.9 10.5 %copy-start.8 = (f32[9,32,128]{2,1,0:T(8,128)S(1)}, f32[9,32,128]{2,1,0:T(8,128)}, u32[]{:S(2)}) copy-start(f32[9,32,128]{2,1,0:T(8,128)} %param.40) | copy-start | bytes 442372
  221.9 10.5 %copy-start.9 = (f32[9,32,128]{2,1,0:T(8,128)S(1)}, f32[9,32,128]{2,1,0:T(8,128)}, u32[]{:S(2)}) copy-start(f32[9,32,128]{2,1,0:T(8,128)} %param.41) | copy-start | bytes 442372
  221.9 10.5 %copy-start.10 = (f32[32,1152]{1,0:T(8,128)S(1)}, f32[32,1152]{1,0:T(8,128)}, u32[]{:S(2)}) copy-start(f32[32,1152]{1,0:T(8,128)} %get-tuple-element.34) | copy-start | bytes 442372
  229.5 3.8 %copy-start.4 = (f32[9,16,256]{2,1,0:T(8,128)S(1)}, f32[9,16,256]{2,1,0:T(8,128)}, u32[]{:S(2)}) copy-start(f32[9,16,256]{2,1,0:T(8,128)} %param.36) | copy-start | bytes 442372
  229.5 3.8 %copy-start.11 = (f32[9,16,256]{2,1,0:T(8,128)S(1)}, f32[9,16,256]{2,1,0:T(8,128)}, u32[]{:S(2)}) copy-start(f32[9,16,256]{2,1,0:T(8,128)} %param.37) | copy-start | bytes 442372
  229.5 3.8 %copy-start.12 = (f32[9,16,256]{2,1,0:T(8,128)S(1)}, f32[9,16,256]{2,1,0:T(8,128)}, u32[]{:S(2)}) copy-start(f32[9,16,256]{2,1,0:T(8,128)} %param.38) | copy-start | bytes 442372

commit v3 on v2

v3 whole, which is shorter than its diff:
```python
from functools import partial

import jax
import jax.numpy as jnp
from jax import lax
from jax.experimental import pallas as pl
from jax.experimental.pallas import tpu as pltpu
from jax.sharding import PartitionSpec as P

GROUPS = 32
GN_EPS = 1e-05
CLIP_LIMIT = 0.02
LEARN_RATE = 0.02
SMALL_RATE = 0.5
BETA_ONE = 0.9
BETA_TWO = 0.95
ADAM_EPS = 1e-08
WEIGHT_DECAY = 0.05
CONTRAST_TEMP = 0.05
FOCAL_ALPHA = 0.25
DICE_WEIGHT = 3.0
STEP_TIME = 10.0
HIGHEST = lax.Precision.HIGHEST

MESH = pl.DeviceIdType.MESH
VMEM = pltpu.VMEM
ANY = pl.ANY
VMEM_LIMIT = 67043328
F32 = jnp.float32
BF16 = jnp.bfloat16
I32 = jnp.int32
SLOTS = 128
DMA = pltpu.SemaphoreType.DMA


def line_lengths(total):
    if total & (total - 1):
        return (total, 1, 1)
    bits = total.bit_length() - 1
    last = bits // 3
    middle = (bits - last) // 2
    return (1 << (bits - last - middle), 1 << middle, 1 << last)


def place(dims):
    index = lax.axis_index("dp")
    return (index // (dims[1] * dims[2]), (index // dims[2]) % dims[1], index % dims[2])


def split_index(dims, index):
    return (
        index // (dims[1] * dims[2]),
        lax.rem(index // dims[2], dims[1]),
        lax.rem(index, dims[2]),
    )


def along(dims, axis, step):
    stride = (dims[1] * dims[2], dims[2], 1)[axis]
    return {"dp": lax.axis_index("dp") + step * stride}


def partner():
    return {"mp": 1 - lax.axis_index("mp")}


def ring_step(dims, pos, axis, offset):
    other = lax.rem(pos[axis] + offset, dims[axis])
    return along(dims, axis, other - pos[axis])


def greet(dims):
    sem = pltpu.get_barrier_semaphore()
    pos = place(dims)
    count = 1
    for axis in range(3):
        for offset in range(1, dims[axis]):
            pl.semaphore_signal(
                sem, inc=1, device_id=ring_step(dims, pos, axis, offset), device_id_type=MESH
            )
            count += 1
    pl.semaphore_signal(sem, inc=1, device_id=partner(), device_id_type=MESH)
    pl.semaphore_wait(sem, count)


GATHER_ORDERS = ((2, 1, 0), (0, 2, 1), (0, 1, 2))
REDUCE_ORDERS = tuple(tuple(reversed(order)) for order in GATHER_ORDERS)


def line_copies(dims):
    return sum(n - 1 for n in dims)


def lane_cuts(width):
    tiles = width // 128
    if width % 128 or tiles < 3:
        return ((0, 0, width),)
    first = max(1, round(tiles * 0.1))
    second = (tiles - first) // 2
    sizes = (first, second, tiles - first - second)
    cuts, start = [], 0
    for order, size in enumerate(sizes):
        cuts.append((order, start * 128, size * 128))
        start += size
    return tuple(cuts)


class Exchange:
    def __init__(self):
        self.stages, self.lands, self.next = [], [], 0

    def finish(self):
        if 0 < self.next <= len(self.stages):
            for copy in self.stages[self.next - 1]:
                copy.wait_recv()
            self.lands[self.next - 1]()

    def start(self):
        if self.next < len(self.stages):
            for copy in self.stages[self.next]:
                copy.start()
        self.next += 1

    def drain(self):
        for stage in self.stages:
            for copy in stage:
                copy.wait_send()


def advance(*exchanges):
    for exchange in exchanges:
        exchange.finish()
    for exchange in exchanges:
        exchange.start()


def complete(*exchanges):
    while any(e.next <= len(e.stages) for e in exchanges):
        advance(*exchanges)


def nothing():
    return None


def gather_exchange(dims, out, send_sems, recv_sems, base, lanes, order, tail=None):
    pos = place(dims)
    result, done = Exchange(), set()
    tail = (slice(None), lanes) if tail is None else tail
    for axis in order:
        view = out.at[tuple(pl.ds(0, dims[k]) if k in done else pos[k] for k in range(3)) + tail]
        copies = []
        for offset in range(1, dims[axis]):
            copies.append(
                pltpu.make_async_remote_copy(
                    src_ref=view,
                    dst_ref=view,
                    send_sem=send_sems.at[base],
                    recv_sem=recv_sems.at[base],
                    device_id=ring_step(dims, pos, axis, offset),
                    device_id_type=MESH,
                )
            )
            base += 1
        if copies:
            result.stages.append(copies)
            result.lands.append(nothing)
        done.add(axis)
    return result


def share_exchange(dims, out, send_sems, recv_sems, core):
    model = lax.axis_index("mp")
    result = gather_exchange(
        dims, out, send_sems, recv_sems, 0, None, (2, 1, 0), (model,) if core else ()
    )
    if core:
        view = out.at[:, :, :, model]
        result.stages.append(
            [
                pltpu.make_async_remote_copy(
                    src_ref=view,
                    dst_ref=view,
                    send_sem=send_sems.at[line_copies(dims)],
                    recv_sem=recv_sems.at[line_copies(dims)],
                    device_id=partner(),
                    device_id_type=MESH,
                )
            ]
        )
        result.lands.append(nothing)
    return result


def landing_shapes(dims, rows, width, order):
    shapes, left = [], {0, 1, 2}
    for axis in order:
        left = left - {axis}
        shapes.append(
            (max(1, dims[axis] - 1),) + tuple(dims[k] for k in sorted(left)) + (rows, width)
        )
    return shapes


def reduce_exchange(dims, total, staged, lands, send_sems, recv_sems, base, lanes, order):
    pos = place(dims)
    result, reduced = Exchange(), set()
    for stage, axis in enumerate(order):
        n = dims[axis]
        free = [k for k in range(3) if k not in reduced and k != axis]

        def view(block, lead=None, axis=axis, reduced=frozenset(reduced)):
            lead = iter(lead) if lead is not None else None
            index = []
            for k in range(3):
                if k == axis:
                    index.append(block)
                elif k in reduced:
                    index.append(pos[k])
                else:
                    index.append(pl.ds(0, dims[k]) if lead is None else next(lead))
            return tuple(index) + (slice(None), lanes)

        copies = []
        for offset in range(1, n):
            copies.append(
                pltpu.make_async_remote_copy(
                    src_ref=staged.at[view(lax.rem(pos[axis] + offset, n))],
                    dst_ref=lands[stage].at[offset - 1],
                    send_sem=send_sems.at[base],
                    recv_sem=recv_sems.at[base],
                    device_id=ring_step(dims, pos, axis, offset),
                    device_id_type=MESH,
                )
            )
            base += 1

        def land(stage=stage, axis=axis, n=n, free=free, view=view):
            sizes = [dims[k] for k in free]
            blocks = 1
            for size in sizes:
                blocks *= size

            def add(i, carry):
                lead, rest = [], i
                for size in reversed(sizes):
                    lead.append(lax.rem(rest, size))
                    rest = rest // size
                lead = lead[::-1]
                index = view(pos[axis], lead)
                value = total[index]
                for k in range(n - 1):
                    value = value + lands[stage][(k,) + tuple(lead)].astype(F32)
                total[index] = value
                if sizes:
                    staged[index] = value.astype(BF16)
                return carry

            if blocks == 1:
                add(jnp.int32(0), 0)
            else:
                lax.fori_loop(0, blocks, add, 0)

        if copies:
            result.stages.append(copies)
            result.lands.append(land)
        reduced.add(axis)
    return result


def share_sems(dims):
    return [DMA((line_copies(dims) + 1,)), DMA((line_copies(dims) + 1,))]


def pair_copy(source, target, sems):
    return pltpu.make_async_remote_copy(
        src_ref=source,
        dst_ref=target,
        send_sem=sems.at[0],
        recv_sem=sems.at[1],
        device_id=partner(),
        device_id_type=MESH,
    )


def params(collective_id):
    return pltpu.CompilerParams(
        collective_id=collective_id, has_side_effects=True, vmem_limit_bytes=VMEM_LIMIT
    )


def gather_groups(dims, outs, send_sems, recv_sems):
    groups, base = [], 0
    for out in outs:
        group = []
        for order, start, size in lane_cuts(out.shape[4]):
            group.append(
                gather_exchange(
                    dims, out, send_sems, recv_sems, base, pl.ds(start, size), GATHER_ORDERS[order]
                )
            )
            base += line_copies(dims)
        groups.append(group)
    return groups


def reduce_groups(dims, totals, staged, lands, send_sems, recv_sems):
    groups, base, lands = [], 0, list(lands)
    for total, stage in zip(totals, staged):
        group = []
        for order, start, size in lane_cuts(total.shape[4]):
            group.append(
                reduce_exchange(
                    dims,
                    total,
                    stage,
                    lands[:3],
                    send_sems,
                    recv_sems,
                    base,
                    pl.ds(start, size),
                    REDUCE_ORDERS[order],
                )
            )
            lands = lands[3:]
            base += line_copies(dims)
        groups.append(group)
    return groups


def flow_slots(dims, shapes):
    return max(1, line_copies(dims) * sum(len(lane_cuts(s[-1])) for s in shapes))


def landing_scratch(dims, shapes):
    scratch = []
    for shape in shapes:
        for order, _, size in lane_cuts(shape[-1]):
            for land in landing_shapes(dims, shape[-2], size, REDUCE_ORDERS[order]):
                scratch.append(VMEM(land, BF16))
    return scratch


def cast_blocks(dims, total, staged):
    def cast(j, carry):
        index = split_index(dims, j)
        staged[index] = total[index].astype(BF16)
        return carry

    lax.fori_loop(0, dims[0] * dims[1] * dims[2], cast, 0)


def run_all(groups):
    exchanges = [exchange for group in groups for exchange in group]
    complete(*exchanges)
    for exchange in exchanges:
        exchange.drain()


def gather_kernel(dims, count, *refs):
    shards, outs = refs[:count], refs[count : 2 * count]
    send_sems, recv_sems, local_sems = refs[2 * count :]
    pos = place(dims)
    local = [
        pltpu.make_async_copy(shards[i], outs[i].at[pos[0], pos[1], pos[2]], local_sems.at[i])
        for i in range(count)
    ]
    for copy in local:
        copy.start()
    greet(dims)
    for copy in local:
        copy.wait()
    run_all(gather_groups(dims, outs, send_sems, recv_sems))


def gather_all(dims, shards):
    count = len(shards)
    shapes = [dims + s.shape for s in shards]
    slots = flow_slots(dims, shapes)
    return pl.pallas_call(
        partial(gather_kernel, dims, count),
        name="gather_weights",
        out_shape=[jax.ShapeDtypeStruct(s, BF16) for s in shapes],
        in_specs=[pl.BlockSpec(memory_space=VMEM)] * count,
        out_specs=[pl.BlockSpec(memory_space=VMEM)] * count,
        scratch_shapes=[DMA((slots,)), DMA((slots,)), DMA((count,))],
        compiler_params=params(1),
    )(*shards)


def reduce_kernel(dims, count, *refs):
    parts, outs = refs[:count], refs[count : 2 * count]
    send_sems, recv_sems, local_sems = refs[2 * count : 2 * count + 3]
    rest = list(refs[2 * count + 3 :])
    totals, staged, lands = rest[:count], rest[count : 2 * count], rest[2 * count :]
    pos = place(dims)
    local = [pltpu.make_async_copy(parts[i], totals[i], local_sems.at[i]) for i in range(count)]
    for copy in local:
        copy.start()
    greet(dims)
    for i in range(count):
        local[i].wait()
        cast_blocks(dims, totals[i], staged[i])
    run_all(reduce_groups(dims, totals, staged, lands, send_sems, recv_sems))
    for i in range(count):
        outs[i][...] = totals[i][pos[0], pos[1], pos[2]]


def reduce_all(dims, parts):
    count = len(parts)
    shapes = [p.shape for p in parts]
    slots = flow_slots(dims, shapes)
    scratch = [DMA((slots,)), DMA((slots,)), DMA((count,))]
    scratch += [VMEM(s, F32) for s in shapes] + [VMEM(s, BF16) for s in shapes]
    scratch += landing_scratch(dims, shapes)
    return pl.pallas_call(
        partial(reduce_kernel, dims, count),
        name="reduce_gradients",
        out_shape=[jax.ShapeDtypeStruct(s[3:], F32) for s in shapes],
        in_specs=[pl.BlockSpec(memory_space=ANY)] * count,
        out_specs=[pl.BlockSpec(memory_space=VMEM)] * count,
        scratch_shapes=scratch,
        compiler_params=params(2),
    )(*parts)


def group_sums(row, spread):
    width = row.shape[1]
    return lax.dot_general(
        jnp.broadcast_to(row, (8, width)),
        spread,
        (((1,), (0,)), ((), ())),
        precision=HIGHEST,
        preferred_element_type=F32,
    )[0:1]


def group_spread(width, group):
    rows = lax.broadcasted_iota(I32, (width, width), 0) // group
    cols = lax.broadcasted_iota(I32, (width, width), 1) // group
    return (rows == cols).astype(F32)


def dot(a, b, contract):
    return lax.dot_general(a, b, ((contract[0], contract[1]), ((), ())), preferred_element_type=F32)


NN = ((1,), (0,))
NT = ((1,), (1,))
TN = ((0,), (0,))


class Map:
    def __init__(self, high, width, live, span, part, channels, group):
        self.high, self.width, self.live = high, width, live
        self.span, self.part, self.channels = span, part, channels
        self.pixels = float(high * live * group)

    def column(self, span):
        shape = (span, self.width, self.channels)
        return lax.broadcasted_iota(I32, shape, 1).reshape(span * self.width, self.channels)

    def masked(self, value, span):
        if self.live == self.width:
            return value
        return jnp.where(self.column(span) < self.live, value, 0.0)

    def at(self, i, span):
        return pl.ds(pl.multiple_of(i * span * self.width, 16), span * self.width)


def take(source, first, count, lanes=slice(None)):
    value = source[pl.ds(first, count), :, lanes]
    return value.reshape(-1, value.shape[2])


def conv_forward(m, source, weight, raw, first=0, last=None, total=None):
    n, tile = m.channels, m.span * m.width

    def body(i, total):
        wide = None
        for du in range(3):
            part = dot(take(source, i * m.span + du, m.span), weight(du), NN)
            wide = part if wide is None else wide + part
        left = pltpu.roll(wide[:, :n], 1, 0)
        right = pltpu.roll(wide[:, 2 * n :], tile - 1, 0)
        if m.live == m.width:
            column = m.column(m.span)
            left = jnp.where(column == 0, 0.0, left)
            right = jnp.where(column == m.width - 1, 0.0, right)
        value = m.masked(left + wide[:, n : 2 * n] + right, m.span)
        raw[m.at(i, m.span), :] = value
        return total + jnp.sum(value, axis=0, keepdims=True)

    last = m.high // m.span if last is None else last
    total = jnp.zeros((1, n), F32) if total is None else total
    return lax.fori_loop(first, last, body, total)


def norm_forward(m, raw, total, spread, gain, bias, store):
    n, part = m.channels, m.part
    mean = group_sums(total, spread) / m.pixels

    def spread_of(i, acc):
        away = m.masked(raw[m.at(i, part), :] - mean, part)
        return acc + jnp.sum(away * away, axis=0, keepdims=True)

    squares = lax.fori_loop(0, m.high // part, spread_of, jnp.zeros((1, n), F32))
    scale = lax.rsqrt(group_sums(squares, spread) / m.pixels + GN_EPS)

    def normalize(i, carry):
        normed = (raw[m.at(i, part), :] - mean) * scale
        raw[m.at(i, part), :] = normed
        value = m.masked(jnp.maximum(normed * gain + bias, 0.0), part)
        store(i, value.astype(BF16))
        return carry

    lax.fori_loop(0, m.high // part, normalize, 0)
    return scale


def norm_backward(m, normed, upstream, spare, shifted, spread, gain, bias, scale):
    n, part = m.channels, m.part
    tile = part * m.width

    def first(i, sums):
        here = normed[m.at(i, part), :]
        value = m.masked(jnp.where(here * gain + bias > 0.0, upstream(i), 0.0), part)
        spare[m.at(i, part), :] = value
        return (
            sums[0] + jnp.sum(value * here, axis=0, keepdims=True),
            sums[1] + jnp.sum(value, axis=0, keepdims=True),
        )

    zero = jnp.zeros((1, n), F32)
    gain_sum, bias_sum = lax.fori_loop(0, m.high // part, first, (zero, zero))
    level = group_sums(bias_sum * gain, spread) / m.pixels
    slope = group_sums(gain_sum * gain, spread) / m.pixels

    def second(i, carry):
        value = scale * (spare[m.at(i, part), :] * gain - level - normed[m.at(i, part), :] * slope)
        value = m.masked(value, part)
        left = pltpu.roll(value, tile - 1, 0)
        right = pltpu.roll(value, 1, 0)
        if m.live == m.width:
            column = m.column(part)
            left = jnp.where(column == m.width - 1, 0.0, left)
            right = jnp.where(column == 0, 0.0, right)
        into = pl.ds(i * part + 1, part)
        for k, piece in enumerate((left, value, right)):
            shifted[into, :, k * n : (k + 1) * n] = piece.astype(BF16).reshape(part, m.width, n)
        return carry

    lax.fori_loop(0, m.high // part, second, 0)
    return gain_sum, bias_sum


def weight_gradient(m, source, shifted, total, lanes):
    width = lanes.stop - lanes.start

    def body(i, carry):
        right = take(shifted, i * m.span + 1, m.span, lanes)
        for du in range(3):
            value = dot(take(source, i * m.span + du, m.span), right, TN)
            into = total.at[..., du * width : (du + 1) * width]
            value = value.reshape(into.shape)

            @pl.when(i == 0)
            def _(into=into, value=value):
                into[...] = value

            @pl.when(i > 0)
            def _(into=into, value=value):
                into[...] += value

        return carry

    lax.fori_loop(0, m.high // m.span, body, 0)


def zero_edges(ref):
    blank = jnp.zeros((1,) + ref.shape[1:], ref.dtype)
    ref[0:1] = blank
    ref[ref.shape[0] - 1 : ref.shape[0]] = blank


def diagonal(n):
    return lax.broadcasted_iota(I32, (n, n), 0) == lax.broadcasted_iota(I32, (n, n), 1)


def as_row(column):
    return jnp.sum(jnp.where(diagonal(column.shape[0]), column, 0.0), axis=0, keepdims=True)


def as_column(row):
    return jnp.sum(jnp.where(diagonal(row.shape[1]), row, 0.0), axis=1, keepdims=True)


def step_kernel(cfg, names, *refs):
    r = dict(zip(names, refs))
    dims, images, fused = cfg["dims"], cfg["images"], cfg["fused"]
    big, small = cfg["mask_map"], cfg["grid_map"]
    nm, ng, kc = big.channels, small.channels, cfg["kc"]
    grid, pad = small.live, small.width
    rows, grid_rows = big.high * big.width, small.high * small.width
    gtile = small.span * small.width
    pos = place(dims)
    model = lax.axis_index("mp")
    own_image = lax.axis_index("dp")

    def lanes_of(width, side):
        return pl.ds(pl.multiple_of(side * width, width), width)

    own_m, away_m = lanes_of(nm, model), lanes_of(nm, 1 - model)
    own_g, away_g = lanes_of(ng, model), lanes_of(ng, 1 - model)
    own_x = lanes_of(r["xm_own"].shape[3], model)
    map_rows, grid_span = pl.ds(1, big.high), pl.ds(1, small.high)
    spread_m = group_spread(nm, 2 * nm // GROUPS)
    spread_g = group_spread(ng, 2 * ng // GROUPS)

    xm, xg, hm, hg, dm = r["xm"], r["xg"], r["hm"], r["hg"], r["dm"]
    dg1, dg2 = r["dg1"], r["dg2"]
    mask_in, grid_in = r["xm_own"].at[0], r["xg_own"].at[0]
    mask_into = xm.at[map_rows, :, own_x]
    grid_into = xg.at[grid_span, pl.ds(0, grid), own_x]
    local = [
        pltpu.make_async_copy(mask_in, mask_into, r["local"].at[0]),
        pltpu.make_async_copy(grid_in, grid_into, r["local"].at[1]),
    ]
    for copy in local:
        copy.start()
    weights = [r["w%d" % i] for i in range(5)]
    groups = []
    if fused:
        for t in range(9):
            for i, value in (
                (0, r["mask_convs"][0, t]),
                (1, r["grid_first"][t]),
                (2, r["mask_convs"][1, t]),
                (3, r["grid_second"][t]),
            ):
                width = value.shape[1]
                weights[i][pos[0], pos[1], pos[2], :, t * width : (t + 1) * width] = value.astype(
                    BF16
                )
        class_in = r["class_conv"]
        for du in range(3):
            pieces = [class_in[3 * du + dv] for dv in range(3)]
            pieces.append(jnp.zeros((class_in.shape[1], 128 - 3 * kc), F32))
            weights[4][pos[0], pos[1], pos[2], :, du * 128 : (du + 1) * 128] = jnp.concatenate(
                pieces, axis=1
            ).astype(BF16)
        groups = gather_groups(dims, weights, r["gs"], r["gr"])

    def bring(*which):
        if fused:
            advance(*[exchange for i in which for exchange in groups[i]])

    greet(dims)
    feature_copies = [
        pair_copy(mask_in, mask_into, r["pair"].at[0]),
        pair_copy(grid_in, grid_into, r["pair"].at[1]),
    ]
    for copy in feature_copies:
        copy.start()
    bring(0)
    bring(1)

    for ref in (xm, xg, hm, hg, dm, dg1, dg2):
        zero_edges(ref)
    xg[:, grid:, :] = jnp.zeros((xg.shape[0], pad - grid, xg.shape[2]), BF16)
    share = jnp.float32(1.0 / images)
    table, bias_table = r["table"], r["bias_table"]
    slots = r["cells"].shape[1]
    table[...] = jnp.full(table.shape, -(1 << 20), I32)
    table[0:1, 0:slots] = r["cells"][...]
    table[1:2, 0:slots] = r["labels"][...]
    bias_table[...] = jnp.zeros(bias_table.shape, F32)
    bias_table[0:1, 0:kc] = r["class_bias"][...]
    cells = table[0:1, :].astype(F32)
    cells = cells + jnp.floor((cells + 0.5) / grid) * (pad - grid)
    cells_row = cells.astype(I32)
    cells_col = as_column(cells).astype(I32)
    labels_col = as_column(table[1:2, :].astype(F32)).astype(I32) - model * kc
    class_bias = bias_table[0:1, :]
    own_count = r["counts"][own_image]
    slot_lanes = lax.broadcasted_iota(I32, (1, SLOTS), 1)
    slot_rows = lax.broadcasted_iota(I32, (SLOTS, 1), 0)
    own_float = jnp.full((1, 1), own_count, I32).astype(F32)
    live_row = (slot_lanes < own_count).astype(F32)
    live_col = (slot_rows < own_count).astype(F32)
    weight_col = live_col * (share / own_float)
    dice_col = DICE_WEIGHT * weight_col
    focal_scale = share / (own_float + 1.0)
    bring(0)
    bring(0)
    bring(1)

    def weight(i, span):
        def part(du):
            value = weights[i][..., du * span : (du + 1) * span]
            return value.reshape(-1, span) if fused else value

        return part

    mask_one, grid_one, mask_two = weight(0, 3 * nm), weight(1, 3 * ng), weight(2, 3 * nm)
    grid_two, class_two = weight(3, 3 * nm), weight(4, 128)

    norms, gnorms = r["mask_norms"], r["grid_norms"]
    row = lambda ref, k: ref[k : k + 1, :]
    bring(2)
    for copy in local:
        copy.wait()
    feature_copies[0].wait()
    bring(0)
    xh1 = r["xh1"]
    half = big.high // big.span // 2
    total = conv_forward(big, xm, mask_one, xh1, 0, half)
    bring(1)
    total = conv_forward(big, xm, mask_one, xh1, half, None, total)
    bring(2)
    bring(3)

    def keep_mask(i, value):
        hm[pl.ds(i * big.part + 1, big.part), :, own_m] = value.reshape(big.part, big.width, nm)

    scale_one = norm_forward(big, xh1, total, spread_m, row(norms, 0), row(norms, 1), keep_mask)
    hm_copy = pair_copy(
        hm.at[map_rows, :, own_m], hm.at[map_rows, :, own_m], r["pair"].at[2]
    )
    hm_copy.start()
    bring(2)
    feature_copies[1].wait()
    bring(1)
    bring(3)
    bring(4)
    xhg = r["xhg"]
    total = conv_forward(small, xg, grid_one, xhg)
    bring(2)
    bring(3)
    bring(4)

    def keep_grid(i, value):
        hg[pl.ds(i * small.part + 1, small.part), :, own_g] = value.reshape(
            small.part, small.width, ng
        )

    scale_grid = norm_forward(
        small, xhg, total, spread_g, row(gnorms, 0), row(gnorms, 1), keep_grid
    )
    hg_copy = pair_copy(
        hg.at[grid_span, :, own_g], hg.at[grid_span, :, own_g], r["pair"].at[3]
    )
    hg_copy.start()

    hm_copy.wait()
    xh2, feature = r["xh2"], r["feature"]
    total = conv_forward(big, hm, mask_two, xh2)
    bring(3)
    bring(4)

    def keep_feature(i, value):
        feature[big.at(i, big.part), :] = value

    scale_two = norm_forward(
        big, xh2, total, spread_m, row(norms, 2), row(norms, 3), keep_feature
    )
    for group in groups:
        complete(*group)
        for exchange in group:
            exchange.drain()

    hg_copy.wait()
    patches = r["patches"]
    lane = lax.broadcasted_iota(I32, (SLOTS, grid_rows), 1)
    depth = hg.shape[2]
    picked = None
    for t in range(9):
        chosen = (lane == cells_col + ((t // 3 - 1) * pad + t % 3 - 1)).astype(F32).astype(BF16)
        part = dot(chosen, take(hg, 1, small.high), NN).astype(BF16)
        patches[:, t * depth : (t + 1) * depth] = part
        w = grid_two(t // 3)[:, (t % 3) * nm : (t % 3 + 1) * nm]
        part = dot(part, w, NN)
        picked = part if picked is None else picked + part
    kernels = r["kernels"]
    kernels[pos[0], pos[1], pos[2], model] = picked.astype(BF16)
    kernel_share = share_exchange(dims, kernels, r["ks"], r["kr"], True)
    advance(kernel_share)

    kernel_rows = kernels[pos[0], pos[1], pos[2], model]
    logits, logits_in = r["logits"], r["logits_in"]
    high_slots = logits.shape[0]
    tile = big.span * big.width
    for i in range(rows // tile):
        span = slice(i * tile, (i + 1) * tile)
        logits[:, span] = dot(kernel_rows[:high_slots], feature[span, :], NT).astype(BF16)
    logits_copy = pair_copy(logits, logits_in, r["pair"].at[4])
    logits_copy.start()
    advance(kernel_share)

    class_hot = (
        (lax.broadcasted_iota(I32, (SLOTS, 128), 1) == labels_col).astype(F32).astype(BF16)
    )

    def class_tile(i, sums):
        value = None
        for du in range(3):
            part = dot(take(hg, i * small.span + du, small.span), class_two(du), NN)
            value = part if value is None else value + part
        x = (
            pltpu.roll(value, 1, 0)
            + pltpu.roll(value, 128 - kc, 1)
            + pltpu.roll(pltpu.roll(value, 128 - 2 * kc, 1), gtile - 1, 0)
            + class_bias
        )
        at = lax.broadcasted_iota(I32, (gtile, SLOTS), 0) + i * gtile
        cell_hot = jnp.where(at == cells_row, live_row, 0.0).astype(BF16)
        t = dot(cell_hot, class_hot, NN)
        lanes = lax.broadcasted_iota(I32, (gtile, 128), 1)
        column = lax.broadcasted_iota(I32, (small.span, pad, 128), 1).reshape(gtile, 128)
        real = (column < grid) & (lanes < kc)
        tiny = jnp.exp(-jnp.abs(x))
        extra = jnp.log1p(tiny)
        inverse = 1.0 / (1.0 + tiny)
        q = jnp.where(x >= 0.0, 1.0, tiny) * inverse
        p = jnp.where(x >= 0.0, tiny, 1.0) * inverse
        log_q = -(jnp.maximum(-x, 0.0) + extra)
        log_p = -(jnp.maximum(x, 0.0) + extra)
        terms = FOCAL_ALPHA * t * p * p * log_q + (1.0 - FOCAL_ALPHA) * (1.0 - t) * q * q * log_p
        slope = FOCAL_ALPHA * t * p * p * (p - 2.0 * q * log_q) + (1.0 - FOCAL_ALPHA) * (
            1.0 - t
        ) * q * q * (2.0 * p * log_p - q)
        slope = jnp.where(real, -focal_scale * slope, 0.0).astype(BF16).astype(F32)
        shifted = (
            pltpu.roll(slope, gtile - 1, 0)
            + pltpu.roll(slope, kc, 1)
            + pltpu.roll(pltpu.roll(slope, 2 * kc, 1), 1, 0)
        )
        dg2[pl.ds(i * small.span + 1, small.span), :, 3 * nm :] = shifted.astype(BF16).reshape(
            small.span, pad, 128
        )
        return (
            sums[0] + jnp.sum(jnp.where(real, -focal_scale * terms, 0.0), axis=0, keepdims=True),
            sums[1] + jnp.sum(slope, axis=0, keepdims=True),
        )

    zero = jnp.zeros((1, 128), F32)
    focal_sum, class_bias_sum = lax.fori_loop(
        0, small.high // small.span, class_tile, (zero, zero)
    )
    advance(kernel_share)

    logits_copy.wait()
    masks = r["masks"].at[0]
    dice_sum = jnp.zeros((1, 1), F32)
    for start in range(0, slots, 16):
        span = slice(start, start + 16)
        x = logits[span, :].astype(F32) + logits_in[span, :].astype(F32)
        s = jax.nn.sigmoid(x)
        mask = masks[start : min(start + 16, slots), :].astype(F32)
        if mask.shape[0] < 16:
            mask = jnp.concatenate([mask, jnp.zeros((16 - mask.shape[0], rows), F32)], axis=0)
        inter = jnp.sum(s * mask, axis=1, keepdims=True)
        whole = jnp.sum(s * s, axis=1, keepdims=True) + jnp.sum(mask, axis=1, keepdims=True) + 1.0
        share_here = dice_col[span]
        dice_sum += jnp.sum(share_here * (1.0 - 2.0 * inter / whole), keepdims=True)
        a = -2.0 * share_here / whole
        b = 2.0 * share_here * inter / (whole * whole)
        logits[span, :] = ((a * mask + 2.0 * b * s) * s * (1.0 - s)).astype(BF16)
    complete(kernel_share)

    own_full = [kernels[pos[0], pos[1], pos[2], k] for k in range(2)]

    def key_block(d):
        index = split_index(dims, d)
        return [kernels[index[0], index[1], index[2], k] for k in range(2)]

    def squares_of(block):
        return sum(
            jnp.sum(jnp.square(part.astype(F32)), axis=1, keepdims=True) for part in block
        )

    own_scale = lax.rsqrt(squares_of(own_full) + 1e-06)
    same_slot = diagonal(SLOTS)

    def scores(d):
        block = key_block(d)
        raw = dot(own_full[0], block[0], NT) + dot(own_full[1], block[1], NT)
        key_scale = lax.rsqrt(as_row(squares_of(block)) + 1e-06)
        scale = own_scale * key_scale / CONTRAST_TEMP
        live = slot_lanes < r["counts"][d]
        allowed = live & jnp.logical_not(same_slot & (d == own_image))
        return block, raw, key_scale, scale, allowed

    def sum_keys(d, acc):
        _, raw, _, scale, allowed = scores(d)
        value = jnp.where(allowed, jnp.exp(raw * scale), 0.0)
        return acc + jnp.sum(value, axis=1, keepdims=True)

    totals_col = lax.fori_loop(0, images, sum_keys, jnp.zeros((SLOTS, 1), F32))
    log_col = jnp.log(totals_col)
    contrast_sum = jnp.sum(
        jnp.where(weight_col > 0.0, weight_col * log_col, 0.0), keepdims=True
    )
    logs = r["logs"]
    logs[pos[0], pos[1], pos[2]] = jnp.broadcast_to(as_row(log_col), (8, SLOTS))
    log_share = share_exchange(dims, logs, r["ls"], r["lr"], False)
    advance(log_share)

    totals = [r["g%d" % i] for i in range(5)]
    out_groups = []
    if fused:
        staged = [weights[2], weights[1], weights[0], weights[3], weights[4]]
        lands = [r["land%d" % i] for i in range(cfg["lands"])]
        out_groups = reduce_groups(dims, totals, staged, lands, r["rs"], r["rr"])

    def send(*which):
        if fused:
            advance(*[exchange for i in which for exchange in out_groups[i]])

    def send_first(i):
        if fused:
            cast_blocks(dims, totals[i], staged[i])
            send(i)

    logit_rows = dot(logits[...], feature[...], NN)
    advance(log_share)
    dlogits, part_rows = logits, big.part * big.width

    def from_logits(i):
        pixels = pl.ds(pl.multiple_of(i * part_rows, part_rows), part_rows)
        return dot(dlogits[:, pixels], kernel_rows[:high_slots], TN)

    gain_two, bias_two = norm_backward(
        big, xh2, from_logits, r["spare"], dm, spread_m, row(norms, 2), row(norms, 3), scale_two
    )
    advance(log_share)
    weight_gradient(big, hm, dm, totals[2], slice(0, 3 * nm))
    send_first(2)
    complete(log_share)
    hidden = hm

    def input_tile(i, carry):
        value = None
        for du in range(3):
            part = dot(take(dm, i * big.span + 2 - du, big.span), mask_two(du), NT)
            value = part if value is None else value + part
        hidden[pl.ds(i * big.span + 1, big.span)] = value.astype(BF16).reshape(
            big.span, big.width, 2 * nm
        )
        return carry

    lax.fori_loop(0, big.high // big.span, input_tile, 0)
    hidden_copy = pair_copy(hidden.at[map_rows, :, away_m], r["dhm_in"], r["pair"].at[5])
    hidden_copy.start()
    send(2)

    def row_terms(d, acc):
        block, raw, key_scale, scale, allowed = scores(d)
        index = split_index(dims, d)
        log_row = logs[index[0], index[1], index[2]][0:1]
        value = raw * scale
        query = jnp.where(allowed, jnp.exp(value - log_col) * weight_col, 0.0)
        key_count = jnp.full((1, 1), r["counts"][d], I32).astype(F32)
        keyed = allowed & (live_col > 0.5)
        key = jnp.where(keyed, jnp.exp(value - log_row) * (share / key_count), 0.0)
        query_low = (query * scale).astype(BF16)
        key_low = (key * scale).astype(BF16)
        mine = jnp.where(model == 0, block[0].astype(F32), block[1].astype(F32)).astype(BF16)
        return (
            acc[0] + dot(query_low, mine, NN) + dot(key_low, mine, NN),
            acc[1]
            + jnp.sum((query + key) * raw * key_scale / CONTRAST_TEMP, axis=1, keepdims=True),
        )

    row_sum, scale_sum = lax.fori_loop(
        0, images, row_terms, (jnp.zeros((SLOTS, nm), F32), jnp.zeros((SLOTS, 1), F32))
    )
    norm_grad = -0.5 * own_scale * own_scale * own_scale * scale_sum
    row_grad = row_sum + 2.0 * kernel_rows.astype(F32) * norm_grad
    row_grad = row_grad + jnp.concatenate(
        [logit_rows, jnp.zeros((SLOTS - high_slots, nm), F32)], axis=0
    )
    row_low = row_grad.astype(BF16)

    weight_gradient(small, hg, dg2, totals[4], slice(3 * nm, 3 * nm + 128))
    send(2)
    for i in range(small.high // small.span):
        at = lax.broadcasted_iota(I32, (gtile, SLOTS), 0) + i * gtile
        for dv in range(3):
            chosen = (at == cells_row + (dv - 1)).astype(F32).astype(BF16)
            dg2[1 + i * small.span : 1 + (i + 1) * small.span, :, dv * nm : (dv + 1) * nm] = (
                dot(chosen, row_low, NN).astype(BF16).reshape(small.span, pad, nm)
            )
    hidden_grid = hg

    def grid_input_tile(i, carry):
        value = None
        for du in range(3):
            first = i * small.span + 2 - du
            part = dot(take(dg2, first, small.span, slice(0, 3 * nm)), grid_two(du), NT) + dot(
                take(dg2, first, small.span, slice(3 * nm, 3 * nm + 128)), class_two(du), NT
            )
            value = part if value is None else value + part
        hidden_grid[pl.ds(i * small.span + 1, small.span)] = value.astype(BF16).reshape(
            small.span, pad, 2 * ng
        )
        return carry

    lax.fori_loop(0, small.high // small.span, grid_input_tile, 0)
    hidden_grid_copy = pair_copy(
        hidden_grid.at[grid_span, :, away_g], r["dhg_in"], r["pair"].at[6]
    )
    hidden_grid_copy.start()
    for t in range(9):
        value = dot(patches[:, t * depth : (t + 1) * depth], row_low, TN)
        into = totals[3].at[..., t * nm : (t + 1) * nm]
        into[...] = value.reshape(into.shape)
    send_first(3)
    send_first(4)
    send(2)

    hidden_grid_copy.wait()
    hidden_grid_in = r["dhg_in"]

    def both_grid_halves(i):
        mine = take(hidden_grid, i * small.part + 1, small.part, own_g)
        return mine.astype(F32) + take(hidden_grid_in, i * small.part, small.part).astype(F32)

    gain_grid, bias_grid = norm_backward(
        small, xhg, both_grid_halves, r["spare_g"], dg1, spread_g, row(gnorms, 0),
        row(gnorms, 1), scale_grid,
    )
    send(3, 4)
    weight_gradient(small, xg, dg1, totals[1], slice(0, 3 * ng))
    send_first(1)
    hidden_copy.wait()
    hidden_in = r["dhm_in"]

    def both_halves(i):
        mine = take(hidden, i * big.part + 1, big.part, own_m)
        return mine.astype(F32) + take(hidden_in, i * big.part, big.part).astype(F32)

    gain_one, bias_one = norm_backward(
        big, xh1, both_halves, r["spare"], dm, spread_m, row(norms, 0), row(norms, 1), scale_one
    )
    send(3, 4)
    send(1)
    weight_gradient(big, xm, dm, totals[0], slice(0, 3 * nm))
    send_first(0)

    smalls = r["smalls"]
    blank = jnp.zeros((1, 128), F32)
    pieces = [gain_one, bias_one, gain_two, bias_two]
    pieces += [gain_grid[:, i : i + nm] for i in range(0, ng, nm)]
    pieces += [bias_grid[:, i : i + nm] for i in range(0, ng, nm)]
    pieces += [class_bias_sum]
    pieces += [blank] * (16 - len(pieces))
    smalls[pos[0], pos[1], pos[2]] = jnp.concatenate(pieces, axis=0)
    small_share = share_exchange(dims, smalls, r["ss"], r["sr"], False)
    advance(small_share)
    send(3, 4)
    send(1)
    send(0)
    advance(small_share)

    squares = jnp.zeros((1, 1), F32)

    def hand_out(i):
        complete(*out_groups[i])
        value = totals[i][pos[0], pos[1], pos[2]]
        r["out%d" % i][...] = value
        return jnp.sum(value * value, keepdims=True)

    if fused:
        for i in (2, 3, 4):
            squares += hand_out(i)
        send(1)
        send(0)
        squares += hand_out(1)
    complete(small_share)

    def add_small(d, acc):
        index = split_index(dims, d)
        return acc + smalls[index[0], index[1], index[2]]

    small_sum = lax.fori_loop(0, images, add_small, jnp.zeros((16, 128), F32))
    r["small_out"][...] = small_sum
    first_model = (model == 0).astype(F32)
    loss = jnp.sum(focal_sum, keepdims=True) + first_model * (dice_sum + contrast_sum)
    if fused:
        squares += hand_out(0)
        first_device = (own_image == 0).astype(F32)
        squares += first_device * jnp.sum(small_sum * small_sum, keepdims=True)
        sums = r["sums"]
        at = lax.broadcasted_iota(I32, (8, 128), 0)
        sums[pos[0], pos[1], pos[2], model] = jnp.where(at == 0, squares, loss)
        sum_share = share_exchange(dims, sums, r["us"], r["ur"], True)
        complete(sum_share)

        def add_sums(d, acc):
            index = split_index(dims, d)
            return acc + sums[index[0], index[1], index[2], 0] + sums[
                index[0], index[1], index[2], 1
            ]

        r["sum_out"][...] = lax.fori_loop(0, images, add_sums, jnp.zeros((8, 128), F32))
        sum_share.drain()
    else:
        r["sum_out"][...] = jnp.broadcast_to(loss, (8, 128))
    for shared in (kernel_share, log_share, small_share):
        shared.drain()
    for group in out_groups:
        for exchange in group:
            exchange.drain()


def run_step(cfg, inputs, weights, blocks):
    dims, fused = cfg["dims"], cfg["fused"]
    big, small = cfg["mask_map"], cfg["grid_map"]
    nm, ng = big.channels, small.channels
    rows, grid_rows = big.high * big.width, small.high * small.width
    inputs = dict(inputs, **weights)
    spaces = dict(xm_own=ANY, xg_own=ANY, counts=pltpu.SMEM)
    names = list(inputs)
    specs = [pl.BlockSpec(memory_space=spaces.get(name, VMEM)) for name in names]
    outs = {"small_out": ((16, 128), F32), "sum_out": ((8, 128), F32)}
    scratch = {}
    if fused:
        for i, shape in enumerate(blocks):
            outs["out%d" % i] = (shape[3:], F32)
            scratch["w%d" % i] = VMEM(shape, BF16)
            scratch["g%d" % i] = VMEM(shape, F32)
        lands = landing_scratch(dims, blocks)
        cfg = dict(cfg, lands=len(lands))
        for i, land in enumerate(lands):
            scratch["land%d" % i] = land
        slots = flow_slots(dims, blocks)
        for name in ("gs", "gr", "rs", "rr"):
            scratch[name] = DMA((slots,))
        scratch["sums"] = VMEM(dims + (2, 8, 128), F32)
        scratch["us"], scratch["ur"] = share_sems(dims)
    else:
        for i in range(5):
            outs["g%d" % i] = (inputs["w%d" % i].shape, F32)
    c_in = 2 * inputs["xm_own"].shape[3]
    depth = 2 * ng
    slot_rows = -(-inputs["masks"].shape[1] // 16) * 16

    def padded(m, channels):
        return VMEM((m.high + 2, m.width, channels), BF16)

    scratch.update(
        xm=padded(big, c_in),
        xg=padded(small, c_in),
        xh1=VMEM((rows, nm), F32),
        hm=padded(big, 2 * nm),
        xhg=VMEM((grid_rows, ng), F32),
        hg=padded(small, depth),
        xh2=VMEM((rows, nm), F32),
        feature=VMEM((rows, nm), BF16),
        patches=VMEM((SLOTS, 9 * depth), BF16),
        kernels=VMEM(dims + (2, SLOTS, nm), BF16),
        logits=VMEM((slot_rows, rows), BF16),
        logits_in=VMEM((slot_rows, rows), BF16),
        logs=VMEM(dims + (8, SLOTS), F32),
        dm=padded(big, 3 * nm),
        spare=VMEM((rows, nm), F32),
        dhm_in=VMEM((big.high, big.width, nm), BF16),
        dg2=padded(small, 3 * nm + 128),
        dhg_in=VMEM((small.high, small.width, ng), BF16),
        dg1=padded(small, 3 * ng),
        spare_g=VMEM((grid_rows, ng), F32),
        smalls=VMEM(dims + (16, 128), F32),
        table=VMEM((8, SLOTS), I32),
        bias_table=VMEM((8, 128), F32),
        local=DMA((2,)),
        pair=DMA((7, 2)),
    )
    for a, b in (("ks", "kr"), ("ls", "lr"), ("ss", "sr")):
        scratch[a], scratch[b] = share_sems(dims)
    names += list(outs) + list(scratch)
    result = pl.pallas_call(
        partial(step_kernel, cfg, tuple(names)),
        name="step",
        out_shape=[jax.ShapeDtypeStruct(s, d) for s, d in outs.values()],
        in_specs=specs,
        out_specs=[pl.BlockSpec(memory_space=VMEM)] * len(outs),
        scratch_shapes=list(scratch.values()),
        compiler_params=params(0),
    )(*inputs.values())
    return dict(zip(outs, result))


def update_kernel(nm, ng, kc, *refs):
    reduced, small, sums = refs[:5], refs[5], refs[6]
    states, outs = refs[7:28], refs[28:]
    total = sums[0:1, 0:1]
    norm = jnp.sqrt(total)
    outs[0][...] = sums[1:2, 0:1]
    outs[1][...] = norm
    factor = jnp.minimum(1.0, CLIP_LIMIT / norm)

    def update(which, index, gradient, rate):
        old = [states[3 * which + k][index] for k in range(3)]
        new = adam_update(*old, gradient * factor, rate)
        for k in range(3):
            outs[2 + 3 * which + k][index] = new[k]

    for t in range(9):
        update(0, (0, t), reduced[0][:, t * nm : (t + 1) * nm], LEARN_RATE)
        update(0, (1, t), reduced[2][:, t * nm : (t + 1) * nm], LEARN_RATE)
        update(1, (t,), reduced[1][:, t * ng : (t + 1) * ng], LEARN_RATE)
        update(2, (t,), reduced[3][:, t * nm : (t + 1) * nm], LEARN_RATE)
        at = t // 3 * 128 + t % 3 * kc
        update(3, (t,), reduced[4][:, at : at + kc], LEARN_RATE)
    update(4, (slice(None),), small[0:4, :], SMALL_RATE)
    per = ng // nm
    for k in range(2):
        pieces = [small[4 + k * per + i : 5 + k * per + i, :] for i in range(per)]
        update(5, (slice(k, k + 1),), jnp.concatenate(pieces, axis=1), SMALL_RATE)
    at = 4 + 2 * per
    update(6, (slice(None),), small[at : at + 1, :kc], SMALL_RATE)


def run_update(nm, ng, kc, reduced, small, sums, states):
    args = list(reduced) + [small, sums] + list(states)
    shapes = [jax.ShapeDtypeStruct((1, 1), F32)] * 2
    shapes += [jax.ShapeDtypeStruct(s.shape, F32) for s in states]
    return pl.pallas_call(
        partial(update_kernel, nm, ng, kc),
        name="update",
        out_shape=shapes,
        in_specs=[pl.BlockSpec(memory_space=VMEM)] * len(args),
        out_specs=[pl.BlockSpec(memory_space=VMEM)] * len(shapes),
        compiler_params=pltpu.CompilerParams(vmem_limit_bytes=VMEM_LIMIT),
    )(*args)


def lanes_of_taps(weight):
    taps, depth, width = weight.shape
    return weight.transpose(1, 0, 2).reshape(depth, taps * width)


def class_lanes(weight):
    _, depth, width = weight.shape
    rows = weight.transpose(1, 0, 2).reshape(depth, 3, 3 * width)
    return jnp.pad(rows, ((0, 0), (0, 0), (0, 128 - 3 * width))).reshape(depth, 384)


def adam_update(weight, moment, square, gradient, rate):
    moment_new = BETA_ONE * moment + (1.0 - BETA_ONE) * gradient
    square_new = BETA_TWO * square + (1.0 - BETA_TWO) * gradient * gradient
    moment_hat = moment_new / (1.0 - BETA_ONE**STEP_TIME)
    square_hat = square_new / (1.0 - BETA_TWO**STEP_TIME)
    weight_new = weight - rate * (
        moment_hat / (jnp.sqrt(square_hat) + ADAM_EPS) + WEIGHT_DECAY * weight
    )
    return (weight_new, moment_new, square_new)


def body(
    mask_features,
    grid_features,
    instance_cells,
    instance_counts,
    instance_labels,
    instance_masks,
    *states,
):
    images = lax.axis_size("dp")
    data_index = lax.axis_index("dp")
    dims = line_lengths(images)
    mask_convs, grid_first, grid_second, class_conv = states[0:12:3]
    mask_norms, grid_norms, class_bias = states[12::3]
    _, high, wide, half = mask_features.shape
    grid = grid_features.shape[1]
    pad = -(-(grid + 1) // 16) * 16
    nm, ng, kc = mask_convs.shape[3], grid_first.shape[2], class_conv.shape[2]
    fused = grid_first.shape[1] % 16 == 0
    cfg = dict(
        dims=dims,
        images=images,
        mask_map=Map(high, wide, wide, 8, 4, nm, 2 * nm // GROUPS),
        grid_map=Map(grid, pad, grid, grid // 2, grid // 2, ng, 2 * ng // GROUPS),
        kc=kc,
        fused=fused,
    )
    inputs = dict(
        xm_own=mask_features,
        xg_own=grid_features,
        masks=instance_masks,
        counts=instance_counts,
        cells=instance_cells,
        labels=instance_labels,
        mask_norms=mask_norms,
        grid_norms=grid_norms,
        class_bias=class_bias[None, :],
    )
    if fused:
        weights = dict(
            mask_convs=mask_convs,
            grid_first=grid_first,
            grid_second=grid_second,
            class_conv=class_conv,
        )
        blocks = [
            dims + (mask_convs.shape[2], 9 * nm),
            dims + (grid_first.shape[1], 9 * ng),
            dims + (mask_convs.shape[2], 9 * nm),
            dims + (grid_second.shape[1], 9 * nm),
            dims + (class_conv.shape[1], 384),
        ]
        out = run_step(cfg, inputs, weights, blocks)
        reduced = [out["out%d" % i] for i in range(5)]
        sums = out["sum_out"]
    else:
        shards = [
            lanes_of_taps(mask_convs[0].astype(BF16)),
            lanes_of_taps(grid_first.astype(BF16)),
            lanes_of_taps(mask_convs[1].astype(BF16)),
            lanes_of_taps(grid_second.astype(BF16)),
            class_lanes(class_conv.astype(BF16)),
        ]
        gathered = gather_all(dims, shards)
        weights = {"w%d" % i: b.reshape(-1, b.shape[-1]) for i, b in enumerate(gathered)}
        out = run_step(cfg, inputs, weights, None)
        reduced = reduce_all(
            dims, [out["g%d" % i].reshape(b.shape) for i, b in enumerate(gathered)]
        )
        squares = sum(jnp.sum(jnp.square(value)) for value in reduced)
        squares += (data_index == 0).astype(F32) * jnp.sum(jnp.square(out["small_out"]))
        pair = lax.psum((squares, out["sum_out"][0, 0]), ("dp", "mp"))
        sums = jnp.broadcast_to(jnp.pad(jnp.stack(pair), (0, 6))[:, None], (8, 128))
    states = states[:18] + tuple(state[None, :] for state in states[18:])
    result = run_update(nm, ng, kc, reduced, out["small_out"], sums, states)
    result = [value.reshape(()) for value in result[:2]] + list(result[2:])
    return tuple(result[:20]) + tuple(value[0] for value in result[20:])


def solution(mesh):
    in_specs = (
        P("dp", None, None, "mp"),
        P("dp", None, None, "mp"),
        P("dp", None),
        P(),
        P("dp", None),
        P("dp", None, None),
        P(None, None, "dp", "mp"),
        P(None, None, "dp", "mp"),
        P(None, None, "dp", "mp"),
        P(None, "dp", "mp"),
        P(None, "dp", "mp"),
        P(None, "dp", "mp"),
        P(None, "dp", "mp"),
        P(None, "dp", "mp"),
        P(None, "dp", "mp"),
        P(None, "dp", "mp"),
        P(None, "dp", "mp"),
        P(None, "dp", "mp"),
        P(None, "mp"),
        P(None, "mp"),
        P(None, "mp"),
        P(None, "mp"),
        P(None, "mp"),
        P(None, "mp"),
        P("mp"),
        P("mp"),
        P("mp"),
    )
    out_specs = (
        P(),
        P(),
        P(None, None, "dp", "mp"),
        P(None, None, "dp", "mp"),
        P(None, None, "dp", "mp"),
        P(None, "dp", "mp"),
        P(None, "dp", "mp"),
        P(None, "dp", "mp"),
        P(None, "dp", "mp"),
        P(None, "dp", "mp"),
        P(None, "dp", "mp"),
        P(None, "dp", "mp"),
        P(None, "dp", "mp"),
        P(None, "dp", "mp"),
        P(None, "mp"),
        P(None, "mp"),
        P(None, "mp"),
        P(None, "mp"),
        P(None, "mp"),
        P(None, "mp"),
        P("mp"),
        P("mp"),
        P("mp"),
    )
    return jax.shard_map(body, mesh=mesh, in_specs=in_specs, out_specs=out_specs, check_vma=False)
```

time: 236 us -> 175 us (0.74)
  Pallas kernels: 198 us -> 170 us
  other arithmetic: 19.2 us -> 0 us
  local copies, waits for them, and re-layouts: 14.6 us -> 3.8 us
  between operations: 3.45 us -> 0.82 us
    pallas_call x1, Pallas kernels: 198 us -> 167 us  [run_step(): pl.pallas_call(partial(step_kernel, cfg, tuple(names)), name='step', out_...]
    sub x8 -> x0, other arithmetic: 9.19 us -> none  [the longest x7 8.38 us: adam_update(): weight - rate * (moment_hat / (jnp.sqrt(square_hat) + ADAM_EPS) + WEIGHT_...]
    pallas_call x0 -> x1, Pallas kernels: none -> 3.35 us  [run_update(): pl.pallas_call(partial(update_kernel, nm, ng, kc), name='update', out_sha...]
    another operation x5 -> x0, local copies, waits for them, and re-layouts: 2.63 us -> none  [the longest x2 1.78 us: body(): jnp.stack([taps_of_lanes(reduced[0], nm), taps_of_lanes(reduced[2], nm)])]
    mul x4 -> x0, other arithmetic: 2.41 us -> none  [the longest x1 0.99 us: body(): first_sum_w * factor]
where the time goes in v3:
time: 175 us
  Pallas kernels  170 us (97%)
  local copies, waits for them, and re-layouts  3.8 us (2%)
    pallas_call x1, Pallas kernels, run_step(): pl.pallas_call(partial(step_kernel, cfg, tuple(names)), name='step', out_...  167 us
    unnamed x1, local copies, waits for them, and re-layouts  3.8 us

profile of v3, /device:TPU:0, one launch (start us, length us, event | category | flops | bytes accessed | tf_op | source)
XLA Modules:
  0.0 174.8 jit_solution(12972878139141965518)
XLA Ops:
  0.7 3.8 %copy.50.refs_2_ = s32[1,100,4096]{2,1,0:T(8,128)} copy(s32[1,100,4096]{2,0,1:T(1,128)} %param.32) | data formatting | bytes 3276800 | tf_op args[5]
  4.5 166.9 %step.1 = (f32[16,128]{1,0:T(8,128)}, f32[8,128]{1,0:T(8,128)}, f32[16,1152]{1,0:T(8,128)}, f32[16,2304]{1,0:T(8,128)}, f32[16,1152]{1,0:T(8,128)}, /*index=5*/f32[32,1152]{1,0:T(8,128)}, f32[32,384]{1,0:T(8,128)}) custom-call(bf16[1,32,128,128]{3,2,1,0:T(8,128)(2,1)} %refs_0_.1, bf16[1,40,40,128]{3,2,1,0:T(8,128)(2,1)} %refs_1_.1, ...), custom_call_target="tpu_custom_call" | custom-call | tf_op jit(solution)/shard_map/step/pallas_call | solution.py:1183
  171.3 3.3 %update.1 = (f32[1,1]{1,0:T(1,128)}, f32[1,1]{1,0:T(1,128)}, f32[2,9,16,128]{3,2,1,0:T(8,128)}, f32[2,9,16,128]{3,2,1,0:T(8,128)}, f32[2,9,16,128]{3,2,1,0:T(8,1...) custom-call(f32[16,1152]{1,0:T(8,128)} %get-tuple-element.53.refs_0_, ...), custom_call_target="tpu_custom_call" | custom-call | tf_op jit(solution)/shard_map/update/pallas_call | solution.py:1230

commit v4 on v3

--- a/solution.py
+++ b/solution.py
@@ -69,18 +69,31 @@
     return along(dims, axis, other - pos[axis])
 
 
+def plane_peers(dims, cores):
+    pos = place(dims)
+    model = lax.axis_index("mp")
+    peers = []
+    for y in range(dims[1]):
+        for x in range(dims[2]):
+            for core in range(2 if cores else 1):
+                if y == x == core == 0:
+                    continue
+                at = (pos[0] * dims[1] + lax.rem(pos[1] + y, dims[1])) * dims[2]
+                peer = {"dp": at + lax.rem(pos[2] + x, dims[2])}
+                if core:
+                    peer["mp"] = 1 - model
+                peers.append(peer)
+    return peers
+
+
 def greet(dims):
     sem = pltpu.get_barrier_semaphore()
     pos = place(dims)
-    count = 1
-    for axis in range(3):
-        for offset in range(1, dims[axis]):
-            pl.semaphore_signal(
-                sem, inc=1, device_id=ring_step(dims, pos, axis, offset), device_id_type=MESH
-            )
-            count += 1
-    pl.semaphore_signal(sem, inc=1, device_id=partner(), device_id_type=MESH)
-    pl.semaphore_wait(sem, count)
+    peers = plane_peers(dims, True)
+    peers += [ring_step(dims, pos, 0, offset) for offset in range(1, dims[0])]
+    for peer in peers:
+        pl.semaphore_signal(sem, inc=1, device_id=peer, device_id_type=MESH)
+    pl.semaphore_wait(sem, len(peers))
 
 
 GATHER_ORDERS = ((2, 1, 0), (0, 2, 1), (0, 1, 2))
@@ -103,6 +116,14 @@
         cuts.append((order, start * 128, size * 128))
         start += size
     return tuple(cuts)
+
+
+def tap_row_cuts(width):
+    third = width // 3
+    if third % 384:
+        return lane_cuts(width)
+    near = third // 384 * 128
+    return ((2, 0, third), (1, third, third), (1, 2 * third, near), (2, 2 * third + near, 2 * near))
 
 
 class Exchange:
@@ -169,26 +190,50 @@
     return result
 
 
-def share_exchange(dims, out, send_sems, recv_sems, core):
-    model = lax.axis_index("mp")
-    result = gather_exchange(
-        dims, out, send_sems, recv_sems, 0, None, (2, 1, 0), (model,) if core else ()
-    )
-    if core:
-        view = out.at[:, :, :, model]
-        result.stages.append(
-            [
-                pltpu.make_async_remote_copy(
-                    src_ref=view,
-                    dst_ref=view,
-                    send_sem=send_sems.at[line_copies(dims)],
-                    recv_sem=recv_sems.at[line_copies(dims)],
-                    device_id=partner(),
-                    device_id_type=MESH,
-                )
-            ]
+def remote(view, send_sem, recv_sem, device):
+    return pltpu.make_async_remote_copy(
+        src_ref=view,
+        dst_ref=view,
+        send_sem=send_sem,
+        recv_sem=recv_sem,
+        device_id=device,
+        device_id_type=MESH,
+    )
+
+
+def core_exchange(out, sems):
+    result = Exchange()
+    view = out.at[:, :, :, lax.axis_index("mp")]
+    result.stages.append([remote(view, sems.at[0], sems.at[1], partner())])
+    result.lands.append(nothing)
+    return result
+
+
+def plane_slots(dims):
+    return 2 * dims[1] * dims[2] + dims[0]
+
+
+def plane_sems(dims):
+    return [DMA((plane_slots(dims),)), DMA((plane_slots(dims),))]
+
+
+def plane_exchange(dims, view, line_view, cores, land, send_sems, recv_sems):
+    result, pos = Exchange(), place(dims)
+    first = [
+        remote(view, send_sems.at[i], recv_sems.at[i], peer)
+        for i, peer in enumerate(plane_peers(dims, cores))
+    ]
+    base = len(first)
+    second = [
+        remote(
+            line_view,
+            send_sems.at[base + offset - 1],
+            recv_sems.at[base + offset - 1],
+            ring_step(dims, pos, 0, offset),
         )
-        result.lands.append(nothing)
+        for offset in range(1, dims[0])
+    ]
+    result.stages, result.lands = [first, second], [land, nothing]
     return result
 
 
@@ -268,8 +313,8 @@
     return result
 
 
-def share_sems(dims):
-    return [DMA((line_copies(dims) + 1,)), DMA((line_copies(dims) + 1,))]
+def share_sems(dims, pieces):
+    return [DMA((pieces * line_copies(dims),)), DMA((pieces * line_copies(dims),))]
 
 
 def pair_copy(source, target, sems):
@@ -304,11 +349,11 @@
     return groups
 
 
-def reduce_groups(dims, totals, staged, lands, send_sems, recv_sems):
+def reduce_groups(dims, totals, staged, lands, send_sems, recv_sems, cuts):
     groups, base, lands = [], 0, list(lands)
-    for total, stage in zip(totals, staged):
+    for total, stage, cut in zip(totals, staged, cuts):
         group = []
-        for order, start, size in lane_cuts(total.shape[4]):
+        for order, start, size in cut:
             group.append(
                 reduce_exchange(
                     dims,
@@ -328,22 +373,22 @@
     return groups
 
 
-def flow_slots(dims, shapes):
-    return max(1, line_copies(dims) * sum(len(lane_cuts(s[-1])) for s in shapes))
-
-
-def landing_scratch(dims, shapes):
+def flow_slots(dims, cuts):
+    return max(1, line_copies(dims) * sum(len(cut) for cut in cuts))
+
+
+def landing_scratch(dims, shapes, cuts):
     scratch = []
-    for shape in shapes:
-        for order, _, size in lane_cuts(shape[-1]):
+    for shape, cut in zip(shapes, cuts):
+        for order, _, size in cut:
             for land in landing_shapes(dims, shape[-2], size, REDUCE_ORDERS[order]):
                 scratch.append(VMEM(land, BF16))
     return scratch
 
 
-def cast_blocks(dims, total, staged):
+def cast_blocks(dims, total, staged, lanes=slice(None)):
     def cast(j, carry):
-        index = split_index(dims, j)
+        index = split_index(dims, j) + (slice(None), lanes)
         staged[index] = total[index].astype(BF16)
         return carry
 
@@ -376,7 +421,7 @@
 def gather_all(dims, shards):
     count = len(shards)
     shapes = [dims + s.shape for s in shards]
-    slots = flow_slots(dims, shapes)
+    slots = flow_slots(dims, [lane_cuts(s[-1]) for s in shapes])
     return pl.pallas_call(
         partial(gather_kernel, dims, count),
         name="gather_weights",
@@ -401,7 +446,8 @@
     for i in range(count):
         local[i].wait()
         cast_blocks(dims, totals[i], staged[i])
-    run_all(reduce_groups(dims, totals, staged, lands, send_sems, recv_sems))
+    cuts = [lane_cuts(total.shape[4]) for total in totals]
+    run_all(reduce_groups(dims, totals, staged, lands, send_sems, recv_sems, cuts))
     for i in range(count):
         outs[i][...] = totals[i][pos[0], pos[1], pos[2]]
 
@@ -409,10 +455,11 @@
 def reduce_all(dims, parts):
     count = len(parts)
     shapes = [p.shape for p in parts]
-    slots = flow_slots(dims, shapes)
+    cuts = [lane_cuts(s[-1]) for s in shapes]
+    slots = flow_slots(dims, cuts)
     scratch = [DMA((slots,)), DMA((slots,)), DMA((count,))]
     scratch += [VMEM(s, F32) for s in shapes] + [VMEM(s, BF16) for s in shapes]
-    scratch += landing_scratch(dims, shapes)
+    scratch += landing_scratch(dims, shapes, cuts)
     return pl.pallas_call(
         partial(reduce_kernel, dims, count),
         name="reduce_gradients",
@@ -555,27 +602,14 @@
     return gain_sum, bias_sum
 
 
-def weight_gradient(m, source, shifted, total, lanes):
+def weight_gradient(m, source, shifted, total, lanes, each=None):
     width = lanes.stop - lanes.start
-
-    def body(i, carry):
-        right = take(shifted, i * m.span + 1, m.span, lanes)
-        for du in range(3):
-            value = dot(take(source, i * m.span + du, m.span), right, TN)
-            into = total.at[..., du * width : (du + 1) * width]
-            value = value.reshape(into.shape)
-
-            @pl.when(i == 0)
-            def _(into=into, value=value):
-                into[...] = value
-
-            @pl.when(i > 0)
-            def _(into=into, value=value):
-                into[...] += value
-
-        return carry
-
-    lax.fori_loop(0, m.high // m.span, body, 0)
+    for du in range(3):
+        value = dot(take(source, du, m.high), take(shifted, 1, m.high, lanes), TN)
+        into = total.at[..., du * width : (du + 1) * width]
+        into[...] = value.reshape(into.shape)
+        if each is not None:
+            each(du)
 
 
 def zero_edges(ref):
@@ -627,8 +661,11 @@
         pltpu.make_async_copy(mask_in, mask_into, r["local"].at[0]),
         pltpu.make_async_copy(grid_in, grid_into, r["local"].at[1]),
     ]
+    masks = r["mask_bits"]
+    mask_copy = pltpu.make_async_copy(r["masks"].at[:, 0, :], masks, r["local"].at[2])
     for copy in local:
         copy.start()
+    mask_copy.start()
     weights = [r["w%d" % i] for i in range(5)]
     groups = []
     if fused:
@@ -714,11 +751,10 @@
     feature_copies[0].wait()
     bring(0)
     xh1 = r["xh1"]
-    half = big.high // big.span // 2
-    total = conv_forward(big, xm, mask_one, xh1, 0, half)
+    total = conv_forward(big, xm, mask_one, xh1)
     bring(1)
-    total = conv_forward(big, xm, mask_one, xh1, half, None, total)
     bring(2)
+    bring(4)
     bring(3)
 
     def keep_mask(i, value):
@@ -729,16 +765,14 @@
         hm.at[map_rows, :, own_m], hm.at[map_rows, :, own_m], r["pair"].at[2]
     )
     hm_copy.start()
-    bring(2)
     feature_copies[1].wait()
     bring(1)
+    xhg = r["xhg"]
+    total = conv_forward(small, xg, grid_one, xhg, 0, 1)
+    bring(2)
+    bring(4)
     bring(3)
-    bring(4)
-    xhg = r["xhg"]
-    total = conv_forward(small, xg, grid_one, xhg)
-    bring(2)
-    bring(3)
-    bring(4)
+    total = conv_forward(small, xg, grid_one, xhg, 1, None, total)
 
     def keep_grid(i, value):
         hg[pl.ds(i * small.part + 1, small.part), :, own_g] = value.reshape(
@@ -754,10 +788,13 @@
     hg_copy.start()
 
     hm_copy.wait()
+    bring(2)
     xh2, feature = r["xh2"], r["feature"]
-    total = conv_forward(big, hm, mask_two, xh2)
+    half = big.high // big.span // 2
+    total = conv_forward(big, hm, mask_two, xh2, 0, half)
+    bring(4)
     bring(3)
-    bring(4)
+    total = conv_forward(big, hm, mask_two, xh2, half, None, total)
 
     def keep_feature(i, value):
         feature[big.at(i, big.part), :] = value
@@ -765,38 +802,18 @@
     scale_two = norm_forward(
         big, xh2, total, spread_m, row(norms, 2), row(norms, 3), keep_feature
     )
-    for group in groups:
-        complete(*group)
-        for exchange in group:
-            exchange.drain()
 
     hg_copy.wait()
     patches = r["patches"]
     lane = lax.broadcasted_iota(I32, (SLOTS, grid_rows), 1)
     depth = hg.shape[2]
-    picked = None
     for t in range(9):
         chosen = (lane == cells_col + ((t // 3 - 1) * pad + t % 3 - 1)).astype(F32).astype(BF16)
-        part = dot(chosen, take(hg, 1, small.high), NN).astype(BF16)
-        patches[:, t * depth : (t + 1) * depth] = part
-        w = grid_two(t // 3)[:, (t % 3) * nm : (t % 3 + 1) * nm]
-        part = dot(part, w, NN)
-        picked = part if picked is None else picked + part
-    kernels = r["kernels"]
-    kernels[pos[0], pos[1], pos[2], model] = picked.astype(BF16)
-    kernel_share = share_exchange(dims, kernels, r["ks"], r["kr"], True)
-    advance(kernel_share)
-
-    kernel_rows = kernels[pos[0], pos[1], pos[2], model]
-    logits, logits_in = r["logits"], r["logits_in"]
-    high_slots = logits.shape[0]
-    tile = big.span * big.width
-    for i in range(rows // tile):
-        span = slice(i * tile, (i + 1) * tile)
-        logits[:, span] = dot(kernel_rows[:high_slots], feature[span, :], NT).astype(BF16)
-    logits_copy = pair_copy(logits, logits_in, r["pair"].at[4])
-    logits_copy.start()
-    advance(kernel_share)
+        patches[:, t * depth : (t + 1) * depth] = dot(
+            chosen, take(hg, 1, small.high), NN
+        ).astype(BF16)
+    if fused:
+        complete(*groups[4])
 
     class_hot = (
         (lax.broadcasted_iota(I32, (SLOTS, 128), 1) == labels_col).astype(F32).astype(BF16)
@@ -848,10 +865,47 @@
     focal_sum, class_bias_sum = lax.fori_loop(
         0, small.high // small.span, class_tile, (zero, zero)
     )
-    advance(kernel_share)
+
+    for group in groups:
+        complete(*group)
+        for exchange in group:
+            exchange.drain()
+    picked = None
+    for t in range(9):
+        w = grid_two(t // 3)[:, (t % 3) * nm : (t % 3 + 1) * nm]
+        part = dot(patches[:, t * depth : (t + 1) * depth], w, NN)
+        picked = part if picked is None else picked + part
+    kernels = r["kernels"]
+    kept = (slots + 15) // 16 * 16
+    if kept < SLOTS:
+        kernels[..., kept:, :] = jnp.zeros(dims + (2, SLOTS - kept, nm), BF16)
+    kernels[pos[0], pos[1], pos[2], model, 0:kept] = picked[0:kept].astype(BF16)
+    upper = kept // 32 * 16
+    kernel_share = [
+        gather_exchange(
+            dims, kernels, r["ks"], r["kr"], i * line_copies(dims), None, order,
+            (model, pl.ds(start, size)),
+        )
+        for i, (order, start, size) in enumerate(
+            ((GATHER_ORDERS[1], 0, upper), (GATHER_ORDERS[2], upper, kept - upper))
+        )
+    ]
+    kernel_cores = core_exchange(kernels, r["pair"].at[7])
+    advance(*kernel_share)
+
+    kernel_rows = kernels[pos[0], pos[1], pos[2], model]
+    logits, logits_in = r["logits"], r["logits_in"]
+    high_slots = logits.shape[0]
+    tile = big.span * big.width
+    for i in range(rows // tile):
+        span = slice(i * tile, (i + 1) * tile)
+        logits[:, span] = dot(kernel_rows[:high_slots], feature[span, :], NT).astype(BF16)
+    logits_copy = pair_copy(logits, logits_in, r["pair"].at[4])
+    logits_copy.start()
+    advance(*kernel_share)
 
     logits_copy.wait()
-    masks = r["masks"].at[0]
+    mask_copy.wait()
     dice_sum = jnp.zeros((1, 1), F32)
     for start in range(0, slots, 16):
         span = slice(start, start + 16)
@@ -867,9 +921,9 @@
         a = -2.0 * share_here / whole
         b = 2.0 * share_here * inter / (whole * whole)
         logits[span, :] = ((a * mask + 2.0 * b * s) * s * (1.0 - s)).astype(BF16)
-    complete(kernel_share)
-
-    own_full = [kernels[pos[0], pos[1], pos[2], k] for k in range(2)]
+    advance(*kernel_share)
+
+    several = 4 if images % 4 == 0 else 1
 
     def key_block(d):
         index = split_index(dims, d)
@@ -880,10 +934,9 @@
             jnp.sum(jnp.square(part.astype(F32)), axis=1, keepdims=True) for part in block
         )
 
-    own_scale = lax.rsqrt(squares_of(own_full) + 1e-06)
     same_slot = diagonal(SLOTS)
 
-    def scores(d):
+    def scores(d, own_scale):
         block = key_block(d)
         raw = dot(own_full[0], block[0], NT) + dot(own_full[1], block[1], NT)
         key_scale = lax.rsqrt(as_row(squares_of(block)) + 1e-06)
@@ -892,27 +945,15 @@
         allowed = live & jnp.logical_not(same_slot & (d == own_image))
         return block, raw, key_scale, scale, allowed
 
-    def sum_keys(d, acc):
-        _, raw, _, scale, allowed = scores(d)
-        value = jnp.where(allowed, jnp.exp(raw * scale), 0.0)
-        return acc + jnp.sum(value, axis=1, keepdims=True)
-
-    totals_col = lax.fori_loop(0, images, sum_keys, jnp.zeros((SLOTS, 1), F32))
-    log_col = jnp.log(totals_col)
-    contrast_sum = jnp.sum(
-        jnp.where(weight_col > 0.0, weight_col * log_col, 0.0), keepdims=True
-    )
-    logs = r["logs"]
-    logs[pos[0], pos[1], pos[2]] = jnp.broadcast_to(as_row(log_col), (8, SLOTS))
-    log_share = share_exchange(dims, logs, r["ls"], r["lr"], False)
-    advance(log_share)
+    def own_key_scale():
+        return lax.rsqrt(squares_of(own_full) + 1e-06)
 
     totals = [r["g%d" % i] for i in range(5)]
     out_groups = []
     if fused:
-        staged = [weights[2], weights[1], weights[0], weights[3], weights[4]]
+        staged = [weights[2], weights[1], weights[0], weights[3], r["class_stage"]]
         lands = [r["land%d" % i] for i in range(cfg["lands"])]
-        out_groups = reduce_groups(dims, totals, staged, lands, r["rs"], r["rr"])
+        out_groups = reduce_groups(dims, totals, staged, lands, r["rs"], r["rr"], cfg["cuts"])
 
     def send(*which):
         if fused:
@@ -923,8 +964,16 @@
             cast_blocks(dims, totals[i], staged[i])
             send(i)
 
+    def send_tap_row(du):
+        if not fused:
+            return
+        third = 3 * nm
+        cast_blocks(dims, totals[0], staged[0], slice(du * third, (du + 1) * third))
+        for (_, start, _), exchange in zip(cfg["cuts"][0], out_groups[0]):
+            if len(out_groups[0]) == 1 and du == 2 or start // third == du:
+                advance(exchange)
+
     logit_rows = dot(logits[...], feature[...], NN)
-    advance(log_share)
     dlogits, part_rows = logits, big.part * big.width
 
     def from_logits(i):
@@ -934,10 +983,37 @@
     gain_two, bias_two = norm_backward(
         big, xh2, from_logits, r["spare"], dm, spread_m, row(norms, 2), row(norms, 3), scale_two
     )
-    advance(log_share)
+    complete(*kernel_share)
+    advance(kernel_cores)
     weight_gradient(big, hm, dm, totals[2], slice(0, 3 * nm))
     send_first(2)
-    complete(log_share)
+    complete(kernel_cores)
+    own_full = [kernels[pos[0], pos[1], pos[2], k] for k in range(2)]
+    own_scale = own_key_scale()
+
+    def sum_keys(i, acc):
+        for k in range(several):
+            _, raw, _, scale, allowed = scores(i * several + k, own_scale)
+            value = jnp.where(allowed, jnp.exp(raw * scale), 0.0)
+            acc = acc + jnp.sum(value, axis=1, keepdims=True)
+        return acc
+
+    totals_col = lax.fori_loop(0, images // several, sum_keys, jnp.zeros((SLOTS, 1), F32))
+    contrast_sum = jnp.sum(
+        jnp.where(weight_col > 0.0, weight_col * jnp.log(totals_col), 0.0), keepdims=True
+    )
+    key_totals = r["key_totals"]
+    key_totals[pos[0], pos[1], pos[2]] = jnp.broadcast_to(as_row(totals_col), (8, SLOTS))
+    total_share = plane_exchange(
+        dims,
+        key_totals.at[pos[0], pos[1], pos[2]],
+        key_totals.at[pos[0]],
+        False,
+        nothing,
+        r["ls"],
+        r["lr"],
+    )
+    advance(total_share)
     hidden = hm
 
     def input_tile(i, carry):
@@ -953,28 +1029,38 @@
     lax.fori_loop(0, big.high // big.span, input_tile, 0)
     hidden_copy = pair_copy(hidden.at[map_rows, :, away_m], r["dhm_in"], r["pair"].at[5])
     hidden_copy.start()
+    advance(total_share)
     send(2)
-
-    def row_terms(d, acc):
-        block, raw, key_scale, scale, allowed = scores(d)
-        index = split_index(dims, d)
-        log_row = logs[index[0], index[1], index[2]][0:1]
-        value = raw * scale
-        query = jnp.where(allowed, jnp.exp(value - log_col) * weight_col, 0.0)
-        key_count = jnp.full((1, 1), r["counts"][d], I32).astype(F32)
-        keyed = allowed & (live_col > 0.5)
-        key = jnp.where(keyed, jnp.exp(value - log_row) * (share / key_count), 0.0)
-        query_low = (query * scale).astype(BF16)
-        key_low = (key * scale).astype(BF16)
-        mine = jnp.where(model == 0, block[0].astype(F32), block[1].astype(F32)).astype(BF16)
-        return (
-            acc[0] + dot(query_low, mine, NN) + dot(key_low, mine, NN),
-            acc[1]
-            + jnp.sum((query + key) * raw * key_scale / CONTRAST_TEMP, axis=1, keepdims=True),
-        )
+    weight_gradient(small, hg, dg2, totals[4], slice(3 * nm, 3 * nm + 128))
+    send_first(4)
+    send(2)
+    complete(total_share)
+
+    own_scale = own_key_scale()
+    query_weight = weight_col / totals_col
+
+    def row_terms(i, acc):
+        for k in range(several):
+            d = i * several + k
+            block, raw, key_scale, scale, allowed = scores(d, own_scale)
+            index = split_index(dims, d)
+            total_row = key_totals[index[0], index[1], index[2]][0:1]
+            value = jnp.where(allowed, jnp.exp(raw * scale), 0.0)
+            key_count = jnp.full((1, 1), r["counts"][d], I32).astype(F32)
+            query = value * query_weight
+            key = value * live_col * (share / key_count / total_row)
+            query_low = (query * scale).astype(BF16)
+            key_low = (key * scale).astype(BF16)
+            mine = jnp.where(model == 0, block[0].astype(F32), block[1].astype(F32)).astype(BF16)
+            acc = (
+                acc[0] + dot(query_low, mine, NN) + dot(key_low, mine, NN),
+                acc[1]
+                + jnp.sum((query + key) * raw * key_scale / CONTRAST_TEMP, axis=1, keepdims=True),
+            )
+        return acc
 
     row_sum, scale_sum = lax.fori_loop(
-        0, images, row_terms, (jnp.zeros((SLOTS, nm), F32), jnp.zeros((SLOTS, 1), F32))
+        0, images // several, row_terms, (jnp.zeros((SLOTS, nm), F32), jnp.zeros((SLOTS, 1), F32))
     )
     norm_grad = -0.5 * own_scale * own_scale * own_scale * scale_sum
     row_grad = row_sum + 2.0 * kernel_rows.astype(F32) * norm_grad
@@ -983,8 +1069,6 @@
     )
     row_low = row_grad.astype(BF16)
 
-    weight_gradient(small, hg, dg2, totals[4], slice(3 * nm, 3 * nm + 128))
-    send(2)
     for i in range(small.high // small.span):
         at = lax.broadcasted_iota(I32, (gtile, SLOTS), 0) + i * gtile
         for dv in range(3):
@@ -1017,7 +1101,7 @@
         into = totals[3].at[..., t * nm : (t + 1) * nm]
         into[...] = value.reshape(into.shape)
     send_first(3)
-    send_first(4)
+    send(4)
     send(2)
 
     hidden_grid_copy.wait()
@@ -1031,9 +1115,10 @@
         small, xhg, both_grid_halves, r["spare_g"], dg1, spread_g, row(gnorms, 0),
         row(gnorms, 1), scale_grid,
     )
-    send(3, 4)
     weight_gradient(small, xg, dg1, totals[1], slice(0, 3 * ng))
     send_first(1)
+    send(4)
+    send(3)
     hidden_copy.wait()
     hidden_in = r["dhm_in"]
 
@@ -1044,71 +1129,89 @@
     gain_one, bias_one = norm_backward(
         big, xh1, both_halves, r["spare"], dm, spread_m, row(norms, 0), row(norms, 1), scale_one
     )
-    send(3, 4)
-    send(1)
-    weight_gradient(big, xm, dm, totals[0], slice(0, 3 * nm))
-    send_first(0)
-
-    smalls = r["smalls"]
-    blank = jnp.zeros((1, 128), F32)
+
     pieces = [gain_one, bias_one, gain_two, bias_two]
     pieces += [gain_grid[:, i : i + nm] for i in range(0, ng, nm)]
     pieces += [bias_grid[:, i : i + nm] for i in range(0, ng, nm)]
     pieces += [class_bias_sum]
-    pieces += [blank] * (16 - len(pieces))
-    smalls[pos[0], pos[1], pos[2]] = jnp.concatenate(pieces, axis=0)
-    small_share = share_exchange(dims, smalls, r["ss"], r["sr"], False)
+    pieces += [jnp.zeros((1, 128), F32)] * (16 - len(pieces))
+    small_plane, small_line = r["small_plane"], r["small_line"]
+    small_plane[pos[1], pos[2]] = jnp.concatenate(pieces, axis=0)
+
+    def plane_total(plane, cores):
+        value = None
+        for y in range(dims[1]):
+            for x in range(dims[2]):
+                for core in range(2) if cores else (None,):
+                    part = plane[y, x] if core is None else plane[y, x, core]
+                    value = part if value is None else value + part
+        return value
+
+    def line_total(line):
+        value = line[0]
+        for z in range(1, dims[0]):
+            value = value + line[z]
+        return value
+
+    def small_sum_here():
+        small_line[pos[0]] = plane_total(small_plane, False)
+
+    small_share = plane_exchange(
+        dims, small_plane.at[pos[1], pos[2]], small_line.at[pos[0]], False, small_sum_here,
+        r["ss"], r["sr"],
+    )
     advance(small_share)
-    send(3, 4)
+
+    def each(du):
+        send_tap_row(du)
+        if du == 0:
+            send(3)
+            send(4)
+        if du == 1:
+            send(1)
+            advance(small_share)
+
+    weight_gradient(big, xm, dm, totals[0], slice(0, 3 * nm), each)
+    send(3)
     send(1)
-    send(0)
-    advance(small_share)
-
-    squares = jnp.zeros((1, 1), F32)
-
-    def hand_out(i):
-        complete(*out_groups[i])
-        value = totals[i][pos[0], pos[1], pos[2]]
-        r["out%d" % i][...] = value
-        return jnp.sum(value * value, keepdims=True)
-
-    if fused:
-        for i in (2, 3, 4):
-            squares += hand_out(i)
-        send(1)
-        send(0)
-        squares += hand_out(1)
     complete(small_share)
-
-    def add_small(d, acc):
-        index = split_index(dims, d)
-        return acc + smalls[index[0], index[1], index[2]]
-
-    small_sum = lax.fori_loop(0, images, add_small, jnp.zeros((16, 128), F32))
+    small_sum = line_total(small_line)
     r["small_out"][...] = small_sum
     first_model = (model == 0).astype(F32)
     loss = jnp.sum(focal_sum, keepdims=True) + first_model * (dice_sum + contrast_sum)
     if fused:
+        squares = (own_image == 0).astype(F32) * jnp.sum(small_sum * small_sum, keepdims=True)
+
+        def hand_out(i):
+            complete(*out_groups[i])
+            value = totals[i][pos[0], pos[1], pos[2]]
+            r["out%d" % i][...] = value
+            return jnp.sum(value * value, keepdims=True)
+
+        squares += hand_out(2)
+        squares += hand_out(4)
+        send(0)
+        squares += hand_out(3)
+        send(0)
+        squares += hand_out(1)
         squares += hand_out(0)
-        first_device = (own_image == 0).astype(F32)
-        squares += first_device * jnp.sum(small_sum * small_sum, keepdims=True)
-        sums = r["sums"]
+        sum_plane, sum_line = r["sum_plane"], r["sum_line"]
         at = lax.broadcasted_iota(I32, (8, 128), 0)
-        sums[pos[0], pos[1], pos[2], model] = jnp.where(at == 0, squares, loss)
-        sum_share = share_exchange(dims, sums, r["us"], r["ur"], True)
+        sum_plane[pos[1], pos[2], model] = jnp.where(at == 0, squares, loss)
+
+        def sums_here():
+            sum_line[pos[0]] = plane_total(sum_plane, True)
+
+        sum_share = plane_exchange(
+            dims, sum_plane.at[pos[1], pos[2], model], sum_line.at[pos[0]], True, sums_here,
+            r["us"], r["ur"],
+        )
         complete(sum_share)
-
-        def add_sums(d, acc):
-            index = split_index(dims, d)
-            return acc + sums[index[0], index[1], index[2], 0] + sums[
-                index[0], index[1], index[2], 1
-            ]
-
-        r["sum_out"][...] = lax.fori_loop(0, images, add_sums, jnp.zeros((8, 128), F32))
+        r["sum_out"][...] = line_total(sum_line)
         sum_share.drain()
     else:
         r["sum_out"][...] = jnp.broadcast_to(loss, (8, 128))
-    for shared in (kernel_share, log_share, small_share):
+    for shared in kernel_share + [kernel_cores, total_share, small_share]:
         shared.drain()
     for group in out_groups:
         for exchange in group:
@@ -1121,7 +1224,7 @@
     nm, ng = big.channels, small.channels
     rows, grid_rows = big.high * big.width, small.high * small.width
     inputs = dict(inputs, **weights)
-    spaces = dict(xm_own=ANY, xg_own=ANY, counts=pltpu.SMEM)
+    spaces = dict(xm_own=ANY, xg_own=ANY, masks=ANY, counts=pltpu.SMEM)
     names = list(inputs)
     specs = [pl.BlockSpec(memory_space=spaces.get(name, VMEM)) for name in names]
     outs = {"small_out": ((16, 128), F32), "sum_out": ((8, 128), F32)}
@@ -1131,21 +1234,25 @@
             outs["out%d" % i] = (shape[3:], F32)
             scratch["w%d" % i] = VMEM(shape, BF16)
             scratch["g%d" % i] = VMEM(shape, F32)
-        lands = landing_scratch(dims, blocks)
-        cfg = dict(cfg, lands=len(lands))
+        gather_cuts = [lane_cuts(shape[-1]) for shape in blocks]
+        cuts = [tap_row_cuts(blocks[0][-1])] + gather_cuts[1:]
+        lands = landing_scratch(dims, blocks, cuts)
+        cfg = dict(cfg, lands=len(lands), cuts=cuts)
         for i, land in enumerate(lands):
             scratch["land%d" % i] = land
-        slots = flow_slots(dims, blocks)
-        for name in ("gs", "gr", "rs", "rr"):
-            scratch[name] = DMA((slots,))
-        scratch["sums"] = VMEM(dims + (2, 8, 128), F32)
-        scratch["us"], scratch["ur"] = share_sems(dims)
+        for names_of, used in ((("gs", "gr"), gather_cuts), (("rs", "rr"), cuts)):
+            for name in names_of:
+                scratch[name] = DMA((flow_slots(dims, used),))
+        scratch["class_stage"] = VMEM(blocks[4], BF16)
+        scratch["sum_plane"] = VMEM(dims[1:] + (2, 8, 128), F32)
+        scratch["sum_line"] = VMEM(dims[:1] + (8, 128), F32)
+        scratch["us"], scratch["ur"] = plane_sems(dims)
     else:
         for i in range(5):
             outs["g%d" % i] = (inputs["w%d" % i].shape, F32)
     c_in = 2 * inputs["xm_own"].shape[3]
     depth = 2 * ng
-    slot_rows = -(-inputs["masks"].shape[1] // 16) * 16
+    slot_rows = -(-inputs["masks"].shape[0] // 16) * 16
 
     def padded(m, channels):
         return VMEM((m.high + 2, m.width, channels), BF16)
@@ -1163,7 +1270,7 @@
         kernels=VMEM(dims + (2, SLOTS, nm), BF16),
         logits=VMEM((slot_rows, rows), BF16),
         logits_in=VMEM((slot_rows, rows), BF16),
-        logs=VMEM(dims + (8, SLOTS), F32),
+        key_totals=VMEM(dims + (8, SLOTS), F32),
         dm=padded(big, 3 * nm),
         spare=VMEM((rows, nm), F32),
         dhm_in=VMEM((big.high, big.width, nm), BF16),
@@ -1171,14 +1278,17 @@
         dhg_in=VMEM((small.high, small.width, ng), BF16),
         dg1=padded(small, 3 * ng),
         spare_g=VMEM((grid_rows, ng), F32),
-        smalls=VMEM(dims + (16, 128), F32),
+        small_plane=VMEM(dims[1:] + (16, 128), F32),
+        small_line=VMEM(dims[:1] + (16, 128), F32),
         table=VMEM((8, SLOTS), I32),
         bias_table=VMEM((8, 128), F32),
-        local=DMA((2,)),
-        pair=DMA((7, 2)),
-    )
-    for a, b in (("ks", "kr"), ("ls", "lr"), ("ss", "sr")):
-        scratch[a], scratch[b] = share_sems(dims)
+        local=DMA((3,)),
+        mask_bits=VMEM((inputs["masks"].shape[0], rows), I32),
+        pair=DMA((8, 2)),
+    )
+    scratch["ks"], scratch["kr"] = share_sems(dims, 2)
+    for a, b in (("ls", "lr"), ("ss", "sr")):
+        scratch[a], scratch[b] = plane_sems(dims)
     names += list(outs) + list(scratch)
     result = pl.pallas_call(
         partial(step_kernel, cfg, tuple(names)),
@@ -1289,7 +1399,7 @@
     inputs = dict(
         xm_own=mask_features,
         xg_own=grid_features,
-        masks=instance_masks,
+        masks=instance_masks.transpose(1, 0, 2),
         counts=instance_counts,
         cells=instance_cells,
         labels=instance_labels,

time: 175 us -> 141 us (0.81)
  Pallas kernels: 170 us -> 140 us
  local copies, waits for them, and re-layouts: 3.8 us -> 0 us
    pallas_call x1, Pallas kernels: 167 us -> 136 us  [run_step(): pl.pallas_call(partial(step_kernel, cfg, tuple(names)), name='step', out_...]
    unnamed x1 -> x0, local copies, waits for them, and re-layouts: 3.8 us -> none
where the time goes in v4:
time: 141 us; the launch traced here: 140 us
  Pallas kernels  140 us (99%)
    pallas_call x1, Pallas kernels, run_step(): pl.pallas_call(partial(step_kernel, cfg, tuple(names)), name='step', out_...  136 us
    pallas_call x1, Pallas kernels, run_update(): pl.pallas_call(partial(update_kernel, nm, ng, kc), name='update', out_sha...  3.35 us

profile of v4, /device:TPU:0, one launch (start us, length us, event | category | flops | bytes accessed | tf_op | source)
XLA Modules:
  0.0 140.4 jit_solution(17840102081935318786)
XLA Ops:
  0.7 136.2 %step.1 = (f32[16,128]{1,0:T(8,128)}, f32[8,128]{1,0:T(8,128)}, f32[16,1152]{1,0:T(8,128)}, f32[16,2304]{1,0:T(8,128)}, f32[16,1152]{1,0:T(8,128)}, /*index=5*/f32[32,1152]{1,0:T(8,128)}, f32[32,384]{1,0:T(8,128)}) custom-call(bf16[1,32,128,128]{3,2,1,0:T(8,128)(2,1)} %refs_0_.1, bf16[1,40,40,128]{3,2,1,0:T(8,128)(2,1)} %refs_1_.1, s32[100,1,4096]{2,1,0:T(1,128)} %bitcast.9, ...), custom_call_target="tpu_custom_call" | custom-call | tf_op jit(solution)/shard_map/step/pallas_call | solution.py:1293
  136.9 3.3 %update.1 = (f32[1,1]{1,0:T(1,128)}, f32[1,1]{1,0:T(1,128)}, f32[2,9,16,128]{3,2,1,0:T(8,128)}, f32[2,9,16,128]{3,2,1,0:T(8,128)}, f32[2,9,16,128]{3,2,1,0:T(8,1...) custom-call(f32[16,1152]{1,0:T(8,128)} %get-tuple-element.53.refs_0_, ...), custom_call_target="tpu_custom_call" | custom-call | tf_op jit(solution)/shard_map/update/pallas_call | solution.py:1340

commit v5 on v4

--- a/solution.py
+++ b/solution.py
@@ -86,14 +86,22 @@
     return peers
 
 
-def greet(dims):
+def greet_start(dims):
     sem = pltpu.get_barrier_semaphore()
     pos = place(dims)
     peers = plane_peers(dims, True)
     peers += [ring_step(dims, pos, 0, offset) for offset in range(1, dims[0])]
     for peer in peers:
         pl.semaphore_signal(sem, inc=1, device_id=peer, device_id_type=MESH)
-    pl.semaphore_wait(sem, len(peers))
+    return sem, len(peers)
+
+
+def greet_end(sem, count):
+    pl.semaphore_wait(sem, count)
+
+
+def greet(dims):
+    greet_end(*greet_start(dims))
 
 
 GATHER_ORDERS = ((2, 1, 0), (0, 2, 1), (0, 1, 2))
@@ -108,7 +116,7 @@
     tiles = width // 128
     if width % 128 or tiles < 3:
         return ((0, 0, width),)
-    first = max(1, round(tiles * 0.1))
+    first = max(1, round(tiles * 0.17))
     second = (tiles - first) // 2
     sizes = (first, second, tiles - first - second)
     cuts, start = [], 0
@@ -249,29 +257,59 @@
 
 def reduce_exchange(dims, total, staged, lands, send_sems, recv_sems, base, lanes, order):
     pos = place(dims)
-    result, reduced = Exchange(), set()
-    for stage, axis in enumerate(order):
+    result = Exchange()
+    axes = [axis for axis in order if dims[axis] > 1]
+
+    def over_blocks(free, inner, body):
+        outer = [k for k in free if k != inner]
+        count = 1
+        for k in outer:
+            count *= dims[k]
+
+        def step(i, carry):
+            where, rest = {}, i
+            for k in reversed(outer):
+                where[k] = lax.rem(rest, dims[k])
+                rest = rest // dims[k]
+            for offset in range(dims[inner] if inner is not None else 1):
+                here = dict(where)
+                if inner is not None:
+                    here[inner] = lax.rem(pos[inner] + offset, dims[inner])
+                body(here, offset)
+            return carry
+
+        if count == 1:
+            step(jnp.int32(0), 0)
+        else:
+            lax.fori_loop(0, count, step, 0)
+
+    def index_of(where):
+        return tuple(where.get(k, pos[k]) for k in range(3)) + (slice(None), lanes)
+
+    def prepare():
+        def cast(where, offset):
+            if offset:
+                staged[index_of(where)] = total[index_of(where)].astype(BF16)
+
+        over_blocks(axes, axes[0], cast)
+
+    result.prepare = prepare
+    for stage, axis in enumerate(axes):
         n = dims[axis]
-        free = [k for k in range(3) if k not in reduced and k != axis]
-
-        def view(block, lead=None, axis=axis, reduced=frozenset(reduced)):
-            lead = iter(lead) if lead is not None else None
-            index = []
-            for k in range(3):
-                if k == axis:
-                    index.append(block)
-                elif k in reduced:
-                    index.append(pos[k])
-                else:
-                    index.append(pl.ds(0, dims[k]) if lead is None else next(lead))
-            return tuple(index) + (slice(None), lanes)
-
+        free = axes[stage + 1 :]
+        inner = free[0] if free else None
         copies = []
         for offset in range(1, n):
+            view = tuple(
+                lax.rem(pos[axis] + offset, n)
+                if k == axis
+                else (pl.ds(0, dims[k]) if k in free else pos[k])
+                for k in range(3)
+            )
             copies.append(
                 pltpu.make_async_remote_copy(
-                    src_ref=staged.at[view(lax.rem(pos[axis] + offset, n))],
-                    dst_ref=lands[stage].at[offset - 1],
+                    src_ref=staged.at[view + (slice(None), lanes)],
+                    dst_ref=lands[order.index(axis)].at[offset - 1],
                     send_sem=send_sems.at[base],
                     recv_sem=recv_sems.at[base],
                     device_id=ring_step(dims, pos, axis, offset),
@@ -280,36 +318,28 @@
             )
             base += 1
 
-        def land(stage=stage, axis=axis, n=n, free=free, view=view):
-            sizes = [dims[k] for k in free]
-            blocks = 1
-            for size in sizes:
-                blocks *= size
-
-            def add(i, carry):
-                lead, rest = [], i
-                for size in reversed(sizes):
-                    lead.append(lax.rem(rest, size))
-                    rest = rest // size
-                lead = lead[::-1]
-                index = view(pos[axis], lead)
+        def land(axis=axis, n=n, free=free, inner=inner):
+            arrived = lands[order.index(axis)]
+            left = sorted(free + [k for k in range(3) if dims[k] == 1 and k in later(axis)])
+
+            def add(where, offset):
+                index = index_of(where)
                 value = total[index]
                 for k in range(n - 1):
-                    value = value + lands[stage][(k,) + tuple(lead)].astype(F32)
-                total[index] = value
-                if sizes:
+                    lead = tuple(where.get(j, 0) for j in left)
+                    value = value + arrived[(k,) + lead].astype(F32)
+                if offset:
                     staged[index] = value.astype(BF16)
-                return carry
-
-            if blocks == 1:
-                add(jnp.int32(0), 0)
-            else:
-                lax.fori_loop(0, blocks, add, 0)
-
-        if copies:
-            result.stages.append(copies)
-            result.lands.append(land)
-        reduced.add(axis)
+                else:
+                    total[index] = value
+
+            over_blocks(free, inner, add)
+
+        def later(axis):
+            return order[order.index(axis) + 1 :]
+
+        result.stages.append(copies)
+        result.lands.append(land)
     return result
 
 
@@ -386,15 +416,6 @@
     return scratch
 
 
-def cast_blocks(dims, total, staged, lanes=slice(None)):
-    def cast(j, carry):
-        index = split_index(dims, j) + (slice(None), lanes)
-        staged[index] = total[index].astype(BF16)
-        return carry
-
-    lax.fori_loop(0, dims[0] * dims[1] * dims[2], cast, 0)
-
-
 def run_all(groups):
     exchanges = [exchange for group in groups for exchange in group]
     complete(*exchanges)
@@ -445,9 +466,12 @@
     greet(dims)
     for i in range(count):
         local[i].wait()
-        cast_blocks(dims, totals[i], staged[i])
     cuts = [lane_cuts(total.shape[4]) for total in totals]
-    run_all(reduce_groups(dims, totals, staged, lands, send_sems, recv_sems, cuts))
+    groups = reduce_groups(dims, totals, staged, lands, send_sems, recv_sems, cuts)
+    for group in groups:
+        for exchange in group:
+            exchange.prepare()
+    run_all(groups)
     for i in range(count):
         outs[i][...] = totals[i][pos[0], pos[1], pos[2]]
 
@@ -651,6 +675,8 @@
     map_rows, grid_span = pl.ds(1, big.high), pl.ds(1, small.high)
     spread_m = group_spread(nm, 2 * nm // GROUPS)
     spread_g = group_spread(ng, 2 * ng // GROUPS)
+
+    greeted = greet_start(dims)
 
     xm, xg, hm, hg, dm = r["xm"], r["xg"], r["hm"], r["hg"], r["dm"]
     dg1, dg2 = r["dg1"], r["dg2"]
@@ -693,15 +719,41 @@
         if fused:
             advance(*[exchange for i in which for exchange in groups[i]])
 
-    greet(dims)
+    greet_end(*greeted)
+    bring(0)
     feature_copies = [
         pair_copy(mask_in, mask_into, r["pair"].at[0]),
         pair_copy(grid_in, grid_into, r["pair"].at[1]),
     ]
-    for copy in feature_copies:
-        copy.start()
-    bring(0)
+    feature_copies[0].start()
     bring(1)
+    feature_copies[1].start()
+
+    totals = [r["g%d" % i] for i in range(5)]
+    out_groups = []
+    if fused:
+        staged = [weights[2], weights[1], weights[0], r["second_stage"], r["class_stage"]]
+        lands = [r["land%d" % i] for i in range(cfg["lands"])]
+        out_groups = reduce_groups(dims, totals, staged, lands, r["rs"], r["rr"], cfg["cuts"])
+
+    def send(*which):
+        if fused:
+            advance(*[exchange for i in which for exchange in out_groups[i]])
+
+    def send_first(i):
+        if fused:
+            for exchange in out_groups[i]:
+                exchange.prepare()
+            send(i)
+
+    def send_tap_row(du):
+        if not fused:
+            return
+        third = 3 * nm
+        for (_, start, _), exchange in zip(cfg["cuts"][0], out_groups[0]):
+            if len(out_groups[0]) == 1 and du == 2 or start // third == du:
+                exchange.prepare()
+                advance(exchange)
 
     for ref in (xm, xg, hm, hg, dm, dg1, dg2):
         zero_edges(ref)
@@ -866,6 +918,8 @@
         0, small.high // small.span, class_tile, (zero, zero)
     )
 
+    weight_gradient(small, hg, dg2, totals[4], slice(3 * nm, 3 * nm + 128))
+
     for group in groups:
         complete(*group)
         for exchange in group:
@@ -892,6 +946,7 @@
     ]
     kernel_cores = core_exchange(kernels, r["pair"].at[7])
     advance(*kernel_share)
+    send_first(4)
 
     kernel_rows = kernels[pos[0], pos[1], pos[2], model]
     logits, logits_in = r["logits"], r["logits_in"]
@@ -922,6 +977,7 @@
         b = 2.0 * share_here * inter / (whole * whole)
         logits[span, :] = ((a * mask + 2.0 * b * s) * s * (1.0 - s)).astype(BF16)
     advance(*kernel_share)
+    send(4)
 
     several = 4 if images % 4 == 0 else 1
 
@@ -948,31 +1004,6 @@
     def own_key_scale():
         return lax.rsqrt(squares_of(own_full) + 1e-06)
 
-    totals = [r["g%d" % i] for i in range(5)]
-    out_groups = []
-    if fused:
-        staged = [weights[2], weights[1], weights[0], weights[3], r["class_stage"]]
-        lands = [r["land%d" % i] for i in range(cfg["lands"])]
-        out_groups = reduce_groups(dims, totals, staged, lands, r["rs"], r["rr"], cfg["cuts"])
-
-    def send(*which):
-        if fused:
-            advance(*[exchange for i in which for exchange in out_groups[i]])
-
-    def send_first(i):
-        if fused:
-            cast_blocks(dims, totals[i], staged[i])
-            send(i)
-
-    def send_tap_row(du):
-        if not fused:
-            return
-        third = 3 * nm
-        cast_blocks(dims, totals[0], staged[0], slice(du * third, (du + 1) * third))
-        for (_, start, _), exchange in zip(cfg["cuts"][0], out_groups[0]):
-            if len(out_groups[0]) == 1 and du == 2 or start // third == du:
-                advance(exchange)
-
     logit_rows = dot(logits[...], feature[...], NN)
     dlogits, part_rows = logits, big.part * big.width
 
@@ -987,6 +1018,7 @@
     advance(kernel_cores)
     weight_gradient(big, hm, dm, totals[2], slice(0, 3 * nm))
     send_first(2)
+    send(4)
     complete(kernel_cores)
     own_full = [kernels[pos[0], pos[1], pos[2], k] for k in range(2)]
     own_scale = own_key_scale()
@@ -1029,10 +1061,6 @@
     lax.fori_loop(0, big.high // big.span, input_tile, 0)
     hidden_copy = pair_copy(hidden.at[map_rows, :, away_m], r["dhm_in"], r["pair"].at[5])
     hidden_copy.start()
-    advance(total_share)
-    send(2)
-    weight_gradient(small, hg, dg2, totals[4], slice(3 * nm, 3 * nm + 128))
-    send_first(4)
     send(2)
     complete(total_share)
 
@@ -1068,6 +1096,13 @@
         [logit_rows, jnp.zeros((SLOTS - high_slots, nm), F32)], axis=0
     )
     row_low = row_grad.astype(BF16)
+    for t in range(9):
+        value = dot(patches[:, t * depth : (t + 1) * depth], row_low, TN)
+        into = totals[3].at[..., t * nm : (t + 1) * nm]
+        into[...] = value.reshape(into.shape)
+    send_first(3)
+    send(2)
+    send(4)
 
     for i in range(small.high // small.span):
         at = lax.broadcasted_iota(I32, (gtile, SLOTS), 0) + i * gtile
@@ -1096,12 +1131,6 @@
         hidden_grid.at[grid_span, :, away_g], r["dhg_in"], r["pair"].at[6]
     )
     hidden_grid_copy.start()
-    for t in range(9):
-        value = dot(patches[:, t * depth : (t + 1) * depth], row_low, TN)
-        into = totals[3].at[..., t * nm : (t + 1) * nm]
-        into[...] = value.reshape(into.shape)
-    send_first(3)
-    send(4)
     send(2)
 
     hidden_grid_copy.wait()
@@ -1115,9 +1144,9 @@
         small, xhg, both_grid_halves, r["spare_g"], dg1, spread_g, row(gnorms, 0),
         row(gnorms, 1), scale_grid,
     )
+    send(3)
     weight_gradient(small, xg, dg1, totals[1], slice(0, 3 * ng))
     send_first(1)
-    send(4)
     send(3)
     hidden_copy.wait()
     hidden_in = r["dhm_in"]
@@ -1164,16 +1193,17 @@
 
     def each(du):
         send_tap_row(du)
-        if du == 0:
+        if du == 1:
+            advance(small_share)
+            send(1)
+        if du == 2:
             send(3)
-            send(4)
-        if du == 1:
-            send(1)
-            advance(small_share)
 
     weight_gradient(big, xm, dm, totals[0], slice(0, 3 * nm), each)
-    send(3)
+    last_group = out_groups[0] if fused else []
+    advance(*last_group[:2])
     send(1)
+    advance(*last_group[2:])
     complete(small_share)
     small_sum = line_total(small_line)
     r["small_out"][...] = small_sum
@@ -1244,6 +1274,7 @@
             for name in names_of:
                 scratch[name] = DMA((flow_slots(dims, used),))
         scratch["class_stage"] = VMEM(blocks[4], BF16)
+        scratch["second_stage"] = VMEM(blocks[3], BF16)
         scratch["sum_plane"] = VMEM(dims[1:] + (2, 8, 128), F32)
         scratch["sum_line"] = VMEM(dims[:1] + (8, 128), F32)
         scratch["us"], scratch["ur"] = plane_sems(dims)

time: 141 us -> 139 us (0.986)
  Pallas kernels: 140 us -> 138 us
where the time goes in v5:
time: 139 us
  Pallas kernels  138 us (99%)
    pallas_call x1, Pallas kernels, run_step(): pl.pallas_call(partial(step_kernel, cfg, tuple(names)), name='step', out_...  135 us
    pallas_call x1, Pallas kernels, run_update(): pl.pallas_call(partial(update_kernel, nm, ng, kc), name='update', out_sha...  3.35 us

profile of v5, /device:TPU:0, one launch (start us, length us, event | category | flops | bytes accessed | tf_op | source)
XLA Modules:
  0.0 139.0 jit_solution(9726618845898001348)
XLA Ops:
  0.7 134.8 %step.1 = (f32[16,128]{1,0:T(8,128)}, f32[8,128]{1,0:T(8,128)}, f32[16,1152]{1,0:T(8,128)}, f32[16,2304]{1,0:T(8,128)}, f32[16,1152]{1,0:T(8,128)}, /*index=5*/f32[32,1152]{1,0:T(8,128)}, f32[32,384]{1,0:T(8,128)}) custom-call(bf16[1,32,128,128]{3,2,1,0:T(8,128)(2,1)} %refs_0_.1, bf16[1,40,40,128]{3,2,1,0:T(8,128)(2,1)} %refs_1_.1, s32[100,1,4096]{2,1,0:T(1,128)} %bitcast.9, ...), custom_call_target="tpu_custom_call" | custom-call | tf_op jit(solution)/shard_map/step/pallas_call | solution.py:1324
  135.5 3.3 %update.1 = (f32[1,1]{1,0:T(1,128)}, f32[1,1]{1,0:T(1,128)}, f32[2,9,16,128]{3,2,1,0:T(8,128)}, f32[2,9,16,128]{3,2,1,0:T(8,128)}, f32[2,9,16,128]{3,2,1,0:T(8,1...) custom-call(f32[16,1152]{1,0:T(8,128)} %get-tuple-element.53.refs_0_, ...), custom_call_target="tpu_custom_call" | custom-call | tf_op jit(solution)/shard_map/update/pallas_call | solution.py:1371

commit v6 on v5

--- a/solution.py
+++ b/solution.py
@@ -803,8 +803,10 @@
     feature_copies[0].wait()
     bring(0)
     xh1 = r["xh1"]
-    total = conv_forward(big, xm, mask_one, xh1)
+    half = big.high // big.span // 2
+    total = conv_forward(big, xm, mask_one, xh1, 0, half)
     bring(1)
+    total = conv_forward(big, xm, mask_one, xh1, half, None, total)
     bring(2)
     bring(4)
     bring(3)

time: 139 us -> 138 us (level)
  no operation moved by 1% of the time
where the time goes in v6:
time: 138 us
  Pallas kernels  137 us (99%)
    pallas_call x1, Pallas kernels, run_step(): pl.pallas_call(partial(step_kernel, cfg, tuple(names)), name='step', out_...  134 us
    pallas_call x1, Pallas kernels, run_update(): pl.pallas_call(partial(update_kernel, nm, ng, kc), name='update', out_sha...  3.35 us

profile of v6, /device:TPU:0, one launch (start us, length us, event | category | flops | bytes accessed | tf_op | source)
XLA Modules:
  0.0 137.8 jit_solution(6990059324117529491)
XLA Ops:
  0.7 133.6 %step.1 = (f32[16,128]{1,0:T(8,128)}, f32[8,128]{1,0:T(8,128)}, f32[16,1152]{1,0:T(8,128)}, f32[16,2304]{1,0:T(8,128)}, f32[16,1152]{1,0:T(8,128)}, /*index=5*/f32[32,1152]{1,0:T(8,128)}, f32[32,384]{1,0:T(8,128)}) custom-call(bf16[1,32,128,128]{3,2,1,0:T(8,128)(2,1)} %refs_0_.1, bf16[1,40,40,128]{3,2,1,0:T(8,128)(2,1)} %refs_1_.1, s32[100,1,4096]{2,1,0:T(1,128)} %bitcast.9, ...), custom_call_target="tpu_custom_call" | custom-call | tf_op jit(solution)/shard_map/step/pallas_call | solution.py:1326
  134.2 3.3 %update.1 = (f32[1,1]{1,0:T(1,128)}, f32[1,1]{1,0:T(1,128)}, f32[2,9,16,128]{3,2,1,0:T(8,128)}, f32[2,9,16,128]{3,2,1,0:T(8,128)}, f32[2,9,16,128]{3,2,1,0:T(8,1...) custom-call(f32[16,1152]{1,0:T(8,128)} %get-tuple-element.53.refs_0_, ...), custom_call_target="tpu_custom_call" | custom-call | tf_op jit(solution)/shard_map/update/pallas_call | solution.py:1373
